TPU v7x, 256 devices: a whole 4x4x8 slice. The times are simulated.
256 devices in a mesh: blk: 32 (over x, z), leaf: 4 (over y), samp: 2 (over core).
Axes of the slice: x: 4, y: 4, z: 8, core: 2. Of those that a mesh axis runs over, the one named last changes fastest.
Arguments:
- points: float32 [3, 32768], P(None, ('blk', 'leaf')), may hold values from 0 to 64, as said below
- neighbors: int32 [128, 8], P(('blk', 'leaf')), may hold values from -1 to 127, as said below
- omega: float32 [512, 32768], P(None, ('blk', 'leaf')), may hold values from -6 to 6
- observed: float32 [32768], P(('blk', 'leaf')), may hold values from -6 to 6
- prior_draws: float32 [64, 32768], P('samp', ('blk', 'leaf')), may hold values from -6 to 6
Outputs:
- weights: float32 [64, 32768], P('samp', ('blk', 'leaf'))
- residual: float32 [64, 32768], P('samp', ('blk', 'leaf'))
Inputs may be any that keep to these rules, and one draw needn't show every extreme that they name: Block g's points lie in the unit cell with integer corner (cx, cy, cz), where cx // 2 = g // 4 and 0 <= cy, cz < 3. `neighbors`: row g lists in ascending order every block h whose unit cell touches g's (cells at most one apart in every coordinate, the first taken periodic of period 2 * 32), which includes every block with a point within distance 1 of a point of g, followed by -1 in the unused slots; the relation is symmetric, and every listed block has a slab index h // 4 equal to or cyclically next to g // 4.
All inputs are finite; a program needn't handle non-finite values.
Results may differ from a plain program's by a relative error of at most 0.0003.
Values sent between devices are 32-bit elements; how exact they have to be, the bound alone decides.
A program may use at most 64 MiB of HBM per device.

v0:
```python
import jax
import jax.numpy as jnp
from jax import lax
from jax.sharding import PartitionSpec as P

PB = 256
ITERS = 2


support_radius = 0.8
noise_variance = 1.0
sketch_shift = 1.0


def shifted_2(block, axis, distance):
    devices = range(lax.axis_size(axis))
    route = [((i - distance) % len(devices), i) for i in devices]
    return lax.ppermute(block, axis, route)


def wendland(row_points, column_points, period):
    offset = row_points[None, :, :, None] - column_points[:, :, None, :]
    half_period = 0.5 * period
    along_x = jnp.mod(offset[:, 0] + half_period, period) - half_period
    squared = along_x * along_x + offset[:, 1] * offset[:, 1] + offset[:, 2] * offset[:, 2]
    radius = jnp.sqrt(squared) / support_radius
    remain = jnp.maximum(1.0 - radius, 0.0)
    return remain**4 * (4.0 * radius + 1.0)


def high_dot(left, right):
    return jnp.dot(left, right, precision=lax.Precision.HIGHEST, preferred_element_type=jnp.float32)


def shifted(values, offset_by):
    return shifted_2(values, "blk", offset_by)


def beside_all(values):
    slab_values = lax.all_gather(values, "leaf", axis=1, tiled=True)
    return jnp.concatenate([shifted(slab_values, 1), slab_values, shifted(slab_values, -1)], axis=1)


def total(values):
    return lax.psum(values, ("blk", "leaf"))


def lower_solve(factor, values):
    return lax.linalg.triangular_solve(factor, values, left_side=True, lower=True)


def local(points, neighbors, omega, observed, prior_draws):
    blk_dev = neighbors.shape[0]
    cycle_count = lax.axis_size("blk")
    slab_blocks = blk_dev * lax.axis_size("leaf")
    period = 2.0 * cycle_count
    own_slab = lax.axis_index("blk")
    usable = neighbors >= 0
    relative = jnp.mod(neighbors // slab_blocks - own_slab + 1, cycle_count)
    chosen = jnp.where(usable, relative * slab_blocks + jnp.mod(neighbors, slab_blocks), 0)
    usable_weight = usable.astype(jnp.float32)
    reach_points = beside_all(points)
    reach_blocks = reach_points.reshape(3, 3 * slab_blocks, PB).transpose(1, 0, 2)
    row_blocks = points.reshape(3, blk_dev, PB).transpose(1, 0, 2)

    def build_tile(block_index):
        kernel_tile = wendland(row_blocks[block_index], reach_blocks[chosen[block_index]], period)
        return kernel_tile * usable_weight[block_index][:, None, None]

    def apply_kernel(values):
        width = values.shape[0]
        reach = beside_all(values).reshape(width, 3 * slab_blocks, PB)
        picked = jnp.take(reach, chosen[0], axis=1)
        pieces = jnp.einsum("cnj,nij->ci", picked, build_tile(0), precision=lax.Precision.HIGHEST)
        return pieces

    sketch = apply_kernel(omega) + sketch_shift * omega
    core_gram = total(high_dot(omega, sketch.T))
    core_gram = 0.5 * (core_gram + core_gram.T)
    factor = jnp.linalg.cholesky(core_gram)
    basis = lower_solve(factor, sketch)
    basis_gram = total(high_dot(basis, basis.T))
    woodbury = noise_variance * jnp.eye(basis.shape[0], dtype=jnp.float32) + 0.5 * (
        basis_gram + basis_gram.T
    )
    wood_factor = jnp.linalg.cholesky(woodbury)

    def inverse_apply(vectors):
        projected = total(high_dot(basis, vectors.T))
        first_solve = lower_solve(wood_factor, projected)
        solved = lax.linalg.triangular_solve(
            wood_factor, first_solve, left_side=True, lower=True, transpose_a=True
        )
        return (vectors - high_dot(solved.T, basis)) / noise_variance

    rhs = observed[None, :] - prior_draws
    weights = jnp.zeros_like(rhs)
    residual = rhs
    precond = inverse_apply(residual)
    direction = precond
    inner_now = total(jnp.sum(residual * precond, axis=1))
    for step_index in range(ITERS):
        image = apply_kernel(direction) + noise_variance * direction
        step_size = inner_now / total(jnp.sum(direction * image, axis=1))
        weights = weights + step_size[:, None] * direction
        residual = residual - step_size[:, None] * image
        if step_index + 1 < ITERS:
            precond = inverse_apply(residual)
            inner_next = total(jnp.sum(residual * precond, axis=1))
            direction = precond + (inner_next / inner_now)[:, None] * direction
            inner_now = inner_next
    return (weights, residual)


def solution(mesh):
    in_specs = (
        P(None, ("blk", "leaf")),
        P(("blk", "leaf"), None),
        P(None, ("blk", "leaf")),
        P(("blk", "leaf")),
        P("samp", ("blk", "leaf")),
    )
    out_specs = (P("samp", ("blk", "leaf")), P("samp", ("blk", "leaf")))
    return jax.shard_map(local, mesh=mesh, in_specs=in_specs, out_specs=out_specs, check_vma=False)
```

profile of v0, /device:TPU:8, one launch (start us, length us, event | category | flops | bytes accessed | tf_op | source)
XLA Modules:
  0.0 2182.1 jit_solution(1720659250722919533)
XLA Ops:
  9.3 12.3 all_gather.13
  21.6 8.1 collective-permute-start.3
  29.7 15.5 all-gather.2.cloned.1.call-done
  56.6 39.3 %collective-permute-done.1 = f32[512,1024]{0,1:T(8,128)} collective-permute-done((f32[512,1024]{0,1:T(8,128)}, f32[512,1024]{0,1:T(8,128)}, u32[]{:S(2)}, u32[]{:S(2)}) %collective-permute-start.1) | collective-permute-done | bytes 2097184 | tf_op jit(solution)/shard_map/ppermute | solution.py:18
  106.9 6.5 copy.13
  127.7 214.8 %all-reduce.7.cloned.1.call-done = f32[512,512]{1,0:T(8,128)} async-done(((f32[512,512]{1,0:T(8,128)}), f32[512,512]{1,0:T(8,128)}) %all-reduce.7.cloned.1.call-update) | async-done | bytes 1048592 | tf_op jit(solution)/shard_map/psum | solution.py:45
  350.6 11.7 cholesky.286
  362.4 9.8 custom-call.35
  374.8 11.7 cholesky.305
  386.6 10.2 custom-call.36
  398.3 11.7 cholesky.326
  410.8 9.8 custom-call.37
  422.1 11.9 cholesky.343
  439.0 11.7 while.9
  450.7 39.3 %custom-call.29 = f32[4,128,128]{1,2,0:T(8,128)S(1)} custom-call(f32[4,128,128]{2,1,0:T(8,128)S(1)} %get-tuple-element.29), custom_call_target="InvertDiagBlocksLowerTriangular" | custom-call | tf_op jit(solution)/shard_map/triangular_solve | solution.py:49
  499.4 218.7 %all-reduce.11.cloned.1.call-done = (f32[512,512]{1,0:T(8,128)}, f32[512,32]{0,1:T(8,128)}) async-done(((f32[512,512]{1,0:T(8,128)}, f32[512,32]{0,1:T(8,128)}), (f32[512,512]{1,0:T(8,128)}, f32[512,32]{0,1:T(8,128)})) %all-reduce.11.cloned.1.call-update) | async-done | bytes 1114128 | tf_op jit(solution)/shard_map/psum | solution.py:45
  726.3 11.7 cholesky.358
  738.7 9.8 custom-call.38
  751.8 11.7 cholesky.377
  764.2 10.2 custom-call.39
  776.8 11.7 cholesky.398
  789.3 9.8 custom-call.40
  800.5 11.9 cholesky.415
  817.1 8.5 while.10
  826.3 40.1 %custom-call.42 = f32[4,128,128]{1,2,0:T(8,128)S(1)} custom-call(f32[4,128,128]{2,1,0:T(8,128)} %copy-done.13), custom_call_target="InvertDiagBlocksLowerTriangular" | custom-call | tf_op jit(solution)/shard_map/triangular_solve/custom-call.9 | solution.py:91
  873.7 11.9 all_gather.14
  890.8 5.8 collective-permute-done.4
  903.9 344.3 %all-reduce.1 = (f32[32]{0:T(128)}, f32[32]{0:T(128)}) all-reduce(f32[32]{0:T(128)} %get-tuple-element.47, f32[32]{0:T(128)S(1)} %get-tuple-element.46), channel_id=1, replica_groups=mesh['blk'=32,'leaf'=4,'samp'=2] {'blk','leaf'}, use_global_device_ids=true, to_apply=%region_12.16 | all-reduce | flops 64 | bytes 512 | tf_op jit(solution)/shard_map/psum | solution.py:45
  1252.6 201.5 %all-reduce.9.cloned.1.call-done = f32[512,32]{0,1:T(8,128)} async-done(((f32[512,32]{0,1:T(8,128)}), f32[512,32]{0,1:T(8,128)}) %all-reduce.9.cloned.1.call-update) | async-done | bytes 65552 | tf_op jit(solution)/shard_map/psum | solution.py:45
  1461.5 342.7 %psum.62 = f32[32]{0:T(128)S(1)} all-reduce(f32[32]{0:T(128)S(1)} %get-tuple-element.101), channel_id=1, replica_groups=mesh['blk'=32,'leaf'=4,'samp'=2] {'blk','leaf'}, use_global_device_ids=true, to_apply=%region_17.22 | all-reduce | flops 32 | bytes 256 | tf_op jit(solution)/shard_map/psum | solution.py:45
  1805.6 12.6 all_gather.15
  1829.6 345.1 %psum.63 = f32[32]{0:T(128)S(1)} all-reduce(f32[32]{0:T(128)S(1)} %get-tuple-element.103), channel_id=1, replica_groups=mesh['blk'=32,'leaf'=4,'samp'=2] {'blk','leaf'}, use_global_device_ids=true, to_apply=%region_19.24 | all-reduce | flops 32 | bytes 256 | tf_op jit(solution)/shard_map/psum | solution.py:45
  (200 shorter events, 150.1 us)
Async XLA Ops:
  7.2 38.0 %all-gather.2.cloned.1.call-start = ((), (), s32[]{:S(2)}) async-start(), calls=%async_computation | async-start | bytes 2621440 | tf_op jit(solution)/shard_map/all_gather | solution.py:40
  9.3 333.2 %all-reduce.7.cloned.1.call-start = ((), (), s32[]{:S(2)}) async-start(), calls=%async_computation.1 | async-start | bytes 2097152 | tf_op jit(solution)/shard_map/psum | solution.py:45
  21.6 30.4 %collective-permute-start.3 = (f32[3,1024]{1,0:T(4,128)S(1)}, f32[3,1024]{1,0:T(4,128)S(1)}, u32[]{:S(2)}, u32[]{:S(2)}) collective-permute-start(f32[3,1024]{1,0:T(4,128)S(1)} %all_gather.13), channel_id=1, source_target_pairs={{8,0},{16,8},{24,16},{32,24},{40,32},{48,40},{56,48},{64,56},{72,6... | collective-permute-start | bytes 36872 | tf_op jit(solution)/shard_map/ppermute | solution.py:18
  29.7 22.3 %collective-permute-start.2 = (f32[3,1024]{1,0:T(4,128)S(1)}, f32[3,1024]{1,0:T(4,128)S(1)}, u32[]{:S(2)}, u32[]{:S(2)}) collective-permute-start(f32[3,1024]{1,0:T(4,128)S(1)} %all_gather.13), channel_id=1, source_target_pairs={{248,0},{0,8},{8,16},{16,24},{24,32},{32,40},{40,48},{48,56},{56,6... | collective-permute-start | bytes 36872 | tf_op jit(solution)/shard_map/ppermute | solution.py:18
  45.2 50.6 %collective-permute-start.1 = (f32[512,1024]{0,1:T(8,128)}, f32[512,1024]{0,1:T(8,128)}, u32[]{:S(2)}, u32[]{:S(2)}) collective-permute-start(f32[512,1024]{0,1:T(8,128)} %all-gather.2.cloned.1.call-done), channel_id=1, source_target_pairs={{8,0},{16,8},{24,16},{32,24},{40,32},{48,40},{56,48},{64,56},{72,6... | collective-permute-start | bytes 6291464 | tf_op jit(solution)/shard_map/ppermute | solution.py:18
  50.6 50.7 %collective-permute-start = (f32[512,1024]{0,1:T(8,128)}, f32[512,1024]{0,1:T(8,128)}, u32[]{:S(2)}, u32[]{:S(2)}) collective-permute-start(f32[512,1024]{0,1:T(8,128)} %all-gather.2.cloned.1.call-done), channel_id=1, source_target_pairs={{248,0},{0,8},{8,16},{16,24},{24,32},{32,40},{40,48},{48,56},{56,6... | collective-permute-start | bytes 6291464 | tf_op jit(solution)/shard_map/ppermute | solution.py:18
  53.9 47.4 %copy-start.7 = (f32[512,1024]{0,1:T(8,128)S(1)}, f32[512,1024]{0,1:T(8,128)}, u32[]{:S(2)}) copy-start(f32[512,1024]{0,1:T(8,128)} %all-gather.2.cloned.1.call-done) | copy-start | bytes 6291460
  113.5 5.6 copy-start.3
  124.5 0.8 copy-start.1
  127.4 590.7 %all-reduce.11.cloned.1.call-start = ((), (), s32[]{:S(2)}) async-start(), calls=%async_computation.3 | async-start | bytes 2228224 | tf_op jit(solution)/shard_map/psum | solution.py:45
  349.6 1.0 copy-start.5
  439.0 53.8 %copy-start.2 = (f32[512,256]{1,0:T(8,128)S(1)}, f32[512,256]{1,0:T(8,128)}, u32[]{:S(2)}) copy-start(f32[512,256]{1,0:T(8,128)} %copy-done.1) | copy-start | bytes 1572868
  492.4 5.7 copy-start.14
  492.5 5.7 copy-start.17
  492.8 6.6 copy-start.6
  494.4 5.0 copy-start.8
  496.1 222.1 %copy-start.12 = (f32[128,256]{1,0:T(8,128)}, f32[128,256]{1,0:T(8,128)S(1)}, u32[]{:S(2)}) copy-start(f32[128,256]{1,0:T(8,128)S(1)} %fusion.69) | copy-start | bytes 393220
  499.4 954.7 %all-reduce.9.cloned.1.call-start = ((), (), s32[]{:S(2)}) async-start(), calls=%async_computation.2 | async-start | bytes 131072 | tf_op jit(solution)/shard_map/psum | solution.py:45
  725.3 1.0 copy-start.4
  751.1 0.7 copy-start.9
  812.4 3.3 copy-start
  825.6 0.7 copy-start.13
  873.7 17.1 copy-start.10
  885.6 5.2 collective-permute-start.5
  888.3 8.3 collective-permute-start.4
  1249.7 0.6 copy-start.15
  1818.3 356.4 %copy-start.11 = (f32[32,256]{1,0:T(8,128)S(1)}, f32[32,256]{1,0:T(8,128)}, u32[]{:S(2)}) copy-start(f32[32,256]{1,0:T(8,128)} %copy-done.10) | copy-start | bytes 98308
  1818.3 356.4 %copy-start.16 = (f32[32,256]{1,0:T(8,128)S(1)}, f32[32,256]{1,0:T(8,128)}, u32[]{:S(2)}) copy-start(f32[32,256]{1,0:T(8,128)} %copy-done.15) | copy-start | bytes 98308
  1818.3 5.0 collective-permute-start.7
  1818.6 8.3 collective-permute-start.6
Sparse Core Ops, SparseCore 0:
  9.8 35.3 all-gather.1
  127.5 214.8 all-reduce.6
  499.5 218.5 all-reduce.10
  1252.7 201.3 all-reduce.8
where the time goes:
time: 2190 us; the launch traced here: 2180 us
  blocking collectives  1070 us (49%)
  waiting for transfers between devices  710 us (32%)
  other arithmetic  262 us (12%)
  matrix products  51.5 us (2%)
  local copies, waits for them, and re-layouts  51.3 us (2%)
    psum x3, blocking collectives, total(): return lax.psum(values, ('blk', 'leaf'))  1030 us
    psum x3, waiting for transfers between devices, total(): return lax.psum(values, ('blk', 'leaf'))  635 us
    another operation x15, other arithmetic, local(): wood_factor = jnp.linalg.cholesky(woodbury)  79.7 us
    another operation x14, other arithmetic, local(): factor = jnp.linalg.cholesky(core_gram)  79 us
    ppermute x8, waiting for transfers between devices, shifted_2(): return lax.ppermute(block, axis, route)  59.7 us
  transfers between devices with their start and end apart: 12, of which 10 were waited for; matrix products, arithmetic and copies ran while one was open for 0% of the time, Pallas kernels for 0%

commit v1 on v0

--- a/solution.py
+++ b/solution.py
@@ -10,6 +10,8 @@
 support_radius = 0.8
 noise_variance = 1.0
 sketch_shift = 1.0
+
+ALL_AXES = ("blk", "leaf", "samp")
 
 
 def shifted_2(block, axis, distance):
@@ -41,10 +43,6 @@
     return jnp.concatenate([shifted(slab_values, 1), slab_values, shifted(slab_values, -1)], axis=1)
 
 
-def total(values):
-    return lax.psum(values, ("blk", "leaf"))
-
-
 def lower_solve(factor, values):
     return lax.linalg.triangular_solve(factor, values, left_side=True, lower=True)
 
@@ -55,6 +53,8 @@
     slab_blocks = blk_dev * lax.axis_size("leaf")
     period = 2.0 * cycle_count
     own_slab = lax.axis_index("blk")
+    n_samp = lax.axis_size("samp")
+    samp_idx = lax.axis_index("samp")
     usable = neighbors >= 0
     relative = jnp.mod(neighbors // slab_blocks - own_slab + 1, cycle_count)
     chosen = jnp.where(usable, relative * slab_blocks + jnp.mod(neighbors, slab_blocks), 0)
@@ -63,52 +63,81 @@
     reach_blocks = reach_points.reshape(3, 3 * slab_blocks, PB).transpose(1, 0, 2)
     row_blocks = points.reshape(3, blk_dev, PB).transpose(1, 0, 2)
 
-    def build_tile(block_index):
-        kernel_tile = wendland(row_blocks[block_index], reach_blocks[chosen[block_index]], period)
-        return kernel_tile * usable_weight[block_index][:, None, None]
+    kernel_tile = wendland(row_blocks[0], reach_blocks[chosen[0]], period)
+    kernel_tile = kernel_tile * usable_weight[0][:, None, None]
 
     def apply_kernel(values):
         width = values.shape[0]
         reach = beside_all(values).reshape(width, 3 * slab_blocks, PB)
         picked = jnp.take(reach, chosen[0], axis=1)
-        pieces = jnp.einsum("cnj,nij->ci", picked, build_tile(0), precision=lax.Precision.HIGHEST)
-        return pieces
+        return jnp.einsum("cnj,nij->ci", picked, kernel_tile, precision=lax.Precision.HIGHEST)
+
+    def slot(x):
+        zeros = jnp.zeros((n_samp,) + x.shape, x.dtype)
+        return lax.dynamic_update_index_in_dim(zeros, x, samp_idx, 0)
+
+    def unslot(xs):
+        return lax.dynamic_index_in_dim(xs, samp_idx, 0, keepdims=False)
+
+    def total_per_samp(values):
+        return jax.tree.map(unslot, lax.psum(jax.tree.map(slot, values), ALL_AXES))
 
     sketch = apply_kernel(omega) + sketch_shift * omega
-    core_gram = total(high_dot(omega, sketch.T))
+    rhs = observed[None, :] - prior_draws
+    half = PB // n_samp
+    omega_half = lax.dynamic_slice_in_dim(omega, samp_idx * half, half, axis=1)
+    sketch_half = lax.dynamic_slice_in_dim(sketch, samp_idx * half, half, axis=1)
+    core_part = high_dot(omega_half, sketch_half.T)
+    square_part = high_dot(sketch_half, sketch_half.T)
+    rhs_part = slot(high_dot(sketch, rhs.T))
+    core_gram, square_gram, rhs_proj = lax.psum((core_part, square_part, rhs_part), ALL_AXES)
+    rhs_proj = unslot(rhs_proj)
+
     core_gram = 0.5 * (core_gram + core_gram.T)
     factor = jnp.linalg.cholesky(core_gram)
     basis = lower_solve(factor, sketch)
-    basis_gram = total(high_dot(basis, basis.T))
+    half_solved = lower_solve(factor, square_gram)
+    basis_gram = lower_solve(factor, half_solved.T)
     woodbury = noise_variance * jnp.eye(basis.shape[0], dtype=jnp.float32) + 0.5 * (
         basis_gram + basis_gram.T
     )
     wood_factor = jnp.linalg.cholesky(woodbury)
 
-    def inverse_apply(vectors):
-        projected = total(high_dot(basis, vectors.T))
+    def precond_from(vectors, projected):
         first_solve = lower_solve(wood_factor, projected)
         solved = lax.linalg.triangular_solve(
             wood_factor, first_solve, left_side=True, lower=True, transpose_a=True
         )
         return (vectors - high_dot(solved.T, basis)) / noise_variance
 
-    rhs = observed[None, :] - prior_draws
+    residual = rhs
+    projected = lower_solve(factor, rhs_proj)
+    precond = precond_from(residual, projected)
+    direction = precond
     weights = jnp.zeros_like(rhs)
-    residual = rhs
-    precond = inverse_apply(residual)
-    direction = precond
-    inner_now = total(jnp.sum(residual * precond, axis=1))
-    for step_index in range(ITERS):
-        image = apply_kernel(direction) + noise_variance * direction
-        step_size = inner_now / total(jnp.sum(direction * image, axis=1))
-        weights = weights + step_size[:, None] * direction
-        residual = residual - step_size[:, None] * image
-        if step_index + 1 < ITERS:
-            precond = inverse_apply(residual)
-            inner_next = total(jnp.sum(residual * precond, axis=1))
-            direction = precond + (inner_next / inner_now)[:, None] * direction
-            inner_now = inner_next
+
+    image = apply_kernel(direction) + noise_variance * direction
+    inner_now, curvature, image_proj = total_per_samp(
+        (
+            jnp.sum(residual * precond, axis=1),
+            jnp.sum(direction * image, axis=1),
+            high_dot(basis, image.T),
+        )
+    )
+    step_size = inner_now / curvature
+    weights = weights + step_size[:, None] * direction
+    residual = residual - step_size[:, None] * image
+    projected = projected - step_size[None, :] * image_proj
+    precond = precond_from(residual, projected)
+    inner_next = total_per_samp(jnp.sum(residual * precond, axis=1))
+    direction = precond + (inner_next / inner_now)[:, None] * direction
+    inner_now = inner_next
+
+    image = apply_kernel(direction) + noise_variance * direction
+    curvature = total_per_samp(jnp.sum(direction * image, axis=1))
+    step_size = inner_now / curvature
+    weights = weights + step_size[:, None] * direction
+    residual = residual - step_size[:, None] * image
     return (weights, residual)
 
 

time: 2190 us -> 1180 us (0.54)
  the two profiles are of different devices: /device:TPU:8 before, /device:TPU:4 now
where the time goes in v1:
time: 1180 us; the launch traced here: 1160 us
  waiting for transfers between devices  490 us (42%)
  other arithmetic  267 us (23%)
  blocking collectives  258 us (22%)
  local copies, waits for them, and re-layouts  59.4 us (5%)
  matrix products  55.7 us (5%)
  between operations  20.6 us (2%)
  starting transfers between devices  13.9 us (1%)
    psum x1, waiting for transfers between devices, local(): lax.psum((core_part, square_part, rhs_part), ALL_AXES)  259 us
    psum x3, blocking collectives, total_per_samp(): return jax.tree.map(unslot, lax.psum(jax.tree.map(slot, values), ALL_AXES))  221 us
    psum x1, waiting for transfers between devices, total_per_samp(): return jax.tree.map(unslot, lax.psum(jax.tree.map(slot, values), ALL_AXES))  158 us
    another operation x14, other arithmetic, local(): factor = jnp.linalg.cholesky(core_gram)  80.3 us
    another operation x15, other arithmetic, local(): wood_factor = jnp.linalg.cholesky(woodbury)  79.8 us
    ppermute x8, waiting for transfers between devices, shifted_2(): return lax.ppermute(block, axis, route)  54.2 us
    another operation x4, other arithmetic, lower_solve(): lax.linalg.triangular_solve(factor, values, left_side=True, lower=True)  41.8 us
    another operation x2, other arithmetic, precond_from(): lax.linalg.triangular_solve(wood_factor, first_solve, left_side=True, low...  41.7 us
  transfers between devices with their start and end apart: 11, of which 9 were waited for; matrix products, arithmetic and copies ran while one was open for 1% of the time, Pallas kernels for 0%

profile of v1, /device:TPU:4, one launch (start us, length us, event | category | flops | bytes accessed | tf_op | source)
XLA Modules:
  0.0 1164.1 jit_solution(11193395616657118959)
XLA Ops:
  9.3 12.6 %all_gather.13 = f32[3,1024]{1,0:T(4,128)S(1)} all-gather(f32[3,256]{1,0:T(4,128)} %param.14), channel_id=1, replica_groups=mesh['blk'=32,'leaf'=4,'samp'=2] {'leaf'}, dimensions={1}, use_global_device_ids=true | all-gather | bytes 15360 | tf_op jit(solution)/shard_map/all_gather | solution.py:42
  21.9 5.8 collective-permute-start.3
  27.7 18.4 %all-gather.2.cloned.1.call-done = f32[512,1024]{0,1:T(8,128)} async-done(((f32[512,256]{0,1:T(8,128)}), f32[512,1024]{0,1:T(8,128)}) %all-gather.2.cloned.1.call-update) | async-done | bytes 2097168 | tf_op jit(solution)/shard_map/all_gather | solution.py:42
  55.9 38.7 %collective-permute-done.1 = f32[512,1024]{0,1:T(8,128)} collective-permute-done((f32[512,1024]{0,1:T(8,128)}, f32[512,1024]{0,1:T(8,128)}, u32[]{:S(2)}, u32[]{:S(2)}) %collective-permute-start.1) | collective-permute-done | bytes 2097184 | tf_op jit(solution)/shard_map/ppermute | solution.py:20
  99.0 5.6 pad_maximum_fusion
  104.6 6.5 copy.12
  111.1 5.6 gather_fusion
  127.8 258.6 %all-reduce.8.cloned.1.call-done = (f32[512,512]{1,0:T(8,128)}, f32[2,512,32]{1,2,0:T(8,128)}, f32[512,512]{1,0:T(8,128)}) async-done(((f32[512,512]{1,0:T(8,128)}, f32[2,512,32]{1,2,0:T(8,128)}, f32[512,512]{1,0:T(8,128)}), (f32[512,512]{1,0:T(8,128)}, f32[2,512,32]{1,2,0:T(8,128)}, f32[512,512]{1,0:T(8,128)})) %all-reduce.8.cloned.1.call-update) | async-done | bytes 2228240 | tf_op jit(solution)/shard_map/psum | solution.py:93
  395.4 11.7 %cholesky.286 = f32[128,128]{1,0:T(8,128)S(1)} custom-call(f32[128,128]{1,0:T(8,128)S(1)} %cholesky.426), custom_call_target="Cholesky" | custom-call | tf_op jit(solution)/shard_map/jit(cholesky)/cholesky | solution.py:97
  407.1 9.8 custom-call.40
  419.6 11.7 %cholesky.305 = f32[128,128]{1,0:T(8,128)S(1)} custom-call(f32[128,128]{1,0:T(8,128)S(1)} %cholesky.430), custom_call_target="Cholesky" | custom-call | tf_op jit(solution)/shard_map/jit(cholesky)/cholesky | solution.py:97
  431.3 10.3 custom-call.41
  444.2 11.7 %cholesky.326 = f32[128,128]{1,0:T(8,128)S(1)} custom-call(f32[128,128]{1,0:T(8,128)S(1)} %cholesky.435), custom_call_target="Cholesky" | custom-call | tf_op jit(solution)/shard_map/jit(cholesky)/cholesky | solution.py:97
  457.2 9.8 custom-call.42
  469.2 11.9 %cholesky.343 = f32[128,128]{1,0:T(8,128)S(1)} custom-call(f32[128,128]{1,0:T(8,128)S(1)} %convolution_subtract_fusion.14), custom_call_target="Cholesky" | custom-call | tf_op jit(solution)/shard_map/jit(cholesky)/cholesky | solution.py:97
  488.2 11.7 %while.15 = (s32[]{:T(128)}, f32[512,512]{1,0:T(8,128)}, s32[4,2]{0,1:T(2,128)S(1)}, f32[4,128,128]{2,1,0:T(8,128)S(1)}, s32[]{:T(128)}) while((s32[]{:T(128)}, f32[512,512]{1,0:T(8,128)}, s32[4,2]{0,1:T(2,128)S(1)}, f32[4,128,128]{2,1,0:T(8,128)S(1)}, s32[]{:T(128)}) %tuple.84), condition=%wide.while_cond.clone, body=%wide.while_body.clone.sunk | while | flops 2 | bytes 131189 | solution.py:47
  500.0 39.3 %custom-call.44 = f32[4,128,128]{1,2,0:T(8,128)S(1)} custom-call(f32[4,128,128]{2,1,0:T(8,128)S(1)} %get-tuple-element.64), custom_call_target="InvertDiagBlocksLowerTriangular" | custom-call | tf_op jit(solution)/shard_map/triangular_solve/custom-call.3 | solution.py:47
  563.6 12.1 %cholesky.358 = f32[128,128]{1,0:T(8,128)S(1)} custom-call(f32[128,128]{1,0:T(8,128)S(1)} %cholesky.439), custom_call_target="Cholesky" | custom-call | tf_op jit(solution)/shard_map/jit(cholesky)/cholesky | solution.py:104
  576.4 9.8 custom-call.45
  589.6 11.7 %cholesky.377 = f32[128,128]{1,0:T(8,128)S(1)} custom-call(f32[128,128]{1,0:T(8,128)S(1)} %cholesky.443), custom_call_target="Cholesky" | custom-call | tf_op jit(solution)/shard_map/jit(cholesky)/cholesky | solution.py:104
  602.0 9.8 custom-call.46
  614.3 11.9 %cholesky.398 = f32[128,128]{1,0:T(8,128)S(1)} custom-call(f32[128,128]{1,0:T(8,128)S(1)} %cholesky.448), custom_call_target="Cholesky" | custom-call | tf_op jit(solution)/shard_map/jit(cholesky)/cholesky | solution.py:104
  626.9 9.8 custom-call.47
  638.1 11.7 %cholesky.415 = f32[128,128]{1,0:T(8,128)S(1)} custom-call(f32[128,128]{1,0:T(8,128)S(1)} %convolution_subtract_fusion.13), custom_call_target="Cholesky" | custom-call | tf_op jit(solution)/shard_map/jit(cholesky)/cholesky | solution.py:104
  654.6 10.8 while.16
  666.2 40.3 %custom-call.50 = f32[4,128,128]{1,2,0:T(8,128)S(1)} custom-call(f32[4,128,128]{2,1,0:T(8,128)} %copy-done.26), custom_call_target="InvertDiagBlocksLowerTriangular" | custom-call | tf_op jit(solution)/shard_map/triangular_solve/custom-call.9 | solution.py:108
  713.1 12.1 %all_gather.14 = f32[32,1024]{1,0:T(8,128)S(1)} all-gather(f32[32,256]{1,0:T(8,128)S(1)} %convolution_subtract_fusion.16), channel_id=1, replica_groups=mesh['blk'=32,'leaf'=4,'samp'=2] {'leaf'}, dimensions={1}, use_global_device_ids=true | all-gather | bytes 163840 | tf_op jit(solution)/shard_map/all_gather | solution.py:42
  745.3 74.1 %all-reduce.1 = (f32[2,32]{1,0:T(2,128)}, f32[2,32]{1,0:T(2,128)}) all-reduce(f32[2,32]{1,0:T(2,128)} %dynamic_update_slice.22, f32[2,32]{1,0:T(2,128)} %dynamic_update_slice.21), channel_id=1, replica_groups=mesh['blk'=32,'leaf'=4,'samp'=2] {'blk','leaf','samp'}, use_global_device_ids=true, to_apply=%region_14.20 | all-reduce | flops 128 | bytes 1024 | tf_op jit(solution)/shard_map/psum | solution.py:83
  822.1 158.5 %all-reduce.6.cloned.1.call-done = f32[2,512,32]{1,2,0:T(8,128)} async-done(((f32[2,512,32]{1,2,0:T(8,128)}), f32[2,512,32]{1,2,0:T(8,128)}) %all-reduce.6.cloned.1.call-update) | async-done | bytes 131088 | tf_op jit(solution)/shard_map/psum | solution.py:83
  985.2 73.6 %psum.62 = f32[2,32]{1,0:T(2,128)S(1)} all-reduce(f32[2,32]{1,0:T(2,128)S(1)} %dynamic_update_slice.24), channel_id=1, replica_groups=mesh['blk'=32,'leaf'=4,'samp'=2] {'blk','leaf','samp'}, use_global_device_ids=true, to_apply=%region_17.23 | all-reduce | flops 64 | bytes 512 | tf_op jit(solution)/shard_map/psum | solution.py:83
  1059.6 12.0 %all_gather.15 = f32[32,1024]{1,0:T(8,128)S(1)} all-gather(f32[32,256]{1,0:T(8,128)S(1)} %multiply_add_fusion.1), channel_id=1, replica_groups=mesh['blk'=32,'leaf'=4,'samp'=2] {'leaf'}, dimensions={1}, use_global_device_ids=true | all-gather | bytes 163840 | tf_op jit(solution)/shard_map/all_gather | solution.py:42
  1082.7 73.6 %psum.63 = f32[2,32]{1,0:T(2,128)S(1)} all-reduce(f32[2,32]{1,0:T(2,128)S(1)} %dynamic_update_slice.25), channel_id=1, replica_groups=mesh['blk'=32,'leaf'=4,'samp'=2] {'blk','leaf','samp'}, use_global_device_ids=true, to_apply=%region_19.25 | all-reduce | flops 64 | bytes 512 | tf_op jit(solution)/shard_map/psum | solution.py:83
  (276 shorter events, 154.3 us)
Async XLA Ops:
  7.2 39.0 %all-gather.2.cloned.1.call-start = ((), (), s32[]{:S(2)}) async-start(), calls=%async_computation | async-start | bytes 2621440 | tf_op jit(solution)/shard_map/all_gather | solution.py:42
  9.3 377.1 %all-reduce.8.cloned.1.call-start = ((), (), s32[]{:S(2)}) async-start(), calls=%async_computation.2 | async-start | bytes 4456448 | tf_op jit(solution)/shard_map/psum | solution.py:93
  21.9 29.5 %collective-permute-start.3 = (f32[3,1024]{1,0:T(4,128)S(1)}, f32[3,1024]{1,0:T(4,128)S(1)}, u32[]{:S(2)}, u32[]{:S(2)}) collective-permute-start(f32[3,1024]{1,0:T(4,128)S(1)} %all_gather.13), channel_id=1, source_target_pairs={{8,0},{16,8},{24,16},{32,24},{40,32},{48,40},{56,48},{64,56},{72,6... | collective-permute-start | bytes 36872 | tf_op jit(solution)/shard_map/ppermute | solution.py:20
  27.7 23.7 %collective-permute-start.2 = (f32[3,1024]{1,0:T(4,128)S(1)}, f32[3,1024]{1,0:T(4,128)S(1)}, u32[]{:S(2)}, u32[]{:S(2)}) collective-permute-start(f32[3,1024]{1,0:T(4,128)S(1)} %all_gather.13), channel_id=1, source_target_pairs={{248,0},{0,8},{8,16},{16,24},{24,32},{32,40},{40,48},{48,56},{56,6... | collective-permute-start | bytes 36872 | tf_op jit(solution)/shard_map/ppermute | solution.py:20
  46.2 48.5 %collective-permute-start.1 = (f32[512,1024]{0,1:T(8,128)}, f32[512,1024]{0,1:T(8,128)}, u32[]{:S(2)}, u32[]{:S(2)}) collective-permute-start(f32[512,1024]{0,1:T(8,128)} %all-gather.2.cloned.1.call-done), channel_id=1, source_target_pairs={{8,0},{16,8},{24,16},{32,24},{40,32},{48,40},{56,48},{64,56},{72,6... | collective-permute-start | bytes 6291464 | tf_op jit(solution)/shard_map/ppermute | solution.py:20
  49.5 49.5 %collective-permute-start = (f32[512,1024]{0,1:T(8,128)}, f32[512,1024]{0,1:T(8,128)}, u32[]{:S(2)}, u32[]{:S(2)}) collective-permute-start(f32[512,1024]{0,1:T(8,128)} %all-gather.2.cloned.1.call-done), channel_id=1, source_target_pairs={{248,0},{0,8},{8,16},{16,24},{24,32},{32,40},{40,48},{48,56},{56,6... | collective-permute-start | bytes 6291464 | tf_op jit(solution)/shard_map/ppermute | solution.py:20
  51.3 65.4 %copy-start.36 = (pred[8]{0:T(512)(128)(4,1)}, pred[8]{0:T(512)(128)(4,1)S(1)}, u32[]{:S(2)}) copy-start(pred[8]{0:T(512)(128)(4,1)S(1)} %compare_and_fusion) | copy-start | bytes 28
  53.3 45.7 %copy-start.11 = (f32[512,1024]{0,1:T(8,128)S(1)}, f32[512,1024]{0,1:T(8,128)}, u32[]{:S(2)}) copy-start(f32[512,1024]{0,1:T(8,128)} %all-gather.2.cloned.1.call-done) | copy-start | bytes 6291460
  111.1 5.6 copy-start.7
  127.5 853.0 %all-reduce.6.cloned.1.call-start = ((), (), s32[]{:S(2)}) async-start(), calls=%async_computation.1 | async-start | bytes 262144 | tf_op jit(solution)/shard_map/psum | solution.py:83
  444.1 95.2 %copy-start.1 = (f32[512,256]{1,0:T(8,128)S(1)}, f32[512,256]{1,0:T(8,128)}, u32[]{:S(2)}) copy-start(f32[512,256]{1,0:T(8,128)} %copy-done) | copy-start | bytes 1572868
  500.0 48.0 %copy-start.32 = (s32[4,2]{0,1:T(2,128)}, s32[4,2]{0,1:T(2,128)S(1)}, u32[]{:S(2)}) copy-start(s32[4,2]{0,1:T(2,128)S(1)} %get-tuple-element.250) | copy-start | bytes 100
  539.3 6.7 copy-start.2
  539.3 8.7 copy-start.15
  706.5 20.8 %copy-start.38 = (s32[8]{0:T(128)S(1)}, s32[8]{0:T(128)}, u32[]{:S(2)}) copy-start(s32[8]{0:T(128)} %get-tuple-element.93) | copy-start | bytes 100
  713.1 17.1 %copy-start.17 = (f32[32,256]{1,0:T(8,128)}, f32[32,256]{1,0:T(8,128)S(1)}, u32[]{:S(2)}) copy-start(f32[32,256]{1,0:T(8,128)S(1)} %convolution_subtract_fusion.16) | copy-start | bytes 98308
  725.2 5.0 collective-permute-start.5
  726.0 7.1 collective-permute-start.4
  736.2 4.3 copy-start.13
  736.2 4.3 copy-start.21
  736.2 4.3 copy-start.28
  980.6 4.1 copy-start.14
  980.6 4.1 copy-start.22
  980.6 4.1 copy-start.29
  980.6 4.1 copy-start.30
  981.6 77.2 %copy-start.39 = (f32[2,32]{1,0:T(2,128)S(1)}, f32[2,32]{1,0:T(2,128)}, u32[]{:S(2)}) copy-start(f32[2,32]{1,0:T(2,128)} %get-tuple-element.89) | copy-start | bytes 772
  983.5 97.2 %copy-start.37 = (pred[8]{0:T(512)(128)(4,1)S(1)}, pred[8]{0:T(512)(128)(4,1)}, u32[]{:S(2)}) copy-start(pred[8]{0:T(512)(128)(4,1)} %copy-done.36) | copy-start | bytes 28
  1071.6 84.7 %copy-start.18 = (f32[32,256]{1,0:T(8,128)S(1)}, f32[32,256]{1,0:T(8,128)}, u32[]{:S(2)}) copy-start(f32[32,256]{1,0:T(8,128)} %copy-done.17) | copy-start | bytes 98308
  1071.6 84.8 %copy-start.31 = (f32[32,256]{1,0:T(8,128)S(1)}, f32[32,256]{1,0:T(8,128)}, u32[]{:S(2)}) copy-start(f32[32,256]{1,0:T(8,128)} %multiply_subtract_fusion.1) | copy-start | bytes 98308
  1071.6 84.8 %copy-start.35 = (f32[32]{0:T(128)S(1)}, f32[32]{0:T(128)}, u32[]{:S(2)}) copy-start(f32[32]{0:T(128)} %copy-done.34) | copy-start | bytes 388
  1071.6 5.3 collective-permute-start.7
  1072.8 7.1 collective-permute-start.6
  (19 other events, 36.1 us)
Sparse Core Ops, SparseCore 0:
  9.8 36.3 all-gather.1
  127.6 258.6 all-reduce.7
  741.9 238.6 all-reduce.5

commit v2 on v1

--- a/solution.py
+++ b/solution.py
@@ -89,29 +89,22 @@
     sketch_half = lax.dynamic_slice_in_dim(sketch, samp_idx * half, half, axis=1)
     core_part = high_dot(omega_half, sketch_half.T)
     square_part = high_dot(sketch_half, sketch_half.T)
+    joint_part = 0.5 * (core_part + core_part.T) + 0.5 * (square_part + square_part.T)
     rhs_part = slot(high_dot(sketch, rhs.T))
-    core_gram, square_gram, rhs_proj = lax.psum((core_part, square_part, rhs_part), ALL_AXES)
+    joint_gram, rhs_proj = lax.psum((joint_part, rhs_part), ALL_AXES)
     rhs_proj = unslot(rhs_proj)
 
-    core_gram = 0.5 * (core_gram + core_gram.T)
-    factor = jnp.linalg.cholesky(core_gram)
-    basis = lower_solve(factor, sketch)
-    half_solved = lower_solve(factor, square_gram)
-    basis_gram = lower_solve(factor, half_solved.T)
-    woodbury = noise_variance * jnp.eye(basis.shape[0], dtype=jnp.float32) + 0.5 * (
-        basis_gram + basis_gram.T
-    )
-    wood_factor = jnp.linalg.cholesky(woodbury)
+    joint_factor = jnp.linalg.cholesky(joint_gram)
 
     def precond_from(vectors, projected):
-        first_solve = lower_solve(wood_factor, projected)
+        first_solve = lower_solve(joint_factor, projected)
         solved = lax.linalg.triangular_solve(
-            wood_factor, first_solve, left_side=True, lower=True, transpose_a=True
+            joint_factor, first_solve, left_side=True, lower=True, transpose_a=True
         )
-        return (vectors - high_dot(solved.T, basis)) / noise_variance
+        return (vectors - high_dot(solved.T, sketch)) / noise_variance
 
     residual = rhs
-    projected = lower_solve(factor, rhs_proj)
+    projected = rhs_proj
     precond = precond_from(residual, projected)
     direction = precond
     weights = jnp.zeros_like(rhs)
@@ -121,7 +114,7 @@
         (
             jnp.sum(residual * precond, axis=1),
             jnp.sum(direction * image, axis=1),
-            high_dot(basis, image.T),
+            high_dot(sketch, image.T),
         )
     )
     step_size = inner_now / curvature

time: 1180 us -> 1010 us (0.86)
  other arithmetic: 267 us -> 141 us
  local copies, waits for them, and re-layouts: 59.4 us -> 40.1 us
  matrix products: 55.7 us -> 40.6 us
    another operation x35 -> x18, other arithmetic: 244 us -> 123 us  [the longest x14 80.7 us: local(): joint_factor = jnp.linalg.cholesky(joint_gram)]
    another operation x42 -> x14, matrix products: 21.4 us -> 8.2 us  [lower_solve(): lax.linalg.triangular_solve(factor, values, left_side=True, lower=True)]
    another operation x42 -> x23, local copies, waits for them, and re-layouts: 25.8 us -> 13.2 us  [the longest x13 12 us: precond_from(): lax.linalg.triangular_solve(joint_factor, first_solve, left_side=True, lo...]
where the time goes in v2:
time: 1010 us; the launch traced here: 1000 us
  waiting for transfers between devices  492 us (49%)
  blocking collectives  258 us (26%)
  other arithmetic  141 us (14%)
  matrix products  40.6 us (4%)
  local copies, waits for them, and re-layouts  40.1 us (4%)
  between operations  17.2 us (2%)
  starting transfers between devices  13.9 us (1%)
    psum x1, waiting for transfers between devices, local(): joint_gram, rhs_proj = lax.psum((joint_part, rhs_part), ALL_AXES)  255 us
    psum x3, blocking collectives, total_per_samp(): return jax.tree.map(unslot, lax.psum(jax.tree.map(slot, values), ALL_AXES))  222 us
    psum x1, waiting for transfers between devices, total_per_samp(): return jax.tree.map(unslot, lax.psum(jax.tree.map(slot, values), ALL_AXES))  164 us
    another operation x14, other arithmetic, local(): joint_factor = jnp.linalg.cholesky(joint_gram)  80.7 us
    ppermute x8, waiting for transfers between devices, shifted_2(): return lax.ppermute(block, axis, route)  54.8 us
    another operation x4, other arithmetic, precond_from(): lax.linalg.triangular_solve(joint_factor, first_solve, left_side=True, lo...  41.8 us
    all_gather x3, blocking collectives, beside_all(): slab_values = lax.all_gather(values, 'leaf', axis=1, tiled=True)  36.6 us
  transfers between devices with their start and end apart: 11, of which 9 were waited for; matrix products, arithmetic and copies ran while one was open for 1% of the time, Pallas kernels for 0%

profile of v2, /device:TPU:4, one launch (start us, length us, event | category | flops | bytes accessed | tf_op | source)
XLA Modules:
  0.0 1003.0 jit_solution(9335899095662480256)
XLA Ops:
  9.3 12.6 %all_gather.13 = f32[3,1024]{1,0:T(4,128)S(1)} all-gather(f32[3,256]{1,0:T(4,128)} %param.11), channel_id=1, replica_groups=mesh['blk'=32,'leaf'=4,'samp'=2] {'leaf'}, dimensions={1}, use_global_device_ids=true | all-gather | bytes 15360 | tf_op jit(solution)/shard_map/all_gather | solution.py:42
  21.9 5.8 collective-permute-start.3
  27.7 18.4 %all-gather.2.cloned.1.call-done = f32[512,1024]{0,1:T(8,128)} async-done(((f32[512,256]{0,1:T(8,128)}), f32[512,1024]{0,1:T(8,128)}) %all-gather.2.cloned.1.call-update) | async-done | bytes 2097168 | tf_op jit(solution)/shard_map/all_gather | solution.py:42
  46.2 3.3 collective-permute-start.1
  53.0 2.6 multiply_multiply_fusion
  55.6 39.1 %collective-permute-done.1 = f32[512,1024]{0,1:T(8,128)} collective-permute-done((f32[512,1024]{0,1:T(8,128)}, f32[512,1024]{0,1:T(8,128)}, u32[]{:S(2)}, u32[]{:S(2)}) %collective-permute-start.1) | collective-permute-done | bytes 2097184 | tf_op jit(solution)/shard_map/ppermute | solution.py:20
  94.7 4.5 collective-permute-done
  99.2 5.6 pad_maximum_fusion
  104.8 6.5 copy.11
  111.3 5.6 gather_fusion
  116.9 5.5 fusion.17
  131.4 3.7 fusion.26
  136.7 254.7 %all-reduce.8.cloned.1.call-done = (f32[512,512]{1,0:T(8,128)}, f32[2,512,32]{1,2,0:T(8,128)}) async-done(((f32[512,512]{1,0:T(8,128)}, f32[2,512,32]{1,2,0:T(8,128)}), (f32[512,512]{1,0:T(8,128)}, f32[2,512,32]{1,2,0:T(8,128)})) %all-reduce.8.cloned.1.call-update) | async-done | bytes 1179664 | tf_op jit(solution)/shard_map/psum | solution.py:94
  397.6 11.7 %cholesky.104 = f32[128,128]{1,0:T(8,128)S(1)} custom-call(f32[128,128]{1,0:T(8,128)S(1)} %cholesky.266), custom_call_target="Cholesky" | custom-call | tf_op jit(solution)/shard_map/jit(cholesky)/cholesky | solution.py:97
  409.4 9.8 custom-call.33
  423.6 11.7 %cholesky.217 = f32[128,128]{1,0:T(8,128)S(1)} custom-call(f32[128,128]{1,0:T(8,128)S(1)} %cholesky.270), custom_call_target="Cholesky" | custom-call | tf_op jit(solution)/shard_map/jit(cholesky)/cholesky | solution.py:97
  436.0 10.2 %custom-call.34 = f32[1,128,128]{1,2,0:T(8,128)S(1)} custom-call(f32[1,128,128]{2,1,0:T(8,128)S(1)} %get-tuple-element.61), custom_call_target="InvertDiagBlocksLowerTriangular" | custom-call | tf_op jit(solution)/shard_map/jit(cholesky)/cholesky | solution.py:97
  448.6 11.7 %cholesky.238 = f32[128,128]{1,0:T(8,128)S(1)} custom-call(f32[128,128]{1,0:T(8,128)S(1)} %cholesky.275), custom_call_target="Cholesky" | custom-call | tf_op jit(solution)/shard_map/jit(cholesky)/cholesky | solution.py:97
  461.7 9.8 custom-call.35
  473.7 11.7 %cholesky.255 = f32[128,128]{1,0:T(8,128)S(1)} custom-call(f32[128,128]{1,0:T(8,128)S(1)} %convolution_subtract_fusion.2), custom_call_target="Cholesky" | custom-call | tf_op jit(solution)/shard_map/jit(cholesky)/cholesky | solution.py:97
  492.5 12.0 %while.8 = (s32[]{:T(128)}, f32[512,512]{1,0:T(8,128)}, s32[4,2]{0,1:T(2,128)S(1)}, f32[4,128,128]{2,1,0:T(8,128)S(1)}, s32[]{:T(128)}) while((s32[]{:T(128)}, f32[512,512]{1,0:T(8,128)}, s32[4,2]{0,1:T(2,128)S(1)}, f32[4,128,128]{2,1,0:T(8,128)S(1)}, s32[]{:T(128)}) %tuple.51), condition=%wide.while_cond.1, body=%wide.while_body.1.sunk | while | flops 2 | bytes 131189 | solution.py:101
  504.6 39.3 %custom-call.39 = f32[4,128,128]{1,2,0:T(8,128)S(1)} custom-call(f32[4,128,128]{2,1,0:T(8,128)S(1)} %get-tuple-element.34), custom_call_target="InvertDiagBlocksLowerTriangular" | custom-call | tf_op jit(solution)/shard_map/triangular_solve/custom-call.8 | solution.py:101
  552.6 12.0 %all_gather.14 = f32[32,1024]{1,0:T(8,128)S(1)} all-gather(f32[32,256]{1,0:T(8,128)S(1)} %convolution_subtract_fusion.4), channel_id=1, replica_groups=mesh['blk'=32,'leaf'=4,'samp'=2] {'leaf'}, dimensions={1}, use_global_device_ids=true | all-gather | bytes 163840 | tf_op jit(solution)/shard_map/all_gather | solution.py:42
  566.7 2.9 collective-permute-done.5
  572.6 2.8 multiply_reduce_fusion.3
  576.9 74.5 %all-reduce.1 = (f32[2,32]{1,0:T(2,128)S(1)}, f32[2,32]{1,0:T(2,128)S(1)}) all-reduce(f32[2,32]{1,0:T(2,128)S(1)} %dynamic_update_slice.22, f32[2,32]{1,0:T(2,128)S(1)} %dynamic_update_slice.21), channel_id=1, replica_groups=mesh['blk'=32,'leaf'=4,'samp'=2] {'blk','leaf','samp'}, use_global_device_ids=true, to_apply=%region_13.17 | all-reduce | flops 128 | bytes 1024 | tf_op jit(solution)/shard_map/psum | solution.py:83
  651.5 164.1 %all-reduce.6.cloned.1.call-done = f32[2,512,32]{1,2,0:T(8,128)} async-done(((f32[2,512,32]{1,2,0:T(8,128)}), f32[2,512,32]{1,2,0:T(8,128)}) %all-reduce.6.cloned.1.call-update) | async-done | bytes 131088 | tf_op jit(solution)/shard_map/psum | solution.py:83
  825.4 73.5 %psum.54 = f32[2,32]{1,0:T(2,128)S(1)} all-reduce(f32[2,32]{1,0:T(2,128)S(1)} %dynamic_update_slice.24), channel_id=1, replica_groups=mesh['blk'=32,'leaf'=4,'samp'=2] {'blk','leaf','samp'}, use_global_device_ids=true, to_apply=%region_16.20 | all-reduce | flops 64 | bytes 512 | tf_op jit(solution)/shard_map/psum | solution.py:83
  899.0 12.0 %all_gather.15 = f32[32,1024]{1,0:T(8,128)S(1)} all-gather(f32[32,256]{1,0:T(8,128)S(1)} %multiply_add_fusion.1), channel_id=1, replica_groups=mesh['blk'=32,'leaf'=4,'samp'=2] {'leaf'}, dimensions={1}, use_global_device_ids=true | all-gather | bytes 163840 | tf_op jit(solution)/shard_map/all_gather | solution.py:42
  913.3 2.9 collective-permute-done.7
  916.2 3.0 collective-permute-done.6
  921.9 73.6 %psum.55 = f32[2,32]{1,0:T(2,128)S(1)} all-reduce(f32[2,32]{1,0:T(2,128)S(1)} %dynamic_update_slice.25), channel_id=1, replica_groups=mesh['blk'=32,'leaf'=4,'samp'=2] {'blk','leaf','samp'}, use_global_device_ids=true, to_apply=%region_18.22 | all-reduce | flops 64 | bytes 512 | tf_op jit(solution)/shard_map/psum | solution.py:83
  (144 shorter events, 80.3 us)
Async XLA Ops:
  7.2 39.0 %all-gather.2.cloned.1.call-start = ((), (), s32[]{:S(2)}) async-start(), calls=%async_computation | async-start | bytes 2621440 | tf_op jit(solution)/shard_map/all_gather | solution.py:42
  9.3 382.2 %all-reduce.8.cloned.1.call-start = ((), (), s32[]{:S(2)}) async-start(), calls=%async_computation.2 | async-start | bytes 2359296 | tf_op jit(solution)/shard_map/psum | solution.py:94
  21.9 29.1 %collective-permute-start.3 = (f32[3,1024]{1,0:T(4,128)S(1)}, f32[3,1024]{1,0:T(4,128)S(1)}, u32[]{:S(2)}, u32[]{:S(2)}) collective-permute-start(f32[3,1024]{1,0:T(4,128)S(1)} %all_gather.13), channel_id=1, source_target_pairs={{8,0},{16,8},{24,16},{32,24},{40,32},{48,40},{56,48},{64,56},{72,6... | collective-permute-start | bytes 36872 | tf_op jit(solution)/shard_map/ppermute | solution.py:20
  27.7 23.3 %collective-permute-start.2 = (f32[3,1024]{1,0:T(4,128)S(1)}, f32[3,1024]{1,0:T(4,128)S(1)}, u32[]{:S(2)}, u32[]{:S(2)}) collective-permute-start(f32[3,1024]{1,0:T(4,128)S(1)} %all_gather.13), channel_id=1, source_target_pairs={{248,0},{0,8},{8,16},{16,24},{24,32},{32,40},{40,48},{48,56},{56,6... | collective-permute-start | bytes 36872 | tf_op jit(solution)/shard_map/ppermute | solution.py:20
  46.2 48.5 %collective-permute-start.1 = (f32[512,1024]{0,1:T(8,128)}, f32[512,1024]{0,1:T(8,128)}, u32[]{:S(2)}, u32[]{:S(2)}) collective-permute-start(f32[512,1024]{0,1:T(8,128)} %all-gather.2.cloned.1.call-done), channel_id=1, source_target_pairs={{8,0},{16,8},{24,16},{32,24},{40,32},{48,40},{56,48},{64,56},{72,6... | collective-permute-start | bytes 6291464 | tf_op jit(solution)/shard_map/ppermute | solution.py:20
  49.5 49.7 %collective-permute-start = (f32[512,1024]{0,1:T(8,128)}, f32[512,1024]{0,1:T(8,128)}, u32[]{:S(2)}, u32[]{:S(2)}) collective-permute-start(f32[512,1024]{0,1:T(8,128)} %all-gather.2.cloned.1.call-done), channel_id=1, source_target_pairs={{248,0},{0,8},{8,16},{16,24},{24,32},{32,40},{40,48},{48,56},{56,6... | collective-permute-start | bytes 6291464 | tf_op jit(solution)/shard_map/ppermute | solution.py:20
  52.9 46.2 %copy-start.2 = (f32[512,1024]{0,1:T(8,128)S(1)}, f32[512,1024]{0,1:T(8,128)}, u32[]{:S(2)}) copy-start(f32[512,1024]{0,1:T(8,128)} %all-gather.2.cloned.1.call-done) | copy-start | bytes 6291460
  111.3 5.6 copy-start
  131.4 3.7 copy-start.5
  131.4 3.7 copy-start.10
  135.7 0.6 copy-start.7
  136.4 679.1 %all-reduce.6.cloned.1.call-start = ((), (), s32[]{:S(2)}) async-start(), calls=%async_computation.1 | async-start | bytes 262144 | tf_op jit(solution)/shard_map/psum | solution.py:83
  396.6 1.0 copy-start.1
  552.6 17.0 %copy-start.3 = (f32[32,256]{1,0:T(8,128)}, f32[32,256]{1,0:T(8,128)S(1)}, u32[]{:S(2)}) copy-start(f32[32,256]{1,0:T(8,128)S(1)} %convolution_subtract_fusion.4) | copy-start | bytes 98308
  564.6 5.0 collective-permute-start.5
  564.9 7.1 collective-permute-start.4
  572.6 78.8 %copy-start.6 = (f32[32,256]{1,0:T(8,128)S(1)}, f32[32,256]{1,0:T(8,128)}, u32[]{:S(2)}) copy-start(f32[32,256]{1,0:T(8,128)} %param.15) | copy-start | bytes 98308
  572.6 242.9 %copy-start.9 = (f32[2,512,32]{1,2,0:T(8,128)S(1)}, f32[2,512,32]{1,2,0:T(8,128)}, u32[]{:S(2)}) copy-start(f32[2,512,32]{1,2,0:T(8,128)} %get-tuple-element.50) | copy-start | bytes 393220
  575.4 323.5 %copy-start.4 = (f32[32,256]{1,0:T(8,128)S(1)}, f32[32,256]{1,0:T(8,128)}, u32[]{:S(2)}) copy-start(f32[32,256]{1,0:T(8,128)} %copy-done.3) | copy-start | bytes 98308
  576.1 0.7 copy-start.8
  911.1 5.2 collective-permute-start.7
  912.1 7.1 collective-permute-start.6
Sparse Core Ops, SparseCore 0:
  9.8 36.3 all-gather.1
  136.5 254.8 all-reduce.7
  576.9 238.6 all-reduce.5

commit v3 on v2

--- a/solution.py
+++ b/solution.py
@@ -2,6 +2,8 @@
 import jax.numpy as jnp
 from jax import lax
 from jax.sharding import PartitionSpec as P
+from jax.experimental import pallas as pl
+from jax.experimental.pallas import tpu as pltpu
 
 PB = 256
 ITERS = 2
@@ -41,6 +43,81 @@
 def beside_all(values):
     slab_values = lax.all_gather(values, "leaf", axis=1, tiled=True)
     return jnp.concatenate([shifted(slab_values, 1), slab_values, shifted(slab_values, -1)], axis=1)
+
+
+def blk_split(n_blk):
+    if n_blk % 8 == 0 and n_blk > 8:
+        return (8, n_blk // 8)
+    return (n_blk, 1)
+
+
+def reduce_phases():
+    inner, outer = blk_split(lax.axis_size("blk"))
+    phases = [("leaf", lax.axis_size("leaf"), 1), ("blk", inner, 1)]
+    if outer > 1:
+        phases.append(("blk", outer, inner))
+    return tuple(p for p in phases if p[1] > 1)
+
+
+def group_peer(axis, n, stride, k):
+    idx = lax.axis_index(axis)
+    own = (idx // stride) % n
+    return own, idx + ((own + k) % n - own) * stride
+
+
+def sum_kernel(phases, x_ref, o_ref, recv, send_sem, recv_sem):
+    barrier = pltpu.get_barrier_semaphore()
+    greeted = 0
+    for axis, n, stride in phases:
+        for k in range(1, n):
+            _, peer = group_peer(axis, n, stride, k)
+            pl.semaphore_signal(
+                barrier, 1, device_id={axis: peer}, device_id_type=pl.DeviceIdType.MESH
+            )
+            greeted += 1
+    pl.semaphore_wait(barrier, greeted)
+    acc = x_ref[...]
+    for p, (axis, n, stride) in enumerate(phases):
+        recv[p, 0] = acc
+        copies = []
+        for k in range(1, n):
+            own, peer = group_peer(axis, n, stride, k)
+            copy = pltpu.make_async_remote_copy(
+                src_ref=x_ref if p == 0 else recv.at[p, 0],
+                dst_ref=recv.at[p, k],
+                send_sem=send_sem.at[p, k],
+                recv_sem=recv_sem.at[p, k],
+                device_id={axis: peer},
+                device_id_type=pl.DeviceIdType.MESH,
+            )
+            copy.start()
+            copies.append(copy)
+        for copy in copies:
+            copy.wait()
+        own, _ = group_peer(axis, n, stride, 0)
+        terms = [recv[p, (own - j) % n] for j in range(n)]
+        acc = terms[0]
+        for term in terms[1:]:
+            acc = acc + term
+    o_ref[...] = acc
+
+
+def group_sum(values, collective_id):
+    phases = reduce_phases()
+    rows = values.shape[0]
+    widest = max(n for _, n, _ in phases)
+    return pl.pallas_call(
+        lambda *refs: sum_kernel(phases, *refs),
+        out_shape=jax.ShapeDtypeStruct(values.shape, jnp.float32),
+        in_specs=[pl.BlockSpec(memory_space=pltpu.VMEM)],
+        out_specs=pl.BlockSpec(memory_space=pltpu.VMEM),
+        scratch_shapes=[
+            pltpu.VMEM((len(phases), widest, rows, 128), jnp.float32),
+            pltpu.SemaphoreType.DMA((len(phases), widest)),
+            pltpu.SemaphoreType.DMA((len(phases), widest)),
+        ],
+        compiler_params=pltpu.CompilerParams(collective_id=collective_id, has_side_effects=True),
+    )(values)
 
 
 def lower_solve(factor, values):
@@ -109,25 +186,38 @@
     direction = precond
     weights = jnp.zeros_like(rhs)
 
+    width = rhs.shape[0]
+    sketch_rows = sketch.shape[0]
+
+    def pack_scalars(*vectors):
+        rows = jnp.stack(vectors)
+        return jnp.pad(rows, ((0, 8 - rows.shape[0]), (0, 128 - width)))
+
     image = apply_kernel(direction) + noise_variance * direction
-    inner_now, curvature, image_proj = total_per_samp(
-        (
-            jnp.sum(residual * precond, axis=1),
-            jnp.sum(direction * image, axis=1),
-            high_dot(sketch, image.T),
-        )
+    image_proj = high_dot(sketch, image.T).reshape(sketch_rows * width // 128, 128)
+    packed = jnp.concatenate(
+        [
+            image_proj,
+            pack_scalars(
+                jnp.sum(residual * precond, axis=1), jnp.sum(direction * image, axis=1)
+            ),
+        ]
     )
+    packed = group_sum(packed, 0)
+    image_proj = packed[:-8].reshape(sketch_rows, width)
+    inner_now = packed[-8, :width]
+    curvature = packed[-7, :width]
     step_size = inner_now / curvature
     weights = weights + step_size[:, None] * direction
     residual = residual - step_size[:, None] * image
     projected = projected - step_size[None, :] * image_proj
     precond = precond_from(residual, projected)
-    inner_next = total_per_samp(jnp.sum(residual * precond, axis=1))
+    inner_next = group_sum(pack_scalars(jnp.sum(residual * precond, axis=1)), 1)[0, :width]
     direction = precond + (inner_next / inner_now)[:, None] * direction
     inner_now = inner_next
 
     image = apply_kernel(direction) + noise_variance * direction
-    curvature = total_per_samp(jnp.sum(direction * image, axis=1))
+    curvature = group_sum(pack_scalars(jnp.sum(direction * image, axis=1)), 1)[0, :width]
     step_size = inner_now / curvature
     weights = weights + step_size[:, None] * direction
     residual = residual - step_size[:, None] * image

time: 1010 us -> 693 us (0.69)
  blocking collectives: 258 us -> 36.6 us
  waiting for transfers between devices: 492 us -> 329 us
  Pallas kernels: 0 us -> 61.3 us
    psum x3 -> x0, blocking collectives: 222 us -> none  [total_per_samp(): return jax.tree.map(unslot, lax.psum(jax.tree.map(slot, values), ALL_AXES))]
    psum x1 -> x0, waiting for transfers between devices: 164 us -> none  [total_per_samp(): return jax.tree.map(unslot, lax.psum(jax.tree.map(slot, values), ALL_AXES))]
    pallas_call x0 -> x3, Pallas kernels: none -> 61.3 us  [group_sum(): pl.pallas_call(lambda *refs: sum_kernel(phases, *refs), out_shape=jax.Sha...]
  transfers between devices with their start and end apart: 11 -> 10, of which waited for: 9 -> 8; matrix products, arithmetic and copies ran while one was open for 1% -> 1% of each run, Pallas kernels for 0% -> 0%
where the time goes in v3:
time: 693 us; the launch traced here: 685 us
  waiting for transfers between devices  329 us (47%)
  other arithmetic  143 us (21%)
  Pallas kernels  61.3 us (9%)
  local copies, waits for them, and re-layouts  42.2 us (6%)
  matrix products  42.1 us (6%)
  blocking collectives  36.6 us (5%)
  between operations  17.3 us (2%)
  starting transfers between devices  13.4 us (2%)
    psum x1, waiting for transfers between devices, local(): joint_gram, rhs_proj = lax.psum((joint_part, rhs_part), ALL_AXES)  255 us
    another operation x14, other arithmetic, local(): joint_factor = jnp.linalg.cholesky(joint_gram)  80.8 us
    pallas_call x3, Pallas kernels, group_sum(): pl.pallas_call(lambda *refs: sum_kernel(phases, *refs), out_shape=jax.Sha...  61.3 us
    ppermute x8, waiting for transfers between devices, shifted_2(): return lax.ppermute(block, axis, route)  55.6 us
    another operation x4, other arithmetic, precond_from(): lax.linalg.triangular_solve(joint_factor, first_solve, left_side=True, lo...  41.7 us
    all_gather x3, blocking collectives, beside_all(): slab_values = lax.all_gather(values, 'leaf', axis=1, tiled=True)  36.6 us
    all_gather x1, waiting for transfers between devices, beside_all(): slab_values = lax.all_gather(values, 'leaf', axis=1, tiled=True)  18.4 us
  transfers between devices with their start and end apart: 10, of which 8 were waited for; matrix products, arithmetic and copies ran while one was open for 1% of the time, Pallas kernels for 0%

profile of v3, /device:TPU:4, one launch (start us, length us, event | category | flops | bytes accessed | tf_op | source)
XLA Modules:
  0.0 685.4 jit_solution(12376500162995527022)
XLA Ops:
  9.3 12.6 %all_gather.13 = f32[3,1024]{1,0:T(4,128)S(1)} all-gather(f32[3,256]{1,0:T(4,128)} %param.11), channel_id=1, replica_groups=mesh['blk'=32,'leaf'=4,'samp'=2] {'leaf'}, dimensions={1}, use_global_device_ids=true | all-gather | bytes 15360 | tf_op jit(solution)/shard_map/all_gather | solution.py:44
  21.9 5.8 collective-permute-start.3
  27.7 18.4 %all-gather.2.cloned.1.call-done = f32[512,1024]{0,1:T(8,128)} async-done(((f32[512,256]{0,1:T(8,128)}), f32[512,1024]{0,1:T(8,128)}) %all-gather.2.cloned.1.call-update) | async-done | bytes 2097168 | tf_op jit(solution)/shard_map/all_gather | solution.py:44
  46.2 3.3 collective-permute-start.1
  52.8 2.6 multiply_multiply_fusion
  55.4 39.3 %collective-permute-done.1 = f32[512,1024]{0,1:T(8,128)} collective-permute-done((f32[512,1024]{0,1:T(8,128)}, f32[512,1024]{0,1:T(8,128)}, u32[]{:S(2)}, u32[]{:S(2)}) %collective-permute-start.1) | collective-permute-done | bytes 2097184 | tf_op jit(solution)/shard_map/ppermute | solution.py:22
  94.7 4.3 collective-permute-done
  99.0 5.6 pad_maximum_fusion
  104.6 6.5 copy.13
  111.1 5.6 gather_fusion
  116.7 5.6 fusion.17
  131.5 3.7 fusion.25
  136.5 255.1 %all-reduce.7.cloned.1.call-done = (f32[512,512]{1,0:T(8,128)}, f32[2,512,32]{1,2,0:T(8,128)}) async-done(((f32[512,512]{1,0:T(8,128)}, f32[2,512,32]{1,2,0:T(8,128)}), (f32[512,512]{1,0:T(8,128)}, f32[2,512,32]{1,2,0:T(8,128)})) %all-reduce.7.cloned.1.call-update) | async-done | bytes 1179664 | tf_op jit(solution)/shard_map/psum | solution.py:171
  391.6 2.6 copy.17
  397.0 11.7 %cholesky.104 = f32[128,128]{1,0:T(8,128)S(1)} custom-call(f32[128,128]{1,0:T(8,128)S(1)} %cholesky.266), custom_call_target="Cholesky" | custom-call | tf_op jit(solution)/shard_map/jit(cholesky)/cholesky | solution.py:174
  410.1 9.8 %custom-call.33 = f32[1,128,128]{1,2,0:T(8,128)S(1)} custom-call(f32[1,128,128]{2,1,0:T(8,128)S(1)} %get-tuple-element.62), custom_call_target="InvertDiagBlocksLowerTriangular" | custom-call | tf_op jit(solution)/shard_map/jit(cholesky)/cholesky | solution.py:174
  423.1 11.9 %cholesky.217 = f32[128,128]{1,0:T(8,128)S(1)} custom-call(f32[128,128]{1,0:T(8,128)S(1)} %cholesky.270), custom_call_target="Cholesky" | custom-call | tf_op jit(solution)/shard_map/jit(cholesky)/cholesky | solution.py:174
  435.7 9.8 %custom-call.34 = f32[1,128,128]{1,2,0:T(8,128)S(1)} custom-call(f32[1,128,128]{2,1,0:T(8,128)S(1)} %get-tuple-element.59), custom_call_target="InvertDiagBlocksLowerTriangular" | custom-call | tf_op jit(solution)/shard_map/jit(cholesky)/cholesky | solution.py:174
  447.9 11.7 %cholesky.238 = f32[128,128]{1,0:T(8,128)S(1)} custom-call(f32[128,128]{1,0:T(8,128)S(1)} %cholesky.275), custom_call_target="Cholesky" | custom-call | tf_op jit(solution)/shard_map/jit(cholesky)/cholesky | solution.py:174
  460.9 9.8 %custom-call.35 = f32[1,128,128]{1,2,0:T(8,128)S(1)} custom-call(f32[1,128,128]{2,1,0:T(8,128)S(1)} %get-tuple-element.56), custom_call_target="InvertDiagBlocksLowerTriangular" | custom-call | tf_op jit(solution)/shard_map/jit(cholesky)/cholesky | solution.py:174
  472.9 12.1 %cholesky.255 = f32[128,128]{1,0:T(8,128)S(1)} custom-call(f32[128,128]{1,0:T(8,128)S(1)} %convolution_subtract_fusion.8), custom_call_target="Cholesky" | custom-call | tf_op jit(solution)/shard_map/jit(cholesky)/cholesky | solution.py:174
  491.8 11.2 %while.8 = (s32[]{:T(128)}, f32[512,512]{1,0:T(8,128)}, s32[4,2]{0,1:T(2,128)S(1)}, f32[4,128,128]{2,1,0:T(8,128)S(1)}, s32[]{:T(128)}) while((s32[]{:T(128)}, f32[512,512]{1,0:T(8,128)}, s32[4,2]{0,1:T(2,128)S(1)}, f32[4,128,128]{2,1,0:T(8,128)S(1)}, s32[]{:T(128)}) %tuple.51), condition=%wide.while_cond.1, body=%wide.while_body.1.sunk | while | flops 2 | bytes 131189 | solution.py:178
  503.0 39.3 %custom-call.39 = f32[4,128,128]{1,2,0:T(8,128)S(1)} custom-call(f32[4,128,128]{2,1,0:T(8,128)S(1)} %get-tuple-element.34), custom_call_target="InvertDiagBlocksLowerTriangular" | custom-call | tf_op jit(solution)/shard_map/triangular_solve/custom-call.8 | solution.py:178
  551.4 12.0 %all_gather.14 = f32[32,1024]{1,0:T(8,128)S(1)} all-gather(f32[32,256]{1,0:T(8,128)S(1)} %convolution_subtract_fusion.10), channel_id=1, replica_groups=mesh['blk'=32,'leaf'=4,'samp'=2] {'leaf'}, dimensions={1}, use_global_device_ids=true | all-gather | bytes 163840 | tf_op jit(solution)/shard_map/all_gather | solution.py:44
  565.6 2.8 collective-permute-done.5
  572.3 3.5 multiply_reduce_fusion.3
  577.7 27.7 %shard_map.68 = f32[136,128]{1,0:T(8,128)} custom-call(f32[136,128]{1,0:T(8,128)} %pad_maximum_fusion.3.refs_0_), custom_call_target="tpu_custom_call" | custom-call | tf_op jit(solution)/shard_map/pallas_call | solution.py:109
  618.5 15.6 %shard_map.69 = f32[8,128]{1,0:T(8,128)} custom-call(f32[8,128]{1,0:T(8,128)} %pad.13.refs_0_), custom_call_target="tpu_custom_call" | custom-call | tf_op jit(solution)/shard_map/pallas_call | solution.py:109
  634.9 12.0 %all_gather.15 = f32[32,1024]{1,0:T(8,128)S(1)} all-gather(f32[32,256]{1,0:T(8,128)S(1)} %multiply_add_fusion.1), channel_id=1, replica_groups=mesh['blk'=32,'leaf'=4,'samp'=2] {'leaf'}, dimensions={1}, use_global_device_ids=true | all-gather | bytes 163840 | tf_op jit(solution)/shard_map/all_gather | solution.py:44
  648.9 2.9 collective-permute-done.7
  651.8 3.8 collective-permute-done.6
  658.9 18.0 %shard_map.70 = f32[8,128]{1,0:T(8,128)} custom-call(f32[8,128]{1,0:T(8,128)} %pad.14.refs_0_), custom_call_target="tpu_custom_call" | custom-call | tf_op jit(solution)/shard_map/pallas_call | solution.py:109
  (138 shorter events, 82.5 us)
Async XLA Ops:
  7.2 39.0 %all-gather.2.cloned.1.call-start = ((), (), s32[]{:S(2)}) async-start(), calls=%async_computation | async-start | bytes 2621440 | tf_op jit(solution)/shard_map/all_gather | solution.py:44
  9.3 382.3 %all-reduce.7.cloned.1.call-start = ((), (), s32[]{:S(2)}) async-start(), calls=%async_computation.1 | async-start | bytes 2359296 | tf_op jit(solution)/shard_map/psum | solution.py:171
  21.9 29.0 %collective-permute-start.3 = (f32[3,1024]{1,0:T(4,128)S(1)}, f32[3,1024]{1,0:T(4,128)S(1)}, u32[]{:S(2)}, u32[]{:S(2)}) collective-permute-start(f32[3,1024]{1,0:T(4,128)S(1)} %all_gather.13), channel_id=1, source_target_pairs={{8,0},{16,8},{24,16},{32,24},{40,32},{48,40},{56,48},{64,56},{72,6... | collective-permute-start | bytes 36872 | tf_op jit(solution)/shard_map/ppermute | solution.py:22
  27.7 23.1 %collective-permute-start.2 = (f32[3,1024]{1,0:T(4,128)S(1)}, f32[3,1024]{1,0:T(4,128)S(1)}, u32[]{:S(2)}, u32[]{:S(2)}) collective-permute-start(f32[3,1024]{1,0:T(4,128)S(1)} %all_gather.13), channel_id=1, source_target_pairs={{248,0},{0,8},{8,16},{16,24},{24,32},{32,40},{40,48},{48,56},{56,6... | collective-permute-start | bytes 36872 | tf_op jit(solution)/shard_map/ppermute | solution.py:22
  46.2 48.5 %collective-permute-start.1 = (f32[512,1024]{0,1:T(8,128)}, f32[512,1024]{0,1:T(8,128)}, u32[]{:S(2)}, u32[]{:S(2)}) collective-permute-start(f32[512,1024]{0,1:T(8,128)} %all-gather.2.cloned.1.call-done), channel_id=1, source_target_pairs={{8,0},{16,8},{24,16},{32,24},{40,32},{48,40},{56,48},{64,56},{72,6... | collective-permute-start | bytes 6291464 | tf_op jit(solution)/shard_map/ppermute | solution.py:22
  49.5 49.5 %collective-permute-start = (f32[512,1024]{0,1:T(8,128)}, f32[512,1024]{0,1:T(8,128)}, u32[]{:S(2)}, u32[]{:S(2)}) collective-permute-start(f32[512,1024]{0,1:T(8,128)} %all-gather.2.cloned.1.call-done), channel_id=1, source_target_pairs={{248,0},{0,8},{8,16},{16,24},{24,32},{32,40},{40,48},{48,56},{56,6... | collective-permute-start | bytes 6291464 | tf_op jit(solution)/shard_map/ppermute | solution.py:22
  52.8 46.2 %copy-start.2 = (f32[512,1024]{0,1:T(8,128)S(1)}, f32[512,1024]{0,1:T(8,128)}, u32[]{:S(2)}) copy-start(f32[512,1024]{0,1:T(8,128)} %all-gather.2.cloned.1.call-done) | copy-start | bytes 6291460
  111.1 5.6 copy-start
  131.5 3.7 copy-start.5
  131.5 3.7 copy-start.9
  135.8 0.7 copy-start.7
  394.2 15.7 %copy-start.8 = (f32[2,512,32]{1,2,0:T(8,128)S(1)}, f32[2,512,32]{1,2,0:T(8,128)}, u32[]{:S(2)}) copy-start(f32[2,512,32]{1,2,0:T(8,128)} %get-tuple-element.48) | copy-start | bytes 393220
  396.0 1.0 copy-start.1
  551.4 17.0 %copy-start.3 = (f32[32,256]{1,0:T(8,128)}, f32[32,256]{1,0:T(8,128)S(1)}, u32[]{:S(2)}) copy-start(f32[32,256]{1,0:T(8,128)S(1)} %convolution_subtract_fusion.10) | copy-start | bytes 98308
  563.4 5.0 collective-permute-start.5
  563.7 7.2 %collective-permute-start.4 = (f32[32,1024]{1,0:T(8,128)S(1)}, f32[32,1024]{1,0:T(8,128)S(1)}, u32[]{:S(2)}, u32[]{:S(2)}) collective-permute-start(f32[32,1024]{1,0:T(8,128)S(1)} %all_gather.14), channel_id=1, source_target_pairs={{248,0},{0,8},{8,16},{16,24},{24,32},{32,40},{40,48},{48,56},{56,6... | collective-permute-start | bytes 393224 | tf_op jit(solution)/shard_map/ppermute | solution.py:22
  572.3 35.4 %copy-start.6 = (f32[32,256]{1,0:T(8,128)S(1)}, f32[32,256]{1,0:T(8,128)}, u32[]{:S(2)}) copy-start(f32[32,256]{1,0:T(8,128)} %param.15) | copy-start | bytes 98308
  607.8 27.0 %copy-start.4 = (f32[32,256]{1,0:T(8,128)S(1)}, f32[32,256]{1,0:T(8,128)}, u32[]{:S(2)}) copy-start(f32[32,256]{1,0:T(8,128)} %copy-done.3) | copy-start | bytes 98308
  646.9 5.0 collective-permute-start.7
  648.6 7.1 %collective-permute-start.6 = (f32[32,1024]{1,0:T(8,128)S(1)}, f32[32,1024]{1,0:T(8,128)S(1)}, u32[]{:S(2)}, u32[]{:S(2)}) collective-permute-start(f32[32,1024]{1,0:T(8,128)S(1)} %all_gather.15), channel_id=1, source_target_pairs={{248,0},{0,8},{8,16},{16,24},{24,32},{32,40},{40,48},{48,56},{56,6... | collective-permute-start | bytes 393224 | tf_op jit(solution)/shard_map/ppermute | solution.py:22
Sparse Core Ops, SparseCore 0:
  9.8 36.3 all-gather.1
  136.6 254.9 all-reduce.6

commit v4 on v3

--- a/solution.py
+++ b/solution.py
@@ -120,6 +120,103 @@
     )(values)
 
 
+def gram_kernel(phases, x_ref, o_ref, *scratch):
+    count = len(phases)
+    recvs = scratch[:count]
+    sums = scratch[count : 2 * count - 1]
+    full = scratch[2 * count - 1]
+    rs_send, rs_recv, ag_send, ag_recv = scratch[2 * count :]
+    barrier = pltpu.get_barrier_semaphore()
+    greeted = 0
+    for axis, n, stride in phases:
+        for k in range(1, n):
+            _, peer = group_peer(axis, n, stride, k)
+            pl.semaphore_signal(
+                barrier, 1, device_id={axis: peer}, device_id_type=pl.DeviceIdType.MESH
+            )
+            greeted += 1
+    pl.semaphore_wait(barrier, greeted)
+    source = x_ref
+    length = x_ref.shape[0]
+    offset = 0
+    for p, (axis, n, stride) in enumerate(phases):
+        own, _ = group_peer(axis, n, stride, 0)
+        part = length // n
+        recv = recvs[p]
+        recv[0] = source[pl.ds(pl.multiple_of(own * part, 8), part)]
+        copies = []
+        for k in range(1, n):
+            _, peer = group_peer(axis, n, stride, k)
+            chunk = (own + k) % n
+            copy = pltpu.make_async_remote_copy(
+                src_ref=source.at[pl.ds(pl.multiple_of(chunk * part, 8), part)],
+                dst_ref=recv.at[k],
+                send_sem=rs_send.at[p, k],
+                recv_sem=rs_recv.at[p, k],
+                device_id={axis: peer},
+                device_id_type=pl.DeviceIdType.MESH,
+            )
+            copy.start()
+            copies.append(copy)
+        for copy in copies:
+            copy.wait()
+        acc = recv[own % n]
+        for j in range(1, n):
+            acc = acc + recv[(own - j) % n]
+        offset = offset + own * part
+        length = part
+        if p < count - 1:
+            sums[p][...] = acc
+            source = sums[p]
+        else:
+            full[pl.ds(pl.multiple_of(offset, 8), part)] = acc
+    for p in reversed(range(count)):
+        axis, n, stride = phases[p]
+        own, _ = group_peer(axis, n, stride, 0)
+        here = full.at[pl.ds(pl.multiple_of(offset, 8), length)]
+        copies = []
+        for k in range(1, n):
+            _, peer = group_peer(axis, n, stride, k)
+            copy = pltpu.make_async_remote_copy(
+                src_ref=here,
+                dst_ref=here,
+                send_sem=ag_send.at[p, k],
+                recv_sem=ag_recv.at[p, k],
+                device_id={axis: peer},
+                device_id_type=pl.DeviceIdType.MESH,
+            )
+            copy.start()
+            copies.append(copy)
+        for copy in copies:
+            copy.wait()
+        offset = offset - own * length
+        length = length * n
+    o_ref[...] = full[...]
+
+
+def gram_sum(values, collective_id):
+    phases = (("samp", lax.axis_size("samp"), 1),) + reduce_phases()
+    phases = tuple(p for p in phases if p[1] > 1)
+    rows = values.shape[0]
+    widest = max(n for _, n, _ in phases)
+    recvs, sums = [], []
+    length = rows
+    for p, (_, n, _) in enumerate(phases):
+        length //= n
+        recvs.append(pltpu.VMEM((n, length, 128), jnp.float32))
+        if p < len(phases) - 1:
+            sums.append(pltpu.VMEM((length, 128), jnp.float32))
+    semaphores = [pltpu.SemaphoreType.DMA((len(phases), widest)) for _ in range(4)]
+    return pl.pallas_call(
+        lambda *refs: gram_kernel(phases, *refs),
+        out_shape=jax.ShapeDtypeStruct(values.shape, jnp.float32),
+        in_specs=[pl.BlockSpec(memory_space=pltpu.VMEM)],
+        out_specs=pl.BlockSpec(memory_space=pltpu.VMEM),
+        scratch_shapes=recvs + sums + [pltpu.VMEM((rows, 128), jnp.float32)] + semaphores,
+        compiler_params=pltpu.CompilerParams(collective_id=collective_id, has_side_effects=True),
+    )(values)
+
+
 def lower_solve(factor, values):
     return lax.linalg.triangular_solve(factor, values, left_side=True, lower=True)
 
@@ -167,9 +264,10 @@
     core_part = high_dot(omega_half, sketch_half.T)
     square_part = high_dot(sketch_half, sketch_half.T)
     joint_part = 0.5 * (core_part + core_part.T) + 0.5 * (square_part + square_part.T)
-    rhs_part = slot(high_dot(sketch, rhs.T))
-    joint_gram, rhs_proj = lax.psum((joint_part, rhs_part), ALL_AXES)
-    rhs_proj = unslot(rhs_proj)
+    rhs_proj = total_per_samp(high_dot(sketch, rhs.T))
+    gram_rows = joint_part.shape[0]
+    joint_gram = gram_sum(joint_part.reshape(gram_rows * gram_rows // 128, 128), 2)
+    joint_gram = joint_gram.reshape(gram_rows, gram_rows)
 
     joint_factor = jnp.linalg.cholesky(joint_gram)
 

time: 693 us -> 594 us (0.86)
  waiting for transfers between devices: 329 us -> 182 us
  Pallas kernels: 61.3 us -> 103 us
    psum x1, waiting for transfers between devices: 255 us -> 108 us  [total_per_samp(): return jax.tree.map(unslot, lax.psum(jax.tree.map(slot, values), ALL_AXES))]
    pallas_call x0 -> x1, Pallas kernels: none -> 43.3 us  [gram_sum(): pl.pallas_call(lambda *refs: gram_kernel(phases, *refs), out_shape=jax.Sh...]
    reshape x0 -> x3, local copies, waits for them, and re-layouts: none -> 7.25 us  [the longest x2 4.97 us: local(): joint_gram = joint_gram.reshape(gram_rows, gram_rows)]
  transfers between devices with their start and end apart: 10 -> 10, of which waited for: 8 -> 8; matrix products, arithmetic and copies ran while one was open for 1% -> 23% of each run, Pallas kernels for 0% -> 0%
where the time goes in v4:
time: 594 us; the launch traced here: 586 us
  waiting for transfers between devices  182 us (31%)
  other arithmetic  143 us (24%)
  Pallas kernels  103 us (17%)
  local copies, waits for them, and re-layouts  48.5 us (8%)
  matrix products  42.2 us (7%)
  blocking collectives  36.6 us (6%)
  between operations  17.3 us (3%)
  starting transfers between devices  13.4 us (2%)
    psum x1, waiting for transfers between devices, total_per_samp(): return jax.tree.map(unslot, lax.psum(jax.tree.map(slot, values), ALL_AXES))  108 us
    another operation x14, other arithmetic, local(): joint_factor = jnp.linalg.cholesky(joint_gram)  80.8 us
    pallas_call x3, Pallas kernels, group_sum(): pl.pallas_call(lambda *refs: sum_kernel(phases, *refs), out_shape=jax.Sha...  59.9 us
    ppermute x8, waiting for transfers between devices, shifted_2(): return lax.ppermute(block, axis, route)  55.7 us
    pallas_call x1, Pallas kernels, gram_sum(): pl.pallas_call(lambda *refs: gram_kernel(phases, *refs), out_shape=jax.Sh...  43.3 us
    another operation x4, other arithmetic, precond_from(): lax.linalg.triangular_solve(joint_factor, first_solve, left_side=True, lo...  41.7 us
    all_gather x3, blocking collectives, beside_all(): slab_values = lax.all_gather(values, 'leaf', axis=1, tiled=True)  36.6 us
    all_gather x1, waiting for transfers between devices, beside_all(): slab_values = lax.all_gather(values, 'leaf', axis=1, tiled=True)  17.8 us
  transfers between devices with their start and end apart: 10, of which 8 were waited for; matrix products, arithmetic and copies ran while one was open for 23% of the time, Pallas kernels for 0%

profile of v4, /device:TPU:4, one launch (start us, length us, event | category | flops | bytes accessed | tf_op | source)
XLA Modules:
  0.0 586.3 jit_solution(9778248755667269908)
XLA Ops:
  9.3 12.6 %all_gather.13 = f32[3,1024]{1,0:T(4,128)S(1)} all-gather(f32[3,256]{1,0:T(4,128)} %param.11), channel_id=1, replica_groups=mesh['blk'=32,'leaf'=4,'samp'=2] {'leaf'}, dimensions={1}, use_global_device_ids=true | all-gather | bytes 15360 | tf_op jit(solution)/shard_map/all_gather | solution.py:44
  21.9 5.8 collective-permute-start.3
  28.4 17.8 %all-gather.2.cloned.1.call-done = f32[512,1024]{0,1:T(8,128)} async-done(((f32[512,256]{0,1:T(8,128)}), f32[512,1024]{0,1:T(8,128)}) %all-gather.2.cloned.1.call-update) | async-done | bytes 2097168 | tf_op jit(solution)/shard_map/all_gather | solution.py:44
  46.2 3.3 collective-permute-start.1
  52.1 2.6 multiply_multiply_fusion
  54.8 39.9 %collective-permute-done.1 = f32[512,1024]{0,1:T(8,128)} collective-permute-done((f32[512,1024]{0,1:T(8,128)}, f32[512,1024]{0,1:T(8,128)}, u32[]{:S(2)}, u32[]{:S(2)}) %collective-permute-start.1) | collective-permute-done | bytes 2097184 | tf_op jit(solution)/shard_map/ppermute | solution.py:22
  94.7 4.3 collective-permute-done
  99.0 5.6 pad_maximum_fusion
  104.6 6.5 %copy.13 = f32[512,12,256]{2,0,1:T(8,128)} copy(f32[512,12,256]{0,2,1:T(8,128)} %bitcast.196) | data formatting | bytes 12582912 | tf_op jit(solution)/shard_map/reshape | solution.py:245
  111.1 5.6 gather_fusion
  116.7 5.6 fusion.17
  131.5 3.6 fusion.25
  137.4 43.3 %shard_map.68 = f32[2048,128]{1,0:T(8,128)} custom-call(f32[2048,128]{1,0:T(8,128)} %reshape.160.refs_0_), custom_call_target="tpu_custom_call" | custom-call | tf_op jit(solution)/shard_map/pallas_call | solution.py:210
  188.4 11.7 %cholesky.104 = f32[128,128]{1,0:T(8,128)S(1)} custom-call(f32[128,128]{1,0:T(8,128)S(1)} %cholesky.266), custom_call_target="Cholesky" | custom-call | tf_op jit(solution)/shard_map/jit(cholesky)/cholesky | solution.py:272
  202.7 9.8 %custom-call.33 = f32[1,128,128]{1,2,0:T(8,128)S(1)} custom-call(f32[1,128,128]{2,1,0:T(8,128)S(1)} %get-tuple-element.60), custom_call_target="InvertDiagBlocksLowerTriangular" | custom-call | tf_op jit(solution)/shard_map/jit(cholesky)/cholesky | solution.py:272
  215.7 11.9 %cholesky.217 = f32[128,128]{1,0:T(8,128)S(1)} custom-call(f32[128,128]{1,0:T(8,128)S(1)} %cholesky.270), custom_call_target="Cholesky" | custom-call | tf_op jit(solution)/shard_map/jit(cholesky)/cholesky | solution.py:272
  228.3 9.8 %custom-call.34 = f32[1,128,128]{1,2,0:T(8,128)S(1)} custom-call(f32[1,128,128]{2,1,0:T(8,128)S(1)} %get-tuple-element.57), custom_call_target="InvertDiagBlocksLowerTriangular" | custom-call | tf_op jit(solution)/shard_map/jit(cholesky)/cholesky | solution.py:272
  240.5 11.7 %cholesky.238 = f32[128,128]{1,0:T(8,128)S(1)} custom-call(f32[128,128]{1,0:T(8,128)S(1)} %cholesky.275), custom_call_target="Cholesky" | custom-call | tf_op jit(solution)/shard_map/jit(cholesky)/cholesky | solution.py:272
  253.4 10.2 %custom-call.35 = f32[1,128,128]{1,2,0:T(8,128)S(1)} custom-call(f32[1,128,128]{2,1,0:T(8,128)S(1)} %get-tuple-element.54), custom_call_target="InvertDiagBlocksLowerTriangular" | custom-call | tf_op jit(solution)/shard_map/jit(cholesky)/cholesky | solution.py:272
  265.9 11.7 %cholesky.255 = f32[128,128]{1,0:T(8,128)S(1)} custom-call(f32[128,128]{1,0:T(8,128)S(1)} %convolution_subtract_fusion.8), custom_call_target="Cholesky" | custom-call | tf_op jit(solution)/shard_map/jit(cholesky)/cholesky | solution.py:272
  284.4 12.0 %while.8 = (s32[]{:T(128)}, f32[512,512]{1,0:T(8,128)}, s32[4,2]{0,1:T(2,128)S(1)}, f32[4,128,128]{2,1,0:T(8,128)S(1)}, s32[]{:T(128)}) while((s32[]{:T(128)}, f32[512,512]{1,0:T(8,128)}, s32[4,2]{0,1:T(2,128)S(1)}, f32[4,128,128]{2,1,0:T(8,128)S(1)}, s32[]{:T(128)}) %tuple.51), condition=%wide.while_cond.1, body=%wide.while_body.1.sunk | while | flops 2 | bytes 131189 | solution.py:276
  296.5 39.3 %custom-call.39 = f32[4,128,128]{1,2,0:T(8,128)S(1)} custom-call(f32[4,128,128]{2,1,0:T(8,128)S(1)} %get-tuple-element.34), custom_call_target="InvertDiagBlocksLowerTriangular" | custom-call | tf_op jit(solution)/shard_map/triangular_solve/custom-call.8 | solution.py:276
  335.8 108.5 %all-reduce.6.cloned.1.call-done = f32[2,512,32]{1,2,0:T(8,128)} async-done(((f32[2,512,32]{1,2,0:T(8,128)}), f32[2,512,32]{1,2,0:T(8,128)}) %all-reduce.6.cloned.1.call-update) | async-done | bytes 131088 | tf_op jit(solution)/shard_map/psum | solution.py:257
  454.3 12.0 %all_gather.14 = f32[32,1024]{1,0:T(8,128)S(1)} all-gather(f32[32,256]{1,0:T(8,128)S(1)} %convolution_subtract_fusion.10), channel_id=1, replica_groups=mesh['blk'=32,'leaf'=4,'samp'=2] {'leaf'}, dimensions={1}, use_global_device_ids=true | all-gather | bytes 163840 | tf_op jit(solution)/shard_map/all_gather | solution.py:44
  468.5 2.8 collective-permute-done.5
  474.9 3.5 multiply_reduce_fusion.3
  480.4 27.3 %shard_map.69 = f32[136,128]{1,0:T(8,128)} custom-call(f32[136,128]{1,0:T(8,128)} %pad_maximum_fusion.3.refs_0_), custom_call_target="tpu_custom_call" | custom-call | tf_op jit(solution)/shard_map/pallas_call | solution.py:109
  520.8 15.0 %shard_map.70 = f32[8,128]{1,0:T(8,128)} custom-call(f32[8,128]{1,0:T(8,128)} %pad.13.refs_0_), custom_call_target="tpu_custom_call" | custom-call | tf_op jit(solution)/shard_map/pallas_call | solution.py:109
  536.6 12.0 %all_gather.15 = f32[32,1024]{1,0:T(8,128)S(1)} all-gather(f32[32,256]{1,0:T(8,128)S(1)} %multiply_add_fusion.1), channel_id=1, replica_groups=mesh['blk'=32,'leaf'=4,'samp'=2] {'leaf'}, dimensions={1}, use_global_device_ids=true | all-gather | bytes 163840 | tf_op jit(solution)/shard_map/all_gather | solution.py:44
  550.6 2.9 collective-permute-done.7
  553.5 3.5 collective-permute-done.6
  560.3 17.6 %shard_map.71 = f32[8,128]{1,0:T(8,128)} custom-call(f32[8,128]{1,0:T(8,128)} %pad.14.refs_0_), custom_call_target="tpu_custom_call" | custom-call | tf_op jit(solution)/shard_map/pallas_call | solution.py:109
  (139 shorter events, 91.1 us)
Async XLA Ops:
  7.2 39.0 %all-gather.2.cloned.1.call-start = ((), (), s32[]{:S(2)}) async-start(), calls=%async_computation | async-start | bytes 2621440 | tf_op jit(solution)/shard_map/all_gather | solution.py:44
  9.3 435.0 %all-reduce.6.cloned.1.call-start = ((), (), s32[]{:S(2)}) async-start(), calls=%async_computation.1 | async-start | bytes 262144 | tf_op jit(solution)/shard_map/psum | solution.py:257
  21.9 28.3 %collective-permute-start.3 = (f32[3,1024]{1,0:T(4,128)S(1)}, f32[3,1024]{1,0:T(4,128)S(1)}, u32[]{:S(2)}, u32[]{:S(2)}) collective-permute-start(f32[3,1024]{1,0:T(4,128)S(1)} %all_gather.13), channel_id=1, source_target_pairs={{8,0},{16,8},{24,16},{32,24},{40,32},{48,40},{56,48},{64,56},{72,6... | collective-permute-start | bytes 36872 | tf_op jit(solution)/shard_map/ppermute | solution.py:22
  27.7 22.5 %collective-permute-start.2 = (f32[3,1024]{1,0:T(4,128)S(1)}, f32[3,1024]{1,0:T(4,128)S(1)}, u32[]{:S(2)}, u32[]{:S(2)}) collective-permute-start(f32[3,1024]{1,0:T(4,128)S(1)} %all_gather.13), channel_id=1, source_target_pairs={{248,0},{0,8},{8,16},{16,24},{24,32},{32,40},{40,48},{48,56},{56,6... | collective-permute-start | bytes 36872 | tf_op jit(solution)/shard_map/ppermute | solution.py:22
  46.2 48.5 %collective-permute-start.1 = (f32[512,1024]{0,1:T(8,128)}, f32[512,1024]{0,1:T(8,128)}, u32[]{:S(2)}, u32[]{:S(2)}) collective-permute-start(f32[512,1024]{0,1:T(8,128)} %all-gather.2.cloned.1.call-done), channel_id=1, source_target_pairs={{8,0},{16,8},{24,16},{32,24},{40,32},{48,40},{56,48},{64,56},{72,6... | collective-permute-start | bytes 6291464 | tf_op jit(solution)/shard_map/ppermute | solution.py:22
  49.5 49.5 %collective-permute-start = (f32[512,1024]{0,1:T(8,128)}, f32[512,1024]{0,1:T(8,128)}, u32[]{:S(2)}, u32[]{:S(2)}) collective-permute-start(f32[512,1024]{0,1:T(8,128)} %all-gather.2.cloned.1.call-done), channel_id=1, source_target_pairs={{248,0},{0,8},{8,16},{16,24},{24,32},{32,40},{40,48},{48,56},{56,6... | collective-permute-start | bytes 6291464 | tf_op jit(solution)/shard_map/ppermute | solution.py:22
  52.1 46.9 %copy-start.2 = (f32[512,1024]{0,1:T(8,128)S(1)}, f32[512,1024]{0,1:T(8,128)}, u32[]{:S(2)}) copy-start(f32[512,1024]{0,1:T(8,128)} %all-gather.2.cloned.1.call-done) | copy-start | bytes 6291460
  111.1 5.6 copy-start
  185.7 15.7 %copy-start.5 = (f32[32,256]{1,0:T(8,128)S(1)}, f32[32,256]{1,0:T(8,128)}, u32[]{:S(2)}) copy-start(f32[32,256]{1,0:T(8,128)} %param.15) | copy-start | bytes 98308
  185.7 15.7 %copy-start.8 = (f32[256]{0:T(256)S(1)}, f32[256]{0:T(256)}, u32[]{:S(2)}) copy-start(f32[256]{0:T(256)} %param.14) | copy-start | bytes 3076
  187.4 1.0 copy-start.1
  202.0 0.6 copy-start.7
  454.3 17.0 %copy-start.3 = (f32[32,256]{1,0:T(8,128)}, f32[32,256]{1,0:T(8,128)S(1)}, u32[]{:S(2)}) copy-start(f32[32,256]{1,0:T(8,128)S(1)} %convolution_subtract_fusion.10) | copy-start | bytes 98308
  466.3 5.0 collective-permute-start.5
  466.3 7.3 %collective-permute-start.4 = (f32[32,1024]{1,0:T(8,128)S(1)}, f32[32,1024]{1,0:T(8,128)S(1)}, u32[]{:S(2)}, u32[]{:S(2)}) collective-permute-start(f32[32,1024]{1,0:T(8,128)S(1)} %all_gather.14), channel_id=1, source_target_pairs={{248,0},{0,8},{8,16},{16,24},{24,32},{32,40},{40,48},{48,56},{56,6... | collective-permute-start | bytes 393224 | tf_op jit(solution)/shard_map/ppermute | solution.py:22
  474.9 35.0 %copy-start.6 = (f32[32,256]{1,0:T(8,128)S(1)}, f32[32,256]{1,0:T(8,128)}, u32[]{:S(2)}) copy-start(f32[32,256]{1,0:T(8,128)} %param.15) | copy-start | bytes 98308
  510.0 26.5 %copy-start.4 = (f32[32,256]{1,0:T(8,128)S(1)}, f32[32,256]{1,0:T(8,128)}, u32[]{:S(2)}) copy-start(f32[32,256]{1,0:T(8,128)} %copy-done.3) | copy-start | bytes 98308
  548.6 5.0 collective-permute-start.7
  549.9 7.1 %collective-permute-start.6 = (f32[32,1024]{1,0:T(8,128)S(1)}, f32[32,1024]{1,0:T(8,128)S(1)}, u32[]{:S(2)}, u32[]{:S(2)}) collective-permute-start(f32[32,1024]{1,0:T(8,128)S(1)} %all_gather.15), channel_id=1, source_target_pairs={{248,0},{0,8},{8,16},{16,24},{24,32},{32,40},{40,48},{48,56},{56,6... | collective-permute-start | bytes 393224 | tf_op jit(solution)/shard_map/ppermute | solution.py:22
Sparse Core Ops, SparseCore 0:
  9.8 36.3 all-gather.1
  202.8 241.4 all-reduce.5

commit v5 on v4

--- a/solution.py
+++ b/solution.py
@@ -264,10 +264,12 @@
     core_part = high_dot(omega_half, sketch_half.T)
     square_part = high_dot(sketch_half, sketch_half.T)
     joint_part = 0.5 * (core_part + core_part.T) + 0.5 * (square_part + square_part.T)
-    rhs_proj = total_per_samp(high_dot(sketch, rhs.T))
     gram_rows = joint_part.shape[0]
     joint_gram = gram_sum(joint_part.reshape(gram_rows * gram_rows // 128, 128), 2)
     joint_gram = joint_gram.reshape(gram_rows, gram_rows)
+    width = rhs.shape[0]
+    rhs_proj = high_dot(sketch, rhs.T).reshape(gram_rows * width // 128, 128)
+    rhs_proj = group_sum(rhs_proj, 3).reshape(gram_rows, width)
 
     joint_factor = jnp.linalg.cholesky(joint_gram)
 
@@ -284,7 +286,6 @@
     direction = precond
     weights = jnp.zeros_like(rhs)
 
-    width = rhs.shape[0]
     sketch_rows = sketch.shape[0]
 
     def pack_scalars(*vectors):

time: 594 us -> 515 us (0.87)
  waiting for transfers between devices: 182 us -> 75.7 us
  Pallas kernels: 103 us -> 129 us
    psum x1 -> x0, waiting for transfers between devices: 108 us -> none  [total_per_samp(): return jax.tree.map(unslot, lax.psum(jax.tree.map(slot, values), ALL_AXES))]
    pallas_call x3 -> x4, Pallas kernels: 59.9 us -> 88.5 us  [group_sum(): pl.pallas_call(lambda *refs: sum_kernel(phases, *refs), out_shape=jax.Sha...]
  transfers between devices with their start and end apart: 10 -> 9, of which waited for: 8 -> 7; matrix products, arithmetic and copies ran while one was open for 23% -> 1% of each run, Pallas kernels for 0% -> 0%
where the time goes in v5:
time: 515 us; the launch traced here: 507 us
  other arithmetic  143 us (28%)
  Pallas kernels  129 us (25%)
  waiting for transfers between devices  75.7 us (15%)
  local copies, waits for them, and re-layouts  48.8 us (9%)
  matrix products  42.1 us (8%)
  blocking collectives  36.7 us (7%)
  between operations  17.3 us (3%)
  starting transfers between devices  13.6 us (3%)
    pallas_call x4, Pallas kernels, group_sum(): pl.pallas_call(lambda *refs: sum_kernel(phases, *refs), out_shape=jax.Sha...  88.5 us
    another operation x14, other arithmetic, local(): joint_factor = jnp.linalg.cholesky(joint_gram)  80.6 us
    ppermute x8, waiting for transfers between devices, shifted_2(): return lax.ppermute(block, axis, route)  57.9 us
    another operation x4, other arithmetic, precond_from(): lax.linalg.triangular_solve(joint_factor, first_solve, left_side=True, lo...  41.7 us
    pallas_call x1, Pallas kernels, gram_sum(): pl.pallas_call(lambda *refs: gram_kernel(phases, *refs), out_shape=jax.Sh...  41 us
    all_gather x3, blocking collectives, beside_all(): slab_values = lax.all_gather(values, 'leaf', axis=1, tiled=True)  36.7 us
    all_gather x1, waiting for transfers between devices, beside_all(): slab_values = lax.all_gather(values, 'leaf', axis=1, tiled=True)  17.8 us
    ppermute x8, starting transfers between devices, shifted_2(): return lax.ppermute(block, axis, route)  13.5 us
  transfers between devices with their start and end apart: 9, of which 7 were waited for; matrix products, arithmetic and copies ran while one was open for 1% of the time, Pallas kernels for 0%

profile of v5, /device:TPU:4, one launch (start us, length us, event | category | flops | bytes accessed | tf_op | source)
XLA Modules:
  0.0 506.7 jit_solution(14429996496856403547)
XLA Ops:
  9.3 12.6 %all_gather.13 = f32[3,1024]{1,0:T(4,128)S(1)} all-gather(f32[3,256]{1,0:T(4,128)} %param.11), channel_id=1, replica_groups=mesh['blk'=32,'leaf'=4,'samp'=2] {'leaf'}, dimensions={1}, use_global_device_ids=true | all-gather | bytes 15360 | tf_op jit(solution)/shard_map/all_gather | solution.py:44
  21.9 5.8 %collective-permute-start.3 = (f32[3,1024]{1,0:T(4,128)S(1)}, f32[3,1024]{1,0:T(4,128)S(1)}, u32[]{:S(2)}, u32[]{:S(2)}) collective-permute-start(f32[3,1024]{1,0:T(4,128)S(1)} %all_gather.13), channel_id=1, source_target_pairs={{8,0},{16,8},{24,16},{32,24},{40,32},{48,40},{56,48},{64,56},{72,6... | collective-permute-start | bytes 36872 | tf_op jit(solution)/shard_map/ppermute | solution.py:22
  28.4 17.8 %all-gather.2.cloned.1.call-done = f32[512,1024]{0,1:T(8,128)} async-done(((f32[512,256]{0,1:T(8,128)}), f32[512,1024]{0,1:T(8,128)}) %all-gather.2.cloned.1.call-update) | async-done | bytes 2097168 | tf_op jit(solution)/shard_map/all_gather | solution.py:44
  46.2 3.3 collective-permute-start.1
  52.1 2.6 multiply_multiply_fusion
  54.8 39.9 %collective-permute-done.1 = f32[512,1024]{0,1:T(8,128)} collective-permute-done((f32[512,1024]{0,1:T(8,128)}, f32[512,1024]{0,1:T(8,128)}, u32[]{:S(2)}, u32[]{:S(2)}) %collective-permute-start.1) | collective-permute-done | bytes 2097184 | tf_op jit(solution)/shard_map/ppermute | solution.py:22
  94.7 4.3 collective-permute-done
  99.0 5.6 %pad_maximum_fusion = f32[512,3072]{0,1:T(8,128)} fusion(f32[512,1024]{0,1:T(8,128)} %collective-permute-done.1, f32[512,1024]{0,1:T(8,128)S(1)} %copy-done.2, f32[512,1024]{0,1:T(8,128)} %collective-permute-done), kind=kLoop, calls=%fused_computation.6 | loop fusion | flops 3145728 | bytes 12582912 | tf_op jit(solution)/shard_map/concatenate | solution.py:45
  104.6 6.5 %copy.13 = f32[512,12,256]{2,0,1:T(8,128)} copy(f32[512,12,256]{0,2,1:T(8,128)} %bitcast.190) | data formatting | bytes 12582912 | tf_op jit(solution)/shard_map/reshape | solution.py:245
  111.1 5.6 %gather_fusion = f32[8,512,256]{2,1,0:T(8,128)} fusion(f32[512,12,256]{2,0,1:T(8,128)} %copy.13, s32[1024]{0:T(1024)S(1)} %pad_clamp_fusion.1), kind=kCustom, calls=%fused_computation.2 | custom fusion | bytes 8388640 | tf_op jit(solution)/shard_map/jit(_take)/gather | solution.py:246
  116.7 5.6 %fusion.17 = f32[512,256]{1,0:T(8,128)S(1)} fusion(f32[512,256]{1,0:T(8,128)S(1)} %copy-done, f32[8,256,256]{2,1,0:T(8,128)S(1)} %multiply_multiply_fusion, f32[8,512,256]{2,1,0:T(8,128)} %gather_fusion, pred[8]{0:T(512)(128)(4,1)S(1)} %compare_and_fusion), kind=kOutput, calls=%fused_computation.28 | convolution fusion | flops 3222405120 | bytes 7340040 | tf_op jit(solution)/shard_map/cnj,nij->ci/dot_general | solution.py:247
  127.7 28.8 %shard_map.69 = f32[128,128]{1,0:T(8,128)} custom-call(f32[128,128]{1,0:T(8,128)} %reshape.168.refs_0_), custom_call_target="tpu_custom_call" | custom-call | tf_op jit(solution)/shard_map/pallas_call | solution.py:109
  162.6 3.7 fusion.24
  168.5 41.0 %shard_map.68 = f32[2048,128]{1,0:T(8,128)} custom-call(f32[2048,128]{1,0:T(8,128)} %reshape.166.refs_0_), custom_call_target="tpu_custom_call" | custom-call | tf_op jit(solution)/shard_map/pallas_call | solution.py:210
  217.2 11.7 %cholesky.104 = f32[128,128]{1,0:T(8,128)S(1)} custom-call(f32[128,128]{1,0:T(8,128)S(1)} %cholesky.266), custom_call_target="Cholesky" | custom-call | tf_op jit(solution)/shard_map/jit(cholesky)/cholesky | solution.py:274
  229.0 9.8 %custom-call.33 = f32[1,128,128]{1,2,0:T(8,128)S(1)} custom-call(f32[1,128,128]{2,1,0:T(8,128)S(1)} %get-tuple-element.60), custom_call_target="InvertDiagBlocksLowerTriangular" | custom-call | tf_op jit(solution)/shard_map/jit(cholesky)/cholesky | solution.py:274
  243.4 11.7 %cholesky.217 = f32[128,128]{1,0:T(8,128)S(1)} custom-call(f32[128,128]{1,0:T(8,128)S(1)} %cholesky.270), custom_call_target="Cholesky" | custom-call | tf_op jit(solution)/shard_map/jit(cholesky)/cholesky | solution.py:274
  255.8 9.8 %custom-call.34 = f32[1,128,128]{1,2,0:T(8,128)S(1)} custom-call(f32[1,128,128]{2,1,0:T(8,128)S(1)} %get-tuple-element.57), custom_call_target="InvertDiagBlocksLowerTriangular" | custom-call | tf_op jit(solution)/shard_map/jit(cholesky)/cholesky | solution.py:274
  268.0 11.7 %cholesky.238 = f32[128,128]{1,0:T(8,128)S(1)} custom-call(f32[128,128]{1,0:T(8,128)S(1)} %cholesky.275), custom_call_target="Cholesky" | custom-call | tf_op jit(solution)/shard_map/jit(cholesky)/cholesky | solution.py:274
  281.0 10.2 %custom-call.35 = f32[1,128,128]{1,2,0:T(8,128)S(1)} custom-call(f32[1,128,128]{2,1,0:T(8,128)S(1)} %get-tuple-element.54), custom_call_target="InvertDiagBlocksLowerTriangular" | custom-call | tf_op jit(solution)/shard_map/jit(cholesky)/cholesky | solution.py:274
  293.4 11.7 %cholesky.255 = f32[128,128]{1,0:T(8,128)S(1)} custom-call(f32[128,128]{1,0:T(8,128)S(1)} %convolution_subtract_fusion.8), custom_call_target="Cholesky" | custom-call | tf_op jit(solution)/shard_map/jit(cholesky)/cholesky | solution.py:274
  312.0 12.0 %while.8 = (s32[]{:T(128)}, f32[512,512]{1,0:T(8,128)}, s32[4,2]{0,1:T(2,128)S(1)}, f32[4,128,128]{2,1,0:T(8,128)S(1)}, s32[]{:T(128)}) while((s32[]{:T(128)}, f32[512,512]{1,0:T(8,128)}, s32[4,2]{0,1:T(2,128)S(1)}, f32[4,128,128]{2,1,0:T(8,128)S(1)}, s32[]{:T(128)}) %tuple.51), condition=%wide.while_cond.1, body=%wide.while_body.1.sunk | while | flops 2 | bytes 131189 | solution.py:278
  324.0 39.3 %custom-call.39 = f32[4,128,128]{1,2,0:T(8,128)S(1)} custom-call(f32[4,128,128]{2,1,0:T(8,128)S(1)} %get-tuple-element.34), custom_call_target="InvertDiagBlocksLowerTriangular" | custom-call | tf_op jit(solution)/shard_map/triangular_solve/custom-call.8 | solution.py:278
  372.4 12.1 %all_gather.14 = f32[32,1024]{1,0:T(8,128)S(1)} all-gather(f32[32,256]{1,0:T(8,128)S(1)} %convolution_subtract_fusion.10), channel_id=1, replica_groups=mesh['blk'=32,'leaf'=4,'samp'=2] {'leaf'}, dimensions={1}, use_global_device_ids=true | all-gather | bytes 163840 | tf_op jit(solution)/shard_map/all_gather | solution.py:44
  389.5 4.5 collective-permute-done.4
  395.3 3.5 multiply_reduce_fusion.3
  400.8 26.3 %shard_map.70 = f32[136,128]{1,0:T(8,128)} custom-call(f32[136,128]{1,0:T(8,128)} %pad_maximum_fusion.3.refs_0_), custom_call_target="tpu_custom_call" | custom-call | tf_op jit(solution)/shard_map/pallas_call | solution.py:109
  440.2 16.0 %shard_map.71 = f32[8,128]{1,0:T(8,128)} custom-call(f32[8,128]{1,0:T(8,128)} %pad.13.refs_0_), custom_call_target="tpu_custom_call" | custom-call | tf_op jit(solution)/shard_map/pallas_call | solution.py:109
  456.9 12.0 %all_gather.15 = f32[32,1024]{1,0:T(8,128)S(1)} all-gather(f32[32,256]{1,0:T(8,128)S(1)} %multiply_add_fusion.1), channel_id=1, replica_groups=mesh['blk'=32,'leaf'=4,'samp'=2] {'leaf'}, dimensions={1}, use_global_device_ids=true | all-gather | bytes 163840 | tf_op jit(solution)/shard_map/all_gather | solution.py:44
  471.0 3.2 collective-permute-done.7
  474.2 3.4 collective-permute-done.6
  480.8 17.4 %shard_map.72 = f32[8,128]{1,0:T(8,128)} custom-call(f32[8,128]{1,0:T(8,128)} %pad.14.refs_0_), custom_call_target="tpu_custom_call" | custom-call | tf_op jit(solution)/shard_map/pallas_call | solution.py:109
  (134 shorter events, 91.8 us)
Async XLA Ops:
  7.2 39.0 %all-gather.2.cloned.1.call-start = ((), (), s32[]{:S(2)}) async-start(), calls=%async_computation | async-start | bytes 2621440 | tf_op jit(solution)/shard_map/all_gather | solution.py:44
  21.9 28.3 %collective-permute-start.3 = (f32[3,1024]{1,0:T(4,128)S(1)}, f32[3,1024]{1,0:T(4,128)S(1)}, u32[]{:S(2)}, u32[]{:S(2)}) collective-permute-start(f32[3,1024]{1,0:T(4,128)S(1)} %all_gather.13), channel_id=1, source_target_pairs={{8,0},{16,8},{24,16},{32,24},{40,32},{48,40},{56,48},{64,56},{72,6... | collective-permute-start | bytes 36872 | tf_op jit(solution)/shard_map/ppermute | solution.py:22
  27.7 22.5 %collective-permute-start.2 = (f32[3,1024]{1,0:T(4,128)S(1)}, f32[3,1024]{1,0:T(4,128)S(1)}, u32[]{:S(2)}, u32[]{:S(2)}) collective-permute-start(f32[3,1024]{1,0:T(4,128)S(1)} %all_gather.13), channel_id=1, source_target_pairs={{248,0},{0,8},{8,16},{16,24},{24,32},{32,40},{40,48},{48,56},{56,6... | collective-permute-start | bytes 36872 | tf_op jit(solution)/shard_map/ppermute | solution.py:22
  46.2 48.5 %collective-permute-start.1 = (f32[512,1024]{0,1:T(8,128)}, f32[512,1024]{0,1:T(8,128)}, u32[]{:S(2)}, u32[]{:S(2)}) collective-permute-start(f32[512,1024]{0,1:T(8,128)} %all-gather.2.cloned.1.call-done), channel_id=1, source_target_pairs={{8,0},{16,8},{24,16},{32,24},{40,32},{48,40},{56,48},{64,56},{72,6... | collective-permute-start | bytes 6291464 | tf_op jit(solution)/shard_map/ppermute | solution.py:22
  49.5 49.5 %collective-permute-start = (f32[512,1024]{0,1:T(8,128)}, f32[512,1024]{0,1:T(8,128)}, u32[]{:S(2)}, u32[]{:S(2)}) collective-permute-start(f32[512,1024]{0,1:T(8,128)} %all-gather.2.cloned.1.call-done), channel_id=1, source_target_pairs={{248,0},{0,8},{8,16},{16,24},{24,32},{32,40},{40,48},{48,56},{56,6... | collective-permute-start | bytes 6291464 | tf_op jit(solution)/shard_map/ppermute | solution.py:22
  52.1 46.9 %copy-start.2 = (f32[512,1024]{0,1:T(8,128)S(1)}, f32[512,1024]{0,1:T(8,128)}, u32[]{:S(2)}) copy-start(f32[512,1024]{0,1:T(8,128)} %all-gather.2.cloned.1.call-done) | copy-start | bytes 6291460
  111.1 5.6 %copy-start = (f32[512,256]{1,0:T(8,128)S(1)}, f32[512,256]{1,0:T(8,128)}, u32[]{:S(2)}) copy-start(f32[512,256]{1,0:T(8,128)} %param.13) | copy-start | bytes 1572868
  122.4 4.1 copy-start.5
  122.4 4.0 copy-start.7
  216.2 1.0 copy-start.1
  372.4 17.1 %copy-start.3 = (f32[32,256]{1,0:T(8,128)}, f32[32,256]{1,0:T(8,128)S(1)}, u32[]{:S(2)}) copy-start(f32[32,256]{1,0:T(8,128)S(1)} %convolution_subtract_fusion.10) | copy-start | bytes 98308
  384.5 5.0 collective-permute-start.5
  386.7 7.2 %collective-permute-start.4 = (f32[32,1024]{1,0:T(8,128)S(1)}, f32[32,1024]{1,0:T(8,128)S(1)}, u32[]{:S(2)}, u32[]{:S(2)}) collective-permute-start(f32[32,1024]{1,0:T(8,128)S(1)} %all_gather.14), channel_id=1, source_target_pairs={{248,0},{0,8},{8,16},{16,24},{24,32},{32,40},{40,48},{48,56},{56,6... | collective-permute-start | bytes 393224 | tf_op jit(solution)/shard_map/ppermute | solution.py:22
  395.3 34.0 %copy-start.6 = (f32[32,256]{1,0:T(8,128)S(1)}, f32[32,256]{1,0:T(8,128)}, u32[]{:S(2)}) copy-start(f32[32,256]{1,0:T(8,128)} %param.15) | copy-start | bytes 98308
  429.4 27.5 %copy-start.4 = (f32[32,256]{1,0:T(8,128)S(1)}, f32[32,256]{1,0:T(8,128)}, u32[]{:S(2)}) copy-start(f32[32,256]{1,0:T(8,128)} %copy-done.3) | copy-start | bytes 98308
  468.9 5.2 %collective-permute-start.7 = (f32[32,1024]{1,0:T(8,128)S(1)}, f32[32,1024]{1,0:T(8,128)S(1)}, u32[]{:S(2)}, u32[]{:S(2)}) collective-permute-start(f32[32,1024]{1,0:T(8,128)S(1)} %all_gather.15), channel_id=1, source_target_pairs={{8,0},{16,8},{24,16},{32,24},{40,32},{48,40},{56,48},{64,56},{72,6... | collective-permute-start | bytes 393224 | tf_op jit(solution)/shard_map/ppermute | solution.py:22
  470.3 7.3 %collective-permute-start.6 = (f32[32,1024]{1,0:T(8,128)S(1)}, f32[32,1024]{1,0:T(8,128)S(1)}, u32[]{:S(2)}, u32[]{:S(2)}) collective-permute-start(f32[32,1024]{1,0:T(8,128)S(1)} %all_gather.15), channel_id=1, source_target_pairs={{248,0},{0,8},{8,16},{16,24},{24,32},{32,40},{40,48},{48,56},{56,6... | collective-permute-start | bytes 393224 | tf_op jit(solution)/shard_map/ppermute | solution.py:22
Sparse Core Ops, SparseCore 0:
  9.8 36.3 all-gather.1

commit v6 on v5

--- a/solution.py
+++ b/solution.py
@@ -217,6 +217,74 @@
     )(values)
 
 
+def halo_kernel(n_blk, n_leaf, x_ref, o_ref, land, send_sem, recv_sem):
+    own_blk = lax.axis_index("blk")
+    own_leaf = lax.axis_index("leaf")
+    targets = []
+    for d in (-1, 1):
+        for leaf in range(n_leaf):
+            targets.append(((own_blk + d + n_blk) % n_blk, leaf, (1 - d) * n_leaf + own_leaf))
+    for k in range(1, n_leaf):
+        targets.append((own_blk, (own_leaf + k) % n_leaf, n_leaf + own_leaf))
+    barrier = pltpu.get_barrier_semaphore()
+    for blk, leaf, _ in targets:
+        pl.semaphore_signal(
+            barrier,
+            1,
+            device_id={"blk": blk, "leaf": leaf},
+            device_id_type=pl.DeviceIdType.MESH,
+        )
+    pl.semaphore_wait(barrier, len(targets))
+    copies = []
+    for i, (blk, leaf, segment) in enumerate(targets):
+        copy = pltpu.make_async_remote_copy(
+            src_ref=x_ref,
+            dst_ref=land.at[segment],
+            send_sem=send_sem.at[i],
+            recv_sem=recv_sem.at[segment],
+            device_id={"blk": blk, "leaf": leaf},
+            device_id_type=pl.DeviceIdType.MESH,
+        )
+        copy.start()
+        copies.append(copy)
+    land[n_leaf + own_leaf] = x_ref[...]
+    incoming = [((own_blk - 1 + n_blk) % n_blk, s, s) for s in range(n_leaf)]
+    incoming += [((own_blk + 1) % n_blk, s, 2 * n_leaf + s) for s in range(n_leaf)]
+    for k in range(1, n_leaf):
+        leaf = (own_leaf + k) % n_leaf
+        incoming.append((own_blk, leaf, n_leaf + leaf))
+    for copy in copies:
+        copy.wait_send()
+    for blk, leaf, segment in incoming:
+        pltpu.make_async_remote_copy(
+            src_ref=x_ref,
+            dst_ref=land.at[segment],
+            send_sem=send_sem.at[0],
+            recv_sem=recv_sem.at[segment],
+            device_id={"blk": blk, "leaf": leaf},
+            device_id_type=pl.DeviceIdType.MESH,
+        ).wait_recv()
+    o_ref[...] = land[...]
+
+
+def halo_gather(values, collective_id):
+    n_blk = lax.axis_size("blk")
+    n_leaf = lax.axis_size("leaf")
+    segments = 3 * n_leaf
+    return pl.pallas_call(
+        lambda *refs: halo_kernel(n_blk, n_leaf, *refs),
+        out_shape=jax.ShapeDtypeStruct((segments,) + values.shape, jnp.float32),
+        in_specs=[pl.BlockSpec(memory_space=pltpu.VMEM)],
+        out_specs=pl.BlockSpec(memory_space=pltpu.VMEM),
+        scratch_shapes=[
+            pltpu.VMEM((segments,) + values.shape, jnp.float32),
+            pltpu.SemaphoreType.DMA((segments,)),
+            pltpu.SemaphoreType.DMA((segments,)),
+        ],
+        compiler_params=pltpu.CompilerParams(collective_id=collective_id, has_side_effects=True),
+    )(values)
+
+
 def lower_solve(factor, values):
     return lax.linalg.triangular_solve(factor, values, left_side=True, lower=True)
 
@@ -233,8 +301,7 @@
     relative = jnp.mod(neighbors // slab_blocks - own_slab + 1, cycle_count)
     chosen = jnp.where(usable, relative * slab_blocks + jnp.mod(neighbors, slab_blocks), 0)
     usable_weight = usable.astype(jnp.float32)
-    reach_points = beside_all(points)
-    reach_blocks = reach_points.reshape(3, 3 * slab_blocks, PB).transpose(1, 0, 2)
+    reach_blocks = halo_gather(points, 4)
     row_blocks = points.reshape(3, blk_dev, PB).transpose(1, 0, 2)
 
     kernel_tile = wendland(row_blocks[0], reach_blocks[chosen[0]], period)
@@ -242,9 +309,9 @@
 
     def apply_kernel(values):
         width = values.shape[0]
-        reach = beside_all(values).reshape(width, 3 * slab_blocks, PB)
-        picked = jnp.take(reach, chosen[0], axis=1)
-        return jnp.einsum("cnj,nij->ci", picked, kernel_tile, precision=lax.Precision.HIGHEST)
+        reach = halo_gather(values, 5 if width == omega.shape[0] else 6)
+        picked = jnp.take(reach, chosen[0], axis=0)
+        return jnp.einsum("ncj,nij->ci", picked, kernel_tile, precision=lax.Precision.HIGHEST)
 
     def slot(x):
         zeros = jnp.zeros((n_samp,) + x.shape, x.dtype)

time: 515 us -> 532 us (1.033)
  Pallas kernels: 129 us -> 285 us
  waiting for transfers between devices: 75.7 us -> 0 us
  blocking collectives: 36.7 us -> 0 us
  starting transfers between devices: 13.6 us -> 0 us
  between operations: 17.3 us -> 4.18 us
  other arithmetic: 143 us -> 150 us
  local copies, waits for them, and re-layouts: 48.8 us -> 42.8 us
    pallas_call x0 -> x4, Pallas kernels: none -> 143 us  [halo_gather(): pl.pallas_call(lambda *refs: halo_kernel(n_blk, n_leaf, *refs), out_shape...]
    ppermute x8 -> x0, waiting for transfers between devices: 57.9 us -> none  [shifted_2(): return lax.ppermute(block, axis, route)]
    all_gather x3 -> x0, blocking collectives: 36.7 us -> none  [beside_all(): slab_values = lax.all_gather(values, 'leaf', axis=1, tiled=True)]
    all_gather x1 -> x0, waiting for transfers between devices: 17.8 us -> none  [beside_all(): slab_values = lax.all_gather(values, 'leaf', axis=1, tiled=True)]
    ppermute x8 -> x0, starting transfers between devices: 13.5 us -> none  [shifted_2(): return lax.ppermute(block, axis, route)]
    another operation x14, other arithmetic: 80.6 us -> 93 us  [local(): joint_factor = jnp.linalg.cholesky(joint_gram)]
    pallas_call x1, Pallas kernels: 41 us -> 51.7 us  [gram_sum(): pl.pallas_call(lambda *refs: gram_kernel(phases, *refs), out_shape=jax.Sh...]
    reshape x3 -> x0, local copies, waits for them, and re-layouts: 6.59 us -> none  [apply_kernel(): reach = beside_all(values).reshape(width, 3 * slab_blocks, PB)]
  transfers between devices with their start and end apart: 9 -> 0, of which waited for: 7 -> 0; matrix products, arithmetic and copies ran while one was open for 1% -> 0% of each run, Pallas kernels for 0% -> 0%
where the time goes in v6:
time: 532 us; the launch traced here: 525 us
  Pallas kernels  285 us (54%)
  other arithmetic  150 us (28%)
  local copies, waits for them, and re-layouts  42.8 us (8%)
  matrix products  42.8 us (8%)
    pallas_call x4, Pallas kernels, halo_gather(): pl.pallas_call(lambda *refs: halo_kernel(n_blk, n_leaf, *refs), out_shape...  143 us
    another operation x14, other arithmetic, local(): joint_factor = jnp.linalg.cholesky(joint_gram)  93 us
    pallas_call x4, Pallas kernels, group_sum(): pl.pallas_call(lambda *refs: sum_kernel(phases, *refs), out_shape=jax.Sha...  90.2 us
    pallas_call x1, Pallas kernels, gram_sum(): pl.pallas_call(lambda *refs: gram_kernel(phases, *refs), out_shape=jax.Sh...  51.7 us
    another operation x4, other arithmetic, precond_from(): lax.linalg.triangular_solve(joint_factor, first_solve, left_side=True, lo...  41.9 us
    another operation x13, local copies, waits for them, and re-layouts, precond_from(): lax.linalg.triangular_solve(joint_factor, first_solve, left_side=True, lo...  12 us
    dot_general x3, matrix products, apply_kernel(): jnp.einsum('ncj,nij->ci', picked, kernel_tile, precision=lax.Precision.HI...  11.3 us

profile of v6, /device:TPU:4, one launch (start us, length us, event | category | flops | bytes accessed | tf_op | source)
XLA Modules:
  0.0 525.2 jit_solution(11196325529426580518)
XLA Ops:
  1.3 13.4 %shard_map.69 = f32[12,3,256]{2,1,0:T(4,128)} custom-call(f32[3,256]{1,0:T(4,128)} %refs_0_.3), custom_call_target="tpu_custom_call" | custom-call | tf_op jit(solution)/shard_map/pallas_call | solution.py:274
  17.5 2.6 multiply_multiply_fusion
  20.2 107.3 %shard_map.68 = f32[12,512,256]{2,1,0:T(8,128)} custom-call(f32[512,256]{1,0:T(8,128)} %refs_0_.2), custom_call_target="tpu_custom_call" | custom-call | tf_op jit(solution)/shard_map/pallas_call | solution.py:274
  127.4 5.7 %gather_fusion = f32[8,512,256]{2,1,0:T(8,128)} fusion(f32[12,512,256]{2,1,0:T(8,128)} %shard_map.68, s32[1024]{0:T(1024)S(1)} %pad_clamp_fusion.1), kind=kCustom, calls=%fused_computation.2 | custom fusion | bytes 8388640 | tf_op jit(solution)/shard_map/jit(_take)/gather | solution.py:313
  133.1 5.7 %fusion.16 = f32[512,256]{1,0:T(8,128)S(1)} fusion(f32[512,256]{1,0:T(8,128)S(1)} %copy-done, f32[8,256,256]{2,1,0:T(8,128)S(1)} %multiply_multiply_fusion, f32[8,512,256]{2,1,0:T(8,128)} %gather_fusion, pred[8]{0:T(512)(128)(4,1)S(1)} %compare_and_fusion), kind=kOutput, calls=%fused_computation.26 | convolution fusion | flops 3222405120 | bytes 7340040 | tf_op jit(solution)/shard_map/ncj,nij->ci/dot_general | solution.py:314
  140.8 2.6 copy.14
  145.4 2.5 copy.15
  148.0 3.6 fusion.23
  153.9 51.7 %shard_map.70 = f32[2048,128]{1,0:T(8,128)} custom-call(f32[2048,128]{1,0:T(8,128)} %reshape.152.refs_0_), custom_call_target="tpu_custom_call" | custom-call | tf_op jit(solution)/shard_map/pallas_call | solution.py:210
  205.6 2.4 reshape.153
  208.0 2.6 copy.16
  213.3 11.7 %cholesky.104 = f32[128,128]{1,0:T(8,128)S(1)} custom-call(f32[128,128]{1,0:T(8,128)S(1)} %cholesky.266), custom_call_target="Cholesky" | custom-call | tf_op jit(solution)/shard_map/jit(cholesky)/cholesky | solution.py:341
  226.2 9.8 %custom-call.33 = f32[1,128,128]{1,2,0:T(8,128)S(1)} custom-call(f32[1,128,128]{2,1,0:T(8,128)S(1)} %get-tuple-element.60), custom_call_target="InvertDiagBlocksLowerTriangular" | custom-call | tf_op jit(solution)/shard_map/jit(cholesky)/cholesky | solution.py:341
  239.3 24.6 %cholesky.217 = f32[128,128]{1,0:T(8,128)S(1)} custom-call(f32[128,128]{1,0:T(8,128)S(1)} %cholesky.270), custom_call_target="Cholesky" | custom-call | tf_op jit(solution)/shard_map/jit(cholesky)/cholesky | solution.py:341
  266.4 9.8 %custom-call.34 = f32[1,128,128]{1,2,0:T(8,128)S(1)} custom-call(f32[1,128,128]{2,1,0:T(8,128)S(1)} %get-tuple-element.57), custom_call_target="InvertDiagBlocksLowerTriangular" | custom-call | tf_op jit(solution)/shard_map/jit(cholesky)/cholesky | solution.py:341
  278.6 11.7 %cholesky.238 = f32[128,128]{1,0:T(8,128)S(1)} custom-call(f32[128,128]{1,0:T(8,128)S(1)} %cholesky.275), custom_call_target="Cholesky" | custom-call | tf_op jit(solution)/shard_map/jit(cholesky)/cholesky | solution.py:341
  292.3 9.8 %custom-call.35 = f32[1,128,128]{1,2,0:T(8,128)S(1)} custom-call(f32[1,128,128]{2,1,0:T(8,128)S(1)} %get-tuple-element.54), custom_call_target="InvertDiagBlocksLowerTriangular" | custom-call | tf_op jit(solution)/shard_map/jit(cholesky)/cholesky | solution.py:341
  304.4 11.7 %cholesky.255 = f32[128,128]{1,0:T(8,128)S(1)} custom-call(f32[128,128]{1,0:T(8,128)S(1)} %convolution_subtract_fusion.8), custom_call_target="Cholesky" | custom-call | tf_op jit(solution)/shard_map/jit(cholesky)/cholesky | solution.py:341
  318.0 2.4 select_select_fusion
  320.4 12.0 %while.8 = (s32[]{:T(128)}, f32[512,512]{1,0:T(8,128)}, s32[4,2]{0,1:T(2,128)S(1)}, f32[4,128,128]{2,1,0:T(8,128)S(1)}, s32[]{:T(128)}) while((s32[]{:T(128)}, f32[512,512]{1,0:T(8,128)}, s32[4,2]{0,1:T(2,128)S(1)}, f32[4,128,128]{2,1,0:T(8,128)S(1)}, s32[]{:T(128)}) %tuple.51), condition=%wide.while_cond.1, body=%wide.while_body.1.sunk | while | flops 2 | bytes 131181 | solution.py:345
  321.1 2.3 bitcast_dynamic-update-slice_fusion.2
  324.1 2.3 bitcast_dynamic-update-slice_fusion.2
  327.1 2.3 bitcast_dynamic-update-slice_fusion.2
  332.4 39.5 %custom-call.39 = f32[4,128,128]{1,2,0:T(8,128)S(1)} custom-call(f32[4,128,128]{2,1,0:T(8,128)S(1)} %get-tuple-element.34), custom_call_target="InvertDiagBlocksLowerTriangular" | custom-call | tf_op jit(solution)/shard_map/triangular_solve/custom-call.8 | solution.py:345
  373.3 27.8 %shard_map.71 = f32[128,128]{1,0:T(8,128)} custom-call(f32[128,128]{1,0:T(8,128)} %reshape.154.refs_0_), custom_call_target="tpu_custom_call" | custom-call | tf_op jit(solution)/shard_map/pallas_call | solution.py:109
  411.7 10.9 %shard_map.72 = f32[12,32,256]{2,1,0:T(8,128)} custom-call(f32[32,256]{1,0:T(8,128)} %convolution_subtract_fusion.10.refs_0_), custom_call_target="tpu_custom_call" | custom-call | tf_op jit(solution)/shard_map/pallas_call | solution.py:274
  424.2 2.8 multiply_reduce_fusion.3
  429.7 27.9 %shard_map.73 = f32[136,128]{1,0:T(8,128)} custom-call(f32[136,128]{1,0:T(8,128)} %pad_maximum_fusion.refs_0_), custom_call_target="tpu_custom_call" | custom-call | tf_op jit(solution)/shard_map/pallas_call | solution.py:109
  470.7 15.6 %shard_map.74 = f32[8,128]{1,0:T(8,128)} custom-call(f32[8,128]{1,0:T(8,128)} %pad.13.refs_0_), custom_call_target="tpu_custom_call" | custom-call | tf_op jit(solution)/shard_map/pallas_call | solution.py:109
  487.7 11.8 %shard_map.75 = f32[12,32,256]{2,1,0:T(8,128)} custom-call(f32[32,256]{1,0:T(8,128)} %multiply_add_fusion.1.refs_0_), custom_call_target="tpu_custom_call" | custom-call | tf_op jit(solution)/shard_map/pallas_call | solution.py:274
  501.1 2.8 multiply_reduce_fusion
  504.4 18.9 %shard_map.76 = f32[8,128]{1,0:T(8,128)} custom-call(f32[8,128]{1,0:T(8,128)} %pad.14.refs_0_), custom_call_target="tpu_custom_call" | custom-call | tf_op jit(solution)/shard_map/pallas_call | solution.py:109
  (106 shorter events, 64.3 us)
Async XLA Ops:
  16.2 1.3 copy-start.6
  127.4 5.7 %copy-start = (f32[512,256]{1,0:T(8,128)S(1)}, f32[512,256]{1,0:T(8,128)}, u32[]{:S(2)}) copy-start(f32[512,256]{1,0:T(8,128)} %refs_0_.2) | copy-start | bytes 1572868
  212.3 1.0 copy-start.1
  278.6 93.3 %copy-start.3 = (f32[32,256]{1,0:T(8,128)S(1)}, f32[32,256]{1,0:T(8,128)}, u32[]{:S(2)}) copy-start(f32[32,256]{1,0:T(8,128)} %param.15) | copy-start | bytes 98308
  278.6 93.3 %copy-start.5 = (f32[256]{0:T(256)S(1)}, f32[256]{0:T(256)}, u32[]{:S(2)}) copy-start(f32[256]{0:T(256)} %param.14) | copy-start | bytes 3076
  459.1 27.9 %copy-start.2 = (f32[32,256]{1,0:T(8,128)S(1)}, f32[32,256]{1,0:T(8,128)}, u32[]{:S(2)}) copy-start(f32[32,256]{1,0:T(8,128)} %convolution_subtract_fusion.10.refs_0_) | copy-start | bytes 98308
  487.7 36.4 %copy-start.4 = (f32[32,256]{1,0:T(8,128)S(1)}, f32[32,256]{1,0:T(8,128)}, u32[]{:S(2)}) copy-start(f32[32,256]{1,0:T(8,128)} %multiply_add_fusion.1.refs_0_) | copy-start | bytes 98308

commit v7 on v6

--- a/solution.py
+++ b/solution.py
@@ -309,7 +309,11 @@
 
     def apply_kernel(values):
         width = values.shape[0]
-        reach = halo_gather(values, 5 if width == omega.shape[0] else 6)
+        if width == omega.shape[0]:
+            reach = beside_all(values).reshape(width, 3 * slab_blocks, PB)
+            picked = jnp.take(reach, chosen[0], axis=1)
+            return jnp.einsum("cnj,nij->ci", picked, kernel_tile, precision=lax.Precision.HIGHEST)
+        reach = halo_gather(values, 6)
         picked = jnp.take(reach, chosen[0], axis=0)
         return jnp.einsum("ncj,nij->ci", picked, kernel_tile, precision=lax.Precision.HIGHEST)
 

time: 532 us -> 513 us (0.964)
  Pallas kernels: 285 us -> 171 us
  waiting for transfers between devices: 0 us -> 62.4 us
  between operations: 4.18 us -> 17.5 us
  local copies, waits for them, and re-layouts: 42.8 us -> 51.3 us
  other arithmetic: 150 us -> 156 us
    pallas_call x4 -> x3, Pallas kernels: 143 us -> 35.1 us  [halo_gather(): pl.pallas_call(lambda *refs: halo_kernel(n_blk, n_leaf, *refs), out_shape...]
    ppermute x0 -> x2, waiting for transfers between devices: none -> 38.9 us  [shifted_2(): return lax.ppermute(block, axis, route)]
    all_gather x0 -> x1, waiting for transfers between devices: none -> 23.4 us  [beside_all(): slab_values = lax.all_gather(values, 'leaf', axis=1, tiled=True)]
    pallas_call x1, Pallas kernels: 51.7 us -> 44.8 us  [gram_sum(): pl.pallas_call(lambda *refs: gram_kernel(phases, *refs), out_shape=jax.Sh...]
    reshape x0 -> x1, local copies, waits for them, and re-layouts: none -> 6.52 us  [apply_kernel(): reach = beside_all(values).reshape(width, 3 * slab_blocks, PB)]
    dot_general x0 -> x1, matrix products: none -> 5.72 us  [apply_kernel(): jnp.einsum('cnj,nij->ci', picked, kernel_tile, precision=lax.Precision.HI...]
    dot_general x3 -> x2, matrix products: 11.3 us -> 5.54 us  [apply_kernel(): jnp.einsum('ncj,nij->ci', picked, kernel_tile, precision=lax.Precision.HI...]
    gather x3 -> x2, local copies, waits for them, and re-layouts: 8.81 us -> 3.12 us  [apply_kernel(): picked = jnp.take(reach, chosen[0], axis=0)]
  transfers between devices with their start and end apart: 0 -> 3, of which waited for: 0 -> 2; matrix products, arithmetic and copies ran while one was open for 0% -> 1% of each run, Pallas kernels for 0% -> 3%
where the time goes in v7:
time: 513 us; the launch traced here: 506 us
  Pallas kernels  171 us (33%)
  other arithmetic  156 us (30%)
  waiting for transfers between devices  62.4 us (12%)
  local copies, waits for them, and re-layouts  51.3 us (10%)
  matrix products  42.8 us (8%)
  between operations  17.5 us (3%)
    another operation x14, other arithmetic, local(): joint_factor = jnp.linalg.cholesky(joint_gram)  93.1 us
    pallas_call x4, Pallas kernels, group_sum(): pl.pallas_call(lambda *refs: sum_kernel(phases, *refs), out_shape=jax.Sha...  91.1 us
    pallas_call x1, Pallas kernels, gram_sum(): pl.pallas_call(lambda *refs: gram_kernel(phases, *refs), out_shape=jax.Sh...  44.8 us
    another operation x4, other arithmetic, precond_from(): lax.linalg.triangular_solve(joint_factor, first_solve, left_side=True, lo...  41.9 us
    ppermute x2, waiting for transfers between devices, shifted_2(): return lax.ppermute(block, axis, route)  38.9 us
    pallas_call x3, Pallas kernels, halo_gather(): pl.pallas_call(lambda *refs: halo_kernel(n_blk, n_leaf, *refs), out_shape...  35.1 us
    all_gather x1, waiting for transfers between devices, beside_all(): slab_values = lax.all_gather(values, 'leaf', axis=1, tiled=True)  23.4 us
    another operation x13, local copies, waits for them, and re-layouts, precond_from(): lax.linalg.triangular_solve(joint_factor, first_solve, left_side=True, lo...  12 us
  transfers between devices with their start and end apart: 3, of which 2 were waited for; matrix products, arithmetic and copies ran while one was open for 1% of the time, Pallas kernels for 3%

profile of v7, /device:TPU:4, one launch (start us, length us, event | category | flops | bytes accessed | tf_op | source)
XLA Modules:
  0.0 505.6 jit_solution(14826305644227813658)
XLA Ops:
  9.3 13.4 %shard_map.68 = f32[12,3,256]{2,1,0:T(4,128)} custom-call(f32[3,256]{1,0:T(4,128)} %refs_0_.1), custom_call_target="tpu_custom_call" | custom-call | tf_op jit(solution)/shard_map/pallas_call | solution.py:274
  22.7 23.4 %all-gather.2.cloned.1.call-done = f32[512,1024]{0,1:T(8,128)} async-done(((f32[512,256]{0,1:T(8,128)}), f32[512,1024]{0,1:T(8,128)}) %all-gather.2.cloned.1.call-update) | async-done | bytes 2097168 | tf_op jit(solution)/shard_map/all_gather | solution.py:44
  47.7 2.6 collective-permute-start.1
  54.4 2.6 multiply_multiply_fusion
  57.0 38.9 %collective-permute-done = f32[512,1024]{0,1:T(8,128)} collective-permute-done((f32[512,1024]{0,1:T(8,128)}, f32[512,1024]{0,1:T(8,128)}, u32[]{:S(2)}, u32[]{:S(2)}) %collective-permute-start) | collective-permute-done | bytes 2097184 | tf_op jit(solution)/shard_map/ppermute | solution.py:22
  96.0 5.6 %pad_maximum_fusion = f32[512,3072]{0,1:T(8,128)} fusion(f32[512,1024]{0,1:T(8,128)} %collective-permute-done.1, f32[512,1024]{0,1:T(8,128)S(1)} %copy-done.2, f32[512,1024]{0,1:T(8,128)} %collective-permute-done), kind=kLoop, calls=%fused_computation.6 | loop fusion | flops 3145728 | bytes 12582912 | tf_op jit(solution)/shard_map/concatenate | solution.py:45
  101.6 6.5 %copy.14 = f32[512,12,256]{2,0,1:T(8,128)} copy(f32[512,12,256]{0,2,1:T(8,128)} %bitcast.169) | data formatting | bytes 12582912 | tf_op jit(solution)/shard_map/reshape | solution.py:313
  108.1 5.6 %gather_fusion = f32[8,512,256]{2,1,0:T(8,128)} fusion(f32[512,12,256]{2,0,1:T(8,128)} %copy.14, s32[1024]{0:T(1024)S(1)} %pad_clamp_fusion.1), kind=kCustom, calls=%fused_computation.2 | custom fusion | bytes 8388640 | tf_op jit(solution)/shard_map/jit(_take)/gather | solution.py:314
  113.7 5.7 %fusion.17 = f32[512,256]{1,0:T(8,128)S(1)} fusion(f32[512,256]{1,0:T(8,128)S(1)} %copy-done, f32[8,256,256]{2,1,0:T(8,128)S(1)} %multiply_multiply_fusion, f32[8,512,256]{2,1,0:T(8,128)} %gather_fusion, pred[8]{0:T(512)(128)(4,1)S(1)} %compare_and_fusion), kind=kOutput, calls=%fused_computation.28 | convolution fusion | flops 3222405120 | bytes 7340040 | tf_op jit(solution)/shard_map/cnj,nij->ci/dot_general | solution.py:315
  123.4 2.5 copy.16
  125.9 2.6 copy.17
  128.5 3.6 fusion.24
  134.5 44.8 %shard_map.69 = f32[2048,128]{1,0:T(8,128)} custom-call(f32[2048,128]{1,0:T(8,128)} %reshape.156.refs_0_), custom_call_target="tpu_custom_call" | custom-call | tf_op jit(solution)/shard_map/pallas_call | solution.py:210
  179.3 2.4 reshape.157
  181.7 2.6 copy.18
  187.0 11.7 %cholesky.104 = f32[128,128]{1,0:T(8,128)S(1)} custom-call(f32[128,128]{1,0:T(8,128)S(1)} %cholesky.266), custom_call_target="Cholesky" | custom-call | tf_op jit(solution)/shard_map/jit(cholesky)/cholesky | solution.py:345
  200.0 9.8 %custom-call.33 = f32[1,128,128]{1,2,0:T(8,128)S(1)} custom-call(f32[1,128,128]{2,1,0:T(8,128)S(1)} %get-tuple-element.60), custom_call_target="InvertDiagBlocksLowerTriangular" | custom-call | tf_op jit(solution)/shard_map/jit(cholesky)/cholesky | solution.py:345
  213.0 24.6 %cholesky.217 = f32[128,128]{1,0:T(8,128)S(1)} custom-call(f32[128,128]{1,0:T(8,128)S(1)} %cholesky.270), custom_call_target="Cholesky" | custom-call | tf_op jit(solution)/shard_map/jit(cholesky)/cholesky | solution.py:345
  238.2 9.8 %custom-call.34 = f32[1,128,128]{1,2,0:T(8,128)S(1)} custom-call(f32[1,128,128]{2,1,0:T(8,128)S(1)} %get-tuple-element.57), custom_call_target="InvertDiagBlocksLowerTriangular" | custom-call | tf_op jit(solution)/shard_map/jit(cholesky)/cholesky | solution.py:345
  250.4 11.7 %cholesky.238 = f32[128,128]{1,0:T(8,128)S(1)} custom-call(f32[128,128]{1,0:T(8,128)S(1)} %cholesky.275), custom_call_target="Cholesky" | custom-call | tf_op jit(solution)/shard_map/jit(cholesky)/cholesky | solution.py:345
  263.4 9.8 %custom-call.35 = f32[1,128,128]{1,2,0:T(8,128)S(1)} custom-call(f32[1,128,128]{2,1,0:T(8,128)S(1)} %get-tuple-element.54), custom_call_target="InvertDiagBlocksLowerTriangular" | custom-call | tf_op jit(solution)/shard_map/jit(cholesky)/cholesky | solution.py:345
  275.5 11.7 %cholesky.255 = f32[128,128]{1,0:T(8,128)S(1)} custom-call(f32[128,128]{1,0:T(8,128)S(1)} %convolution_subtract_fusion.8), custom_call_target="Cholesky" | custom-call | tf_op jit(solution)/shard_map/jit(cholesky)/cholesky | solution.py:345
  294.1 12.0 %while.8 = (s32[]{:T(128)}, f32[512,512]{1,0:T(8,128)}, s32[4,2]{0,1:T(2,128)S(1)}, f32[4,128,128]{2,1,0:T(8,128)S(1)}, s32[]{:T(128)}) while((s32[]{:T(128)}, f32[512,512]{1,0:T(8,128)}, s32[4,2]{0,1:T(2,128)S(1)}, f32[4,128,128]{2,1,0:T(8,128)S(1)}, s32[]{:T(128)}) %tuple.51), condition=%wide.while_cond.1, body=%wide.while_body.1.sunk | while | flops 2 | bytes 131181 | solution.py:349
  306.1 39.5 %custom-call.39 = f32[4,128,128]{1,2,0:T(8,128)S(1)} custom-call(f32[4,128,128]{2,1,0:T(8,128)S(1)} %get-tuple-element.34), custom_call_target="InvertDiagBlocksLowerTriangular" | custom-call | tf_op jit(solution)/shard_map/triangular_solve/custom-call.8 | solution.py:349
  347.0 28.4 %shard_map.70 = f32[128,128]{1,0:T(8,128)} custom-call(f32[128,128]{1,0:T(8,128)} %reshape.158.refs_0_), custom_call_target="tpu_custom_call" | custom-call | tf_op jit(solution)/shard_map/pallas_call | solution.py:109
  386.0 11.4 %shard_map.71 = f32[12,32,256]{2,1,0:T(8,128)} custom-call(f32[32,256]{1,0:T(8,128)} %convolution_subtract_fusion.10.refs_0_), custom_call_target="tpu_custom_call" | custom-call | tf_op jit(solution)/shard_map/pallas_call | solution.py:274
  398.9 2.8 multiply_reduce_fusion.3
  404.5 28.1 %shard_map.72 = f32[136,128]{1,0:T(8,128)} custom-call(f32[136,128]{1,0:T(8,128)} %pad_maximum_fusion.1.refs_0_), custom_call_target="tpu_custom_call" | custom-call | tf_op jit(solution)/shard_map/pallas_call | solution.py:109
  445.7 15.0 %shard_map.73 = f32[8,128]{1,0:T(8,128)} custom-call(f32[8,128]{1,0:T(8,128)} %pad.13.refs_0_), custom_call_target="tpu_custom_call" | custom-call | tf_op jit(solution)/shard_map/pallas_call | solution.py:109
  462.0 10.3 %shard_map.74 = f32[12,32,256]{2,1,0:T(8,128)} custom-call(f32[32,256]{1,0:T(8,128)} %multiply_add_fusion.1.refs_0_), custom_call_target="tpu_custom_call" | custom-call | tf_op jit(solution)/shard_map/pallas_call | solution.py:274
  474.0 2.8 multiply_reduce_fusion
  477.3 19.7 %shard_map.75 = f32[8,128]{1,0:T(8,128)} custom-call(f32[8,128]{1,0:T(8,128)} %pad.14.refs_0_), custom_call_target="tpu_custom_call" | custom-call | tf_op jit(solution)/shard_map/pallas_call | solution.py:109
  (115 shorter events, 78.0 us)
Async XLA Ops:
  7.2 39.0 %all-gather.2.cloned.1.call-start = ((), (), s32[]{:S(2)}) async-start(), calls=%async_computation | async-start | bytes 2621440 | tf_op jit(solution)/shard_map/all_gather | solution.py:44
  46.2 49.8 %collective-permute-start = (f32[512,1024]{0,1:T(8,128)}, f32[512,1024]{0,1:T(8,128)}, u32[]{:S(2)}, u32[]{:S(2)}) collective-permute-start(f32[512,1024]{0,1:T(8,128)} %all-gather.2.cloned.1.call-done), channel_id=1, source_target_pairs={{248,0},{0,8},{8,16},{16,24},{24,32},{32,40},{40,48},{48,56},{56,6... | collective-permute-start | bytes 6291464 | tf_op jit(solution)/shard_map/ppermute | solution.py:22
  47.7 48.2 %collective-permute-start.1 = (f32[512,1024]{0,1:T(8,128)}, f32[512,1024]{0,1:T(8,128)}, u32[]{:S(2)}, u32[]{:S(2)}) collective-permute-start(f32[512,1024]{0,1:T(8,128)} %all-gather.2.cloned.1.call-done), channel_id=1, source_target_pairs={{8,0},{16,8},{24,16},{32,24},{40,32},{48,40},{56,48},{64,56},{72,6... | collective-permute-start | bytes 6291464 | tf_op jit(solution)/shard_map/ppermute | solution.py:22
  54.4 41.6 %copy-start.2 = (f32[512,1024]{0,1:T(8,128)S(1)}, f32[512,1024]{0,1:T(8,128)}, u32[]{:S(2)}) copy-start(f32[512,1024]{0,1:T(8,128)} %all-gather.2.cloned.1.call-done) | copy-start | bytes 6291460
  108.1 5.6 %copy-start = (f32[512,256]{1,0:T(8,128)S(1)}, f32[512,256]{1,0:T(8,128)}, u32[]{:S(2)}) copy-start(f32[512,256]{1,0:T(8,128)} %param.13) | copy-start | bytes 1572868
  186.0 1.0 copy-start.1
  250.4 95.3 %copy-start.4 = (f32[32,256]{1,0:T(8,128)S(1)}, f32[32,256]{1,0:T(8,128)}, u32[]{:S(2)}) copy-start(f32[32,256]{1,0:T(8,128)} %param.15) | copy-start | bytes 98308
  250.4 95.3 %copy-start.6 = (f32[256]{0:T(256)S(1)}, f32[256]{0:T(256)}, u32[]{:S(2)}) copy-start(f32[256]{0:T(256)} %param.14) | copy-start | bytes 3076
  434.8 26.5 %copy-start.3 = (f32[32,256]{1,0:T(8,128)S(1)}, f32[32,256]{1,0:T(8,128)}, u32[]{:S(2)}) copy-start(f32[32,256]{1,0:T(8,128)} %convolution_subtract_fusion.10.refs_0_) | copy-start | bytes 98308
  462.0 35.7 %copy-start.5 = (f32[32,256]{1,0:T(8,128)S(1)}, f32[32,256]{1,0:T(8,128)}, u32[]{:S(2)}) copy-start(f32[32,256]{1,0:T(8,128)} %multiply_add_fusion.1.refs_0_) | copy-start | bytes 98308
Sparse Core Ops, SparseCore 0:
  9.8 36.3 all-gather.1

commit v8 on v7

--- a/solution.py
+++ b/solution.py
@@ -304,18 +304,28 @@
     reach_blocks = halo_gather(points, 4)
     row_blocks = points.reshape(3, blk_dev, PB).transpose(1, 0, 2)
 
-    kernel_tile = wendland(row_blocks[0], reach_blocks[chosen[0]], period)
-    kernel_tile = kernel_tile * usable_weight[0][:, None, None]
+    segments = 3 * slab_blocks
+    listed = jnp.zeros((segments,), jnp.float32).at[chosen[0]].max(usable_weight[0])
+    kernel_tile = wendland(row_blocks[0], reach_blocks, period) * listed[:, None, None]
 
     def apply_kernel(values):
         width = values.shape[0]
         if width == omega.shape[0]:
-            reach = beside_all(values).reshape(width, 3 * slab_blocks, PB)
-            picked = jnp.take(reach, chosen[0], axis=1)
-            return jnp.einsum("cnj,nij->ci", picked, kernel_tile, precision=lax.Precision.HIGHEST)
+            slab_values = lax.all_gather(values, "leaf", axis=1, tiled=True)
+            parts = (shifted(slab_values, 1), slab_values, shifted(slab_values, -1))
+            out = None
+            for i, part in enumerate(parts):
+                tile = kernel_tile[i * slab_blocks : (i + 1) * slab_blocks]
+                term = jnp.einsum(
+                    "cnj,nij->ci",
+                    part.reshape(width, slab_blocks, PB),
+                    tile,
+                    precision=lax.Precision.HIGHEST,
+                )
+                out = term if out is None else out + term
+            return out
         reach = halo_gather(values, 6)
-        picked = jnp.take(reach, chosen[0], axis=0)
-        return jnp.einsum("ncj,nij->ci", picked, kernel_tile, precision=lax.Precision.HIGHEST)
+        return jnp.einsum("ncj,nij->ci", reach, kernel_tile, precision=lax.Precision.HIGHEST)
 
     def slot(x):
         zeros = jnp.zeros((n_samp,) + x.shape, x.dtype)

time: 513 us -> 510 us (level)
  Pallas kernels: 171 us -> 209 us
  waiting for transfers between devices: 62.4 us -> 36.9 us
  other arithmetic: 156 us -> 143 us
  matrix products: 42.8 us -> 54.3 us
  local copies, waits for them, and re-layouts: 51.3 us -> 40.4 us
    ppermute x2, waiting for transfers between devices: 38.9 us -> 0.01 us  [shifted_2(): return lax.ppermute(block, axis, route)]
    pallas_call x3, Pallas kernels: 35.1 us -> 72 us  [halo_gather(): pl.pallas_call(lambda *refs: halo_kernel(n_blk, n_leaf, *refs), out_shape...]
    all_gather x1, waiting for transfers between devices: 23.4 us -> 36.9 us  [apply_kernel(): slab_values = lax.all_gather(values, 'leaf', axis=1, tiled=True)]
    another operation x14, other arithmetic: 93.1 us -> 80.9 us  [local(): joint_factor = jnp.linalg.cholesky(joint_gram)]
    gather x5 -> x0, local copies, waits for them, and re-layouts: 10.1 us -> none  [the longest x1 5.58 us: apply_kernel(): picked = jnp.take(reach, chosen[0], axis=1)]
    reshape x1 -> x0, local copies, waits for them, and re-layouts: 6.52 us -> none  [apply_kernel(): reach = beside_all(values).reshape(width, 3 * slab_blocks, PB)]
    dot_general x3 -> x5, matrix products: 11.3 us -> 17 us  [the longest x3 9.1 us: apply_kernel(): jnp.einsum('cnj,nij->ci', part.reshape(width, slab_blocks, PB), tile, pre...]
    concatenate x1 -> x0, other arithmetic: 5.59 us -> none  [beside_all(): jnp.concatenate([shifted(slab_values, 1), slab_values, shifted(slab_value...]
  transfers between devices with their start and end apart: 3 -> 3, of which waited for: 2 -> 1; matrix products, arithmetic and copies ran while one was open for 1% -> 3% of each run, Pallas kernels for 3% -> 10%
where the time goes in v8:
time: 510 us; the launch traced here: 504 us
  Pallas kernels  209 us (41%)
  other arithmetic  143 us (28%)
  matrix products  54.3 us (11%)
  local copies, waits for them, and re-layouts  40.4 us (8%)
  waiting for transfers between devices  36.9 us (7%)
  between operations  17.3 us (3%)
    pallas_call x4, Pallas kernels, group_sum(): pl.pallas_call(lambda *refs: sum_kernel(phases, *refs), out_shape=jax.Sha...  93.2 us
    another operation x14, other arithmetic, local(): joint_factor = jnp.linalg.cholesky(joint_gram)  80.9 us
    pallas_call x3, Pallas kernels, halo_gather(): pl.pallas_call(lambda *refs: halo_kernel(n_blk, n_leaf, *refs), out_shape...  72 us
    pallas_call x1, Pallas kernels, gram_sum(): pl.pallas_call(lambda *refs: gram_kernel(phases, *refs), out_shape=jax.Sh...  43.3 us
    another operation x4, other arithmetic, precond_from(): lax.linalg.triangular_solve(joint_factor, first_solve, left_side=True, lo...  42.6 us
    all_gather x1, waiting for transfers between devices, apply_kernel(): slab_values = lax.all_gather(values, 'leaf', axis=1, tiled=True)  36.9 us
    another operation x13, local copies, waits for them, and re-layouts, precond_from(): lax.linalg.triangular_solve(joint_factor, first_solve, left_side=True, lo...  13.6 us
    dot_general x6, matrix products, high_dot(): jnp.dot(left, right, precision=lax.Precision.HIGHEST, preferred_element_t...  11.4 us
  transfers between devices with their start and end apart: 3, of which 1 were waited for; matrix products, arithmetic and copies ran while one was open for 3% of the time, Pallas kernels for 10%

profile of v8, /device:TPU:4, one launch (start us, length us, event | category | flops | bytes accessed | tf_op | source)
XLA Modules:
  0.0 504.0 jit_solution(13922383103611082656)
XLA Ops:
  9.3 36.9 %all-gather.2.cloned.1.call-done = f32[512,1024]{0,1:T(8,128)} async-done(((f32[512,256]{0,1:T(8,128)}), f32[512,1024]{0,1:T(8,128)}) %all-gather.2.cloned.1.call-update) | async-done | bytes 2097168 | tf_op jit(solution)/shard_map/all_gather | solution.py:314
  46.2 3.3 collective-permute-start.1
  50.2 51.0 %shard_map.68 = f32[12,3,256]{2,1,0:T(4,128)} custom-call(f32[3,256]{1,0:T(4,128)} %refs_0_.1), custom_call_target="tpu_custom_call" | custom-call | tf_op jit(solution)/shard_map/pallas_call | solution.py:274
  105.2 4.2 multiply_multiply_fusion
  111.3 3.6 convolution_bitcast_fusion
  114.9 3.6 fusion.12
  125.1 2.6 copy.21
  127.6 3.6 fusion.17
  133.6 43.3 %shard_map.69 = f32[2048,128]{1,0:T(8,128)} custom-call(f32[2048,128]{1,0:T(8,128)} %reshape.153.refs_0_), custom_call_target="tpu_custom_call" | custom-call | tf_op jit(solution)/shard_map/pallas_call | solution.py:210
  179.2 2.6 copy.22
  184.6 11.9 %cholesky.104 = f32[128,128]{1,0:T(8,128)S(1)} custom-call(f32[128,128]{1,0:T(8,128)S(1)} %cholesky.266), custom_call_target="Cholesky" | custom-call | tf_op jit(solution)/shard_map/jit(cholesky)/cholesky | solution.py:355
  197.7 9.8 %custom-call.33 = f32[1,128,128]{1,2,0:T(8,128)S(1)} custom-call(f32[1,128,128]{2,1,0:T(8,128)S(1)} %get-tuple-element.57), custom_call_target="InvertDiagBlocksLowerTriangular" | custom-call | tf_op jit(solution)/shard_map/jit(cholesky)/cholesky | solution.py:355
  210.8 11.7 %cholesky.217 = f32[128,128]{1,0:T(8,128)S(1)} custom-call(f32[128,128]{1,0:T(8,128)S(1)} %cholesky.270), custom_call_target="Cholesky" | custom-call | tf_op jit(solution)/shard_map/jit(cholesky)/cholesky | solution.py:355
  223.2 9.8 %custom-call.34 = f32[1,128,128]{1,2,0:T(8,128)S(1)} custom-call(f32[1,128,128]{2,1,0:T(8,128)S(1)} %get-tuple-element.54), custom_call_target="InvertDiagBlocksLowerTriangular" | custom-call | tf_op jit(solution)/shard_map/jit(cholesky)/cholesky | solution.py:355
  235.4 12.1 %cholesky.238 = f32[128,128]{1,0:T(8,128)S(1)} custom-call(f32[128,128]{1,0:T(8,128)S(1)} %cholesky.275), custom_call_target="Cholesky" | custom-call | tf_op jit(solution)/shard_map/jit(cholesky)/cholesky | solution.py:355
  248.8 9.8 %custom-call.35 = f32[1,128,128]{1,2,0:T(8,128)S(1)} custom-call(f32[1,128,128]{2,1,0:T(8,128)S(1)} %get-tuple-element.51), custom_call_target="InvertDiagBlocksLowerTriangular" | custom-call | tf_op jit(solution)/shard_map/jit(cholesky)/cholesky | solution.py:355
  260.9 11.7 %cholesky.255 = f32[128,128]{1,0:T(8,128)S(1)} custom-call(f32[128,128]{1,0:T(8,128)S(1)} %convolution_subtract_fusion.8), custom_call_target="Cholesky" | custom-call | tf_op jit(solution)/shard_map/jit(cholesky)/cholesky | solution.py:355
  279.5 13.6 %while.8 = (s32[]{:T(128)}, f32[512,512]{1,0:T(8,128)}, s32[4,2]{0,1:T(2,128)S(1)}, f32[4,128,128]{2,1,0:T(8,128)}, s32[]{:T(128)}) while((s32[]{:T(128)}, f32[512,512]{1,0:T(8,128)}, s32[4,2]{0,1:T(2,128)S(1)}, f32[4,128,128]{2,1,0:T(8,128)}, s32[]{:T(128)}) %tuple.49), condition=%wide.while_cond.1, body=%wide.while_body.1.sunk | while | flops 2 | bytes 132705 | solution.py:359
  280.1 2.8 bitcast_dynamic-update-slice_fusion.2
  283.5 2.8 bitcast_dynamic-update-slice_fusion.2
  286.9 2.8 bitcast_dynamic-update-slice_fusion.2
  290.3 2.7 bitcast_dynamic-update-slice_fusion.2
  293.0 40.3 %custom-call.39 = f32[4,128,128]{1,2,0:T(8,128)S(1)} custom-call(f32[4,128,128]{2,1,0:T(8,128)} %get-tuple-element.33), custom_call_target="InvertDiagBlocksLowerTriangular" | custom-call | tf_op jit(solution)/shard_map/triangular_solve/custom-call.8 | solution.py:359
  333.4 2.8 fusion.110
  337.8 30.2 %shard_map.70 = f32[128,128]{1,0:T(8,128)} custom-call(f32[128,128]{1,0:T(8,128)} %reshape.155.refs_0_), custom_call_target="tpu_custom_call" | custom-call | tf_op jit(solution)/shard_map/pallas_call | solution.py:109
  381.5 10.6 %shard_map.71 = f32[12,32,256]{2,1,0:T(8,128)} custom-call(f32[32,256]{1,0:T(8,128)} %convolution_subtract_fusion.10.refs_0_), custom_call_target="tpu_custom_call" | custom-call | tf_op jit(solution)/shard_map/pallas_call | solution.py:274
  392.1 4.0 multiply_reduce_fusion.3
  401.0 28.6 %shard_map.72 = f32[136,128]{1,0:T(8,128)} custom-call(f32[136,128]{1,0:T(8,128)} %pad_maximum_fusion.refs_0_), custom_call_target="tpu_custom_call" | custom-call | tf_op jit(solution)/shard_map/pallas_call | solution.py:109
  444.6 15.5 %shard_map.73 = f32[8,128]{1,0:T(8,128)} custom-call(f32[8,128]{1,0:T(8,128)} %pad.13.refs_0_), custom_call_target="tpu_custom_call" | custom-call | tf_op jit(solution)/shard_map/pallas_call | solution.py:109
  461.5 10.5 %shard_map.74 = f32[12,32,256]{2,1,0:T(8,128)} custom-call(f32[32,256]{1,0:T(8,128)} %multiply_add_fusion.1.refs_0_), custom_call_target="tpu_custom_call" | custom-call | tf_op jit(solution)/shard_map/pallas_call | solution.py:274
  472.0 3.9 multiply_reduce_fusion
  476.6 18.9 %shard_map.75 = f32[8,128]{1,0:T(8,128)} custom-call(f32[8,128]{1,0:T(8,128)} %pad.14.refs_0_), custom_call_target="tpu_custom_call" | custom-call | tf_op jit(solution)/shard_map/pallas_call | solution.py:109
  (116 shorter events, 78.7 us)
Async XLA Ops:
  7.2 39.0 %all-gather.2.cloned.1.call-start = ((), (), s32[]{:S(2)}) async-start(), calls=%async_computation | async-start | bytes 2621440 | tf_op jit(solution)/shard_map/all_gather | solution.py:314
  46.2 65.1 %collective-permute-start.1 = (f32[512,1024]{0,1:T(8,128)}, f32[512,1024]{0,1:T(8,128)}, u32[]{:S(2)}, u32[]{:S(2)}) collective-permute-start(f32[512,1024]{0,1:T(8,128)} %all-gather.2.cloned.1.call-done), channel_id=1, source_target_pairs={{8,0},{16,8},{24,16},{32,24},{40,32},{48,40},{56,48},{64,56},{72,6... | collective-permute-start | bytes 6291464 | tf_op jit(solution)/shard_map/ppermute | solution.py:22
  49.5 65.4 %collective-permute-start = (f32[512,1024]{0,1:T(8,128)}, f32[512,1024]{0,1:T(8,128)}, u32[]{:S(2)}, u32[]{:S(2)}) collective-permute-start(f32[512,1024]{0,1:T(8,128)} %all-gather.2.cloned.1.call-done), channel_id=1, source_target_pairs={{248,0},{0,8},{8,16},{16,24},{24,32},{32,40},{40,48},{48,56},{56,6... | collective-permute-start | bytes 6291464 | tf_op jit(solution)/shard_map/ppermute | solution.py:22
  105.1 4.2 copy-start.5
  111.3 3.6 copy-start.3
  114.9 3.6 copy-start.6
  118.5 2.0 copy-start
  183.6 1.0 copy-start.4
  207.5 125.8 %copy-start.8 = (f32[32,256]{1,0:T(8,128)S(1)}, f32[32,256]{1,0:T(8,128)}, u32[]{:S(2)}) copy-start(f32[32,256]{1,0:T(8,128)} %param.13) | copy-start | bytes 98308
  207.6 125.8 %copy-start.10 = (f32[256]{0:T(256)S(1)}, f32[256]{0:T(256)}, u32[]{:S(2)}) copy-start(f32[256]{0:T(256)} %param.12) | copy-start | bytes 3076
  392.0 4.0 copy-start.1
  396.1 64.8 %copy-start.7 = (f32[32,256]{1,0:T(8,128)S(1)}, f32[32,256]{1,0:T(8,128)}, u32[]{:S(2)}) copy-start(f32[32,256]{1,0:T(8,128)} %convolution_subtract_fusion.10.refs_0_) | copy-start | bytes 98308
  433.4 9.9 %copy-start.2 = (f32[512,256]{0,1:T(8,128)S(1)}, f32[512,256]{0,1:T(8,128)}, u32[]{:S(2)}) copy-start(f32[512,256]{0,1:T(8,128)} %copy-done) | copy-start | bytes 1572868
  461.5 34.7 %copy-start.9 = (f32[32,256]{1,0:T(8,128)S(1)}, f32[32,256]{1,0:T(8,128)}, u32[]{:S(2)}) copy-start(f32[32,256]{1,0:T(8,128)} %multiply_add_fusion.1.refs_0_) | copy-start | bytes 98308
Sparse Core Ops, SparseCore 0:
  9.8 36.3 all-gather.1

commit v9 on v8

--- a/solution.py
+++ b/solution.py
@@ -308,9 +308,9 @@
     listed = jnp.zeros((segments,), jnp.float32).at[chosen[0]].max(usable_weight[0])
     kernel_tile = wendland(row_blocks[0], reach_blocks, period) * listed[:, None, None]
 
-    def apply_kernel(values):
+    def apply_kernel(values, wide=False):
         width = values.shape[0]
-        if width == omega.shape[0]:
+        if wide:
             slab_values = lax.all_gather(values, "leaf", axis=1, tiled=True)
             parts = (shifted(slab_values, 1), slab_values, shifted(slab_values, -1))
             out = None
@@ -337,7 +337,10 @@
     def total_per_samp(values):
         return jax.tree.map(unslot, lax.psum(jax.tree.map(slot, values), ALL_AXES))
 
-    sketch = apply_kernel(omega) + sketch_shift * omega
+    sketch_rows = omega.shape[0]
+    omega_rows = lax.dynamic_slice_in_dim(omega, samp_idx * (sketch_rows // n_samp), sketch_rows // n_samp)
+    sketch = apply_kernel(omega_rows, wide=True) + sketch_shift * omega_rows
+    sketch = lax.all_gather(sketch, "samp", axis=0, tiled=True)
     rhs = observed[None, :] - prior_draws
     half = PB // n_samp
     omega_half = lax.dynamic_slice_in_dim(omega, samp_idx * half, half, axis=1)

time: 510 us -> 439 us (0.86)
  Pallas kernels: 209 us -> 171 us
  matrix products: 54.3 us -> 31.4 us
  local copies, waits for them, and re-layouts: 40.4 us -> 25.8 us
  waiting for transfers between devices: 36.9 us -> 27.5 us
  other arithmetic: 143 us -> 152 us
    pallas_call x3, Pallas kernels: 72 us -> 34.5 us  [halo_gather(): pl.pallas_call(lambda *refs: halo_kernel(n_blk, n_leaf, *refs), out_shape...]
    all_gather x1, waiting for transfers between devices: 36.9 us -> 9.93 us  [apply_kernel(): slab_values = lax.all_gather(values, 'leaf', axis=1, tiled=True)]
    ppermute x2, waiting for transfers between devices: 0.01 us -> 17.6 us  [shifted_2(): return lax.ppermute(block, axis, route)]
    another operation x14, other arithmetic: 80.9 us -> 91.2 us  [local(): joint_factor = jnp.linalg.cholesky(joint_gram)]
    dot_general x6, matrix products: 11.4 us -> 4.58 us  [high_dot(): jnp.dot(left, right, precision=lax.Precision.HIGHEST, preferred_element_t...]
    another operation x14, matrix products: 9.79 us -> 3.57 us  [lower_solve(): lax.linalg.triangular_solve(factor, values, left_side=True, lower=True)]
    another operation x14, matrix products: 8.24 us -> 2.91 us  [precond_from(): lax.linalg.triangular_solve(joint_factor, first_solve, left_side=True, lo...]
  transfers between devices with their start and end apart: 3 -> 3, of which waited for: 1 -> 3; matrix products, arithmetic and copies ran while one was open for 3% -> 4% of each run, Pallas kernels for 10% -> 3%
where the time goes in v9:
time: 439 us; the launch traced here: 432 us
  Pallas kernels  171 us (39%)
  other arithmetic  152 us (35%)
  matrix products  31.4 us (7%)
  waiting for transfers between devices  27.5 us (6%)
  local copies, waits for them, and re-layouts  25.8 us (6%)
  between operations  17.5 us (4%)
    pallas_call x4, Pallas kernels, group_sum(): pl.pallas_call(lambda *refs: sum_kernel(phases, *refs), out_shape=jax.Sha...  93.4 us
    another operation x14, other arithmetic, local(): joint_factor = jnp.linalg.cholesky(joint_gram)  91.2 us
    pallas_call x1, Pallas kernels, gram_sum(): pl.pallas_call(lambda *refs: gram_kernel(phases, *refs), out_shape=jax.Sh...  43.2 us
    another operation x4, other arithmetic, precond_from(): lax.linalg.triangular_solve(joint_factor, first_solve, left_side=True, lo...  40.5 us
    pallas_call x3, Pallas kernels, halo_gather(): pl.pallas_call(lambda *refs: halo_kernel(n_blk, n_leaf, *refs), out_shape...  34.5 us
    ppermute x2, waiting for transfers between devices, shifted_2(): return lax.ppermute(block, axis, route)  17.6 us
    another operation x13, local copies, waits for them, and re-layouts, precond_from(): lax.linalg.triangular_solve(joint_factor, first_solve, left_side=True, lo...  9.98 us
    all_gather x1, waiting for transfers between devices, apply_kernel(): slab_values = lax.all_gather(values, 'leaf', axis=1, tiled=True)  9.93 us
  transfers between devices with their start and end apart: 3, of which 3 were waited for; matrix products, arithmetic and copies ran while one was open for 4% of the time, Pallas kernels for 3%

profile of v9, /device:TPU:4, one launch (start us, length us, event | category | flops | bytes accessed | tf_op | source)
XLA Modules:
  0.0 431.7 jit_solution(11089091826649042138)
XLA Ops:
  8.9 13.4 %shard_map.68 = f32[12,3,256]{2,1,0:T(4,128)} custom-call(f32[3,256]{1,0:T(4,128)} %refs_0_.1), custom_call_target="tpu_custom_call" | custom-call | tf_op jit(solution)/shard_map/pallas_call | solution.py:274
  23.9 5.5 %broadcast_subtract_fusion = f32[12,3,256,256]{3,2,0,1:T(8,128)} fusion(f32[12,3,256]{2,0,1:T(8,128)S(1)} %copy.16, f32[3,256]{1,0:T(4,128)} %refs_0_.1), kind=kLoop, calls=%fused_computation.4 | loop fusion | flops 2359296 | bytes 9477120 | tf_op jit(solution)/shard_map/sub | solution.py:26
  29.4 9.9 %all-gather.2.cloned.1.call-done = f32[256,1024]{1,0:T(8,128)} async-done(((f32[256,256]{1,0:T(8,128)}), f32[256,1024]{1,0:T(8,128)}) %all-gather.2.cloned.1.call-update) | async-done | bytes 1048592 | tf_op jit(solution)/shard_map/all_gather | solution.py:314
  39.3 3.3 collective-permute-start.1
  43.4 6.4 %multiply_multiply_fusion = f32[12,256,256]{2,1,0:T(8,128)S(1)} fusion(f32[12,3,256,256]{3,2,0,1:T(8,128)} %broadcast_subtract_fusion, f32[12]{0:T(128)S(1)} %scatter_custom_fusion), kind=kLoop, calls=%fused_computation.17 | loop fusion | flops 17301504 | bytes 12582960 | tf_op jit(solution)/shard_map/mul | solution.py:309
  50.9 13.6 %collective-permute-done.1 = f32[256,1024]{1,0:T(8,128)S(1)} collective-permute-done((f32[256,1024]{1,0:T(8,128)}, f32[256,1024]{1,0:T(8,128)S(1)}, u32[]{:S(2)}, u32[]{:S(2)}) %collective-permute-start.1) | collective-permute-done | bytes 1048608 | tf_op jit(solution)/shard_map/ppermute | solution.py:22
  65.5 4.0 collective-permute-done
  71.1 3.0 fusion.11
  74.1 2.4 all_gather.7
  81.2 3.0 fusion.23
  84.2 2.3 reshape.153.refs_0_
  86.5 43.2 %shard_map.69 = f32[2048,128]{1,0:T(8,128)} custom-call(f32[2048,128]{1,0:T(8,128)} %reshape.153.refs_0_), custom_call_target="tpu_custom_call" | custom-call | tf_op jit(solution)/shard_map/pallas_call | solution.py:210
  132.7 11.7 %cholesky.104 = f32[128,128]{1,0:T(8,128)S(1)} custom-call(f32[128,128]{1,0:T(8,128)S(1)} %cholesky.266), custom_call_target="Cholesky" | custom-call | tf_op jit(solution)/shard_map/jit(cholesky)/cholesky | solution.py:358
  144.6 9.8 %custom-call.33 = f32[1,128,128]{1,2,0:T(8,128)S(1)} custom-call(f32[1,128,128]{2,1,0:T(8,128)S(1)} %get-tuple-element.57), custom_call_target="InvertDiagBlocksLowerTriangular" | custom-call | tf_op jit(solution)/shard_map/jit(cholesky)/cholesky | solution.py:358
  157.0 24.6 %cholesky.217 = f32[128,128]{1,0:T(8,128)S(1)} custom-call(f32[128,128]{1,0:T(8,128)S(1)} %cholesky.270), custom_call_target="Cholesky" | custom-call | tf_op jit(solution)/shard_map/jit(cholesky)/cholesky | solution.py:358
  181.6 9.8 %custom-call.34 = f32[1,128,128]{1,2,0:T(8,128)S(1)} custom-call(f32[1,128,128]{2,1,0:T(8,128)S(1)} %get-tuple-element.54), custom_call_target="InvertDiagBlocksLowerTriangular" | custom-call | tf_op jit(solution)/shard_map/jit(cholesky)/cholesky | solution.py:358
  193.0 11.7 %cholesky.238 = f32[128,128]{1,0:T(8,128)S(1)} custom-call(f32[128,128]{1,0:T(8,128)S(1)} %cholesky.275), custom_call_target="Cholesky" | custom-call | tf_op jit(solution)/shard_map/jit(cholesky)/cholesky | solution.py:358
  205.4 9.8 %custom-call.35 = f32[1,128,128]{1,2,0:T(8,128)S(1)} custom-call(f32[1,128,128]{2,1,0:T(8,128)S(1)} %get-tuple-element.51), custom_call_target="InvertDiagBlocksLowerTriangular" | custom-call | tf_op jit(solution)/shard_map/jit(cholesky)/cholesky | solution.py:358
  216.6 11.7 %cholesky.255 = f32[128,128]{1,0:T(8,128)S(1)} custom-call(f32[128,128]{1,0:T(8,128)S(1)} %convolution_subtract_fusion.8), custom_call_target="Cholesky" | custom-call | tf_op jit(solution)/shard_map/jit(cholesky)/cholesky | solution.py:358
  232.2 10.0 %while.8 = (s32[]{:T(128)}, f32[512,512]{1,0:T(8,128)S(1)}, s32[4,2]{0,1:T(2,128)S(1)}, f32[4,128,128]{2,1,0:T(8,128)}, s32[]{:T(128)}) while((s32[]{:T(128)}, f32[512,512]{1,0:T(8,128)S(1)}, s32[4,2]{0,1:T(2,128)S(1)}, f32[4,128,128]{2,1,0:T(8,128)}, s32[]{:T(128)}) %tuple.49), condition=%wide.while_cond.1, body=%wide.while_body.1.sunk | while | flops 2 | bytes 132705 | solution.py:362
  232.8 1.9 bitcast_dynamic-update-slice_fusion.2
  235.3 1.9 bitcast_dynamic-update-slice_fusion.2
  240.3 1.9 bitcast_dynamic-update-slice_fusion.2
  242.2 40.3 %custom-call.39 = f32[4,128,128]{1,2,0:T(8,128)S(1)} custom-call(f32[4,128,128]{2,1,0:T(8,128)} %get-tuple-element.33), custom_call_target="InvertDiagBlocksLowerTriangular" | custom-call | tf_op jit(solution)/shard_map/triangular_solve/custom-call.8 | solution.py:362
  283.9 30.2 %shard_map.70 = f32[128,128]{1,0:T(8,128)} custom-call(f32[128,128]{1,0:T(8,128)} %reshape.155.refs_0_), custom_call_target="tpu_custom_call" | custom-call | tf_op jit(solution)/shard_map/pallas_call | solution.py:109
  319.3 10.3 %shard_map.71 = f32[12,32,256]{2,1,0:T(8,128)} custom-call(f32[32,256]{1,0:T(8,128)} %convolution_subtract_fusion.10.refs_0_), custom_call_target="tpu_custom_call" | custom-call | tf_op jit(solution)/shard_map/pallas_call | solution.py:274
  329.6 4.9 %multiply_reduce_fusion.3 = (f32[32]{0:T(128)S(1)}, f32[32]{0:T(128)S(1)}, f32[32,256]{1,0:T(8,128)S(1)}) fusion(f32[32,256]{1,0:T(8,128)} %convolution_subtract_fusion.10.refs_0_, f32[32,256]{1,0:T(8,128)S(1)} %copy-done.6, f32[256]{0:T(256)S(1)} %copy-done.8, f32[12,32,256]{2,1,0:T(8,128)} %shard_map.71, f32[12,256,256]{2,1,0:T(8,128)} %copy-done.1), kind=kOutput, calls=%fused_computation.176 | convolution fusion | flops 302038976 | bytes 3638528 | tf_op jit(solution)/shard_map/ncj,nij->ci/dot_general | solution.py:328
  335.8 29.2 %shard_map.72 = f32[136,128]{1,0:T(8,128)} custom-call(f32[136,128]{1,0:T(8,128)} %pad_maximum_fusion.refs_0_), custom_call_target="tpu_custom_call" | custom-call | tf_op jit(solution)/shard_map/pallas_call | solution.py:109
  371.3 15.3 %shard_map.73 = f32[8,128]{1,0:T(8,128)} custom-call(f32[8,128]{1,0:T(8,128)} %pad.13.refs_0_), custom_call_target="tpu_custom_call" | custom-call | tf_op jit(solution)/shard_map/pallas_call | solution.py:109
  388.0 10.7 %shard_map.74 = f32[12,32,256]{2,1,0:T(8,128)} custom-call(f32[32,256]{1,0:T(8,128)} %multiply_add_fusion.1.refs_0_), custom_call_target="tpu_custom_call" | custom-call | tf_op jit(solution)/shard_map/pallas_call | solution.py:274
  398.7 4.9 %multiply_reduce_fusion = (f32[32]{0:T(128)S(1)}, f32[32,256]{1,0:T(8,128)S(1)}) fusion(f32[32,256]{1,0:T(8,128)} %multiply_add_fusion.1.refs_0_, f32[12,32,256]{2,1,0:T(8,128)} %shard_map.74, f32[12,256,256]{2,1,0:T(8,128)} %copy-done.1), kind=kOutput, calls=%fused_computation.171 | convolution fusion | flops 302014432 | bytes 3604608 | tf_op jit(solution)/shard_map/ncj,nij->ci/dot_general | solution.py:328
  404.2 18.8 %shard_map.75 = f32[8,128]{1,0:T(8,128)} custom-call(f32[8,128]{1,0:T(8,128)} %pad.14.refs_0_), custom_call_target="tpu_custom_call" | custom-call | tf_op jit(solution)/shard_map/pallas_call | solution.py:109
  (116 shorter events, 44.6 us)
Async XLA Ops:
  7.2 1.0 copy-start
  7.2 32.1 %all-gather.2.cloned.1.call-start = ((), (), s32[]{:S(2)}) async-start(), calls=%async_computation | async-start | bytes 1310720 | tf_op jit(solution)/shard_map/all_gather | solution.py:314
  23.9 18.8 %copy-start.9 = (s32[1,8]{1,0:T(1,128)S(1)}, s32[1,8]{1,0:T(1,128)}, u32[]{:S(2)}) copy-start(s32[1,8]{1,0:T(1,128)} %param.10) | copy-start | bytes 100
  39.3 25.1 %collective-permute-start.1 = (f32[256,1024]{1,0:T(8,128)}, f32[256,1024]{1,0:T(8,128)S(1)}, u32[]{:S(2)}, u32[]{:S(2)}) collective-permute-start(f32[256,1024]{1,0:T(8,128)} %all-gather.2.cloned.1.call-done), channel_id=1, source_target_pairs={{8,0},{16,8},{24,16},{32,24},{40,32},{48,40},{56,48},{64,56},{72,6... | collective-permute-start | bytes 3145736 | tf_op jit(solution)/shard_map/ppermute | solution.py:22
  43.3 6.5 %copy-start.4 = (f32[256,1024]{1,0:T(8,128)S(1)}, f32[256,1024]{1,0:T(8,128)}, u32[]{:S(2)}) copy-start(f32[256,1024]{1,0:T(8,128)} %all-gather.2.cloned.1.call-done) | copy-start | bytes 3145732
  43.3 26.2 %collective-permute-start = (f32[256,1024]{1,0:T(8,128)}, f32[256,1024]{1,0:T(8,128)}, u32[]{:S(2)}, u32[]{:S(2)}) collective-permute-start(f32[256,1024]{1,0:T(8,128)} %all-gather.2.cloned.1.call-done), channel_id=1, source_target_pairs={{248,0},{0,8},{8,16},{16,24},{24,32},{32,40},{40,48},{48,56},{56,6... | collective-permute-start | bytes 3145736 | tf_op jit(solution)/shard_map/ppermute | solution.py:22
  49.8 14.7 %copy-start.1 = (f32[12,256,256]{2,1,0:T(8,128)}, f32[12,256,256]{2,1,0:T(8,128)S(1)}, u32[]{:S(2)}) copy-start(f32[12,256,256]{2,1,0:T(8,128)S(1)} %multiply_multiply_fusion) | copy-start | bytes 9437188
  49.8 21.3 %copy-start.3 = (f32[256,256]{1,0:T(8,128)S(1)}, f32[256,256]{1,0:T(8,128)}, u32[]{:S(2)}) copy-start(f32[256,256]{1,0:T(8,128)} %constant_dynamic-slice_fusion.1) | copy-start | bytes 786436
  131.7 1.0 copy-start.2
  154.4 128.1 %copy-start.6 = (f32[32,256]{1,0:T(8,128)S(1)}, f32[32,256]{1,0:T(8,128)}, u32[]{:S(2)}) copy-start(f32[32,256]{1,0:T(8,128)} %param.13) | copy-start | bytes 98308
  154.4 128.1 %copy-start.8 = (f32[256]{0:T(256)S(1)}, f32[256]{0:T(256)}, u32[]{:S(2)}) copy-start(f32[256]{0:T(256)} %param.12) | copy-start | bytes 3076
  334.5 52.8 %copy-start.5 = (f32[32,256]{1,0:T(8,128)S(1)}, f32[32,256]{1,0:T(8,128)}, u32[]{:S(2)}) copy-start(f32[32,256]{1,0:T(8,128)} %convolution_subtract_fusion.10.refs_0_) | copy-start | bytes 98308
  388.0 35.8 %copy-start.7 = (f32[32,256]{1,0:T(8,128)S(1)}, f32[32,256]{1,0:T(8,128)}, u32[]{:S(2)}) copy-start(f32[32,256]{1,0:T(8,128)} %multiply_add_fusion.1.refs_0_) | copy-start | bytes 98308
Sparse Core Ops, SparseCore 0:
  9.8 29.4 all-gather.1

commit v10 on v9

--- a/solution.py
+++ b/solution.py
@@ -120,12 +120,13 @@
     )(values)
 
 
-def gram_kernel(phases, x_ref, o_ref, *scratch):
+def gram_kernel(phases, x_ref, y_ref, o_ref, z_ref, *scratch):
     count = len(phases)
     recvs = scratch[:count]
     sums = scratch[count : 2 * count - 1]
     full = scratch[2 * count - 1]
-    rs_send, rs_recv, ag_send, ag_recv = scratch[2 * count :]
+    rs_send, rs_recv, ag_send, ag_recv, side, side_send, side_recv = scratch[2 * count :]
+    side_acc = y_ref[...]
     barrier = pltpu.get_barrier_semaphore()
     greeted = 0
     for axis, n, stride in phases:
@@ -145,6 +146,20 @@
         recv = recvs[p]
         recv[0] = source[pl.ds(pl.multiple_of(own * part, 8), part)]
         copies = []
+        if axis != "samp":
+            side[p, 0] = side_acc
+            for k in range(1, n):
+                _, peer = group_peer(axis, n, stride, k)
+                copy = pltpu.make_async_remote_copy(
+                    src_ref=side.at[p, 0],
+                    dst_ref=side.at[p, k],
+                    send_sem=side_send.at[p, k],
+                    recv_sem=side_recv.at[p, k],
+                    device_id={axis: peer},
+                    device_id_type=pl.DeviceIdType.MESH,
+                )
+                copy.start()
+                copies.append(copy)
         for k in range(1, n):
             _, peer = group_peer(axis, n, stride, k)
             chunk = (own + k) % n
@@ -163,6 +178,10 @@
         acc = recv[own % n]
         for j in range(1, n):
             acc = acc + recv[(own - j) % n]
+        if axis != "samp":
+            side_acc = side[p, own % n]
+            for j in range(1, n):
+                side_acc = side_acc + side[p, (own - j) % n]
         offset = offset + own * part
         length = part
         if p < count - 1:
@@ -192,9 +211,10 @@
         offset = offset - own * length
         length = length * n
     o_ref[...] = full[...]
-
-
-def gram_sum(values, collective_id):
+    z_ref[...] = side_acc
+
+
+def gram_sum(values, side_values, collective_id):
     phases = (("samp", lax.axis_size("samp"), 1),) + reduce_phases()
     phases = tuple(p for p in phases if p[1] > 1)
     rows = values.shape[0]
@@ -207,14 +227,22 @@
         if p < len(phases) - 1:
             sums.append(pltpu.VMEM((length, 128), jnp.float32))
     semaphores = [pltpu.SemaphoreType.DMA((len(phases), widest)) for _ in range(4)]
+    side_scratch = [
+        pltpu.VMEM((len(phases), widest) + side_values.shape, jnp.float32),
+        pltpu.SemaphoreType.DMA((len(phases), widest)),
+        pltpu.SemaphoreType.DMA((len(phases), widest)),
+    ]
     return pl.pallas_call(
         lambda *refs: gram_kernel(phases, *refs),
-        out_shape=jax.ShapeDtypeStruct(values.shape, jnp.float32),
-        in_specs=[pl.BlockSpec(memory_space=pltpu.VMEM)],
-        out_specs=pl.BlockSpec(memory_space=pltpu.VMEM),
-        scratch_shapes=recvs + sums + [pltpu.VMEM((rows, 128), jnp.float32)] + semaphores,
+        out_shape=(
+            jax.ShapeDtypeStruct(values.shape, jnp.float32),
+            jax.ShapeDtypeStruct(side_values.shape, jnp.float32),
+        ),
+        in_specs=[pl.BlockSpec(memory_space=pltpu.VMEM)] * 2,
+        out_specs=(pl.BlockSpec(memory_space=pltpu.VMEM),) * 2,
+        scratch_shapes=recvs + sums + [pltpu.VMEM((rows, 128), jnp.float32)] + semaphores + side_scratch,
         compiler_params=pltpu.CompilerParams(collective_id=collective_id, has_side_effects=True),
-    )(values)
+    )(values, side_values)
 
 
 def halo_kernel(n_blk, n_leaf, x_ref, o_ref, land, send_sem, recv_sem):
@@ -349,11 +377,11 @@
     square_part = high_dot(sketch_half, sketch_half.T)
     joint_part = 0.5 * (core_part + core_part.T) + 0.5 * (square_part + square_part.T)
     gram_rows = joint_part.shape[0]
-    joint_gram = gram_sum(joint_part.reshape(gram_rows * gram_rows // 128, 128), 2)
-    joint_gram = joint_gram.reshape(gram_rows, gram_rows)
     width = rhs.shape[0]
     rhs_proj = high_dot(sketch, rhs.T).reshape(gram_rows * width // 128, 128)
-    rhs_proj = group_sum(rhs_proj, 3).reshape(gram_rows, width)
+    joint_gram, rhs_proj = gram_sum(joint_part.reshape(gram_rows * gram_rows // 128, 128), rhs_proj, 2)
+    joint_gram = joint_gram.reshape(gram_rows, gram_rows)
+    rhs_proj = rhs_proj.reshape(gram_rows, width)
 
     joint_factor = jnp.linalg.cholesky(joint_gram)
 

time: 439 us -> 415 us (0.945)
  other arithmetic: 152 us -> 140 us
  Pallas kernels: 171 us -> 160 us
    pallas_call x4 -> x3, Pallas kernels: 93.4 us -> 65.5 us  [group_sum(): pl.pallas_call(lambda *refs: sum_kernel(phases, *refs), out_shape=jax.Sha...]
    pallas_call x1, Pallas kernels: 43.2 us -> 59.7 us  [gram_sum(): pl.pallas_call(lambda *refs: gram_kernel(phases, *refs), out_shape=(jax.S...]
    another operation x14, other arithmetic: 91.2 us -> 78.8 us  [local(): joint_factor = jnp.linalg.cholesky(joint_gram)]
where the time goes in v10:
time: 415 us; the launch traced here: 408 us
  Pallas kernels  160 us (39%)
  other arithmetic  140 us (34%)
  matrix products  31.6 us (8%)
  waiting for transfers between devices  27.5 us (7%)
  local copies, waits for them, and re-layouts  25 us (6%)
  between operations  17.4 us (4%)
    another operation x14, other arithmetic, local(): joint_factor = jnp.linalg.cholesky(joint_gram)  78.8 us
    pallas_call x3, Pallas kernels, group_sum(): pl.pallas_call(lambda *refs: sum_kernel(phases, *refs), out_shape=jax.Sha...  65.5 us
    pallas_call x1, Pallas kernels, gram_sum(): pl.pallas_call(lambda *refs: gram_kernel(phases, *refs), out_shape=(jax.S...  59.7 us
    another operation x4, other arithmetic, precond_from(): lax.linalg.triangular_solve(joint_factor, first_solve, left_side=True, lo...  40.4 us
    pallas_call x3, Pallas kernels, halo_gather(): pl.pallas_call(lambda *refs: halo_kernel(n_blk, n_leaf, *refs), out_shape...  35.1 us
    ppermute x2, waiting for transfers between devices, shifted_2(): return lax.ppermute(block, axis, route)  17.6 us
    another operation x13, local copies, waits for them, and re-layouts, precond_from(): lax.linalg.triangular_solve(joint_factor, first_solve, left_side=True, lo...  9.98 us
    all_gather x1, waiting for transfers between devices, apply_kernel(): slab_values = lax.all_gather(values, 'leaf', axis=1, tiled=True)  9.93 us
  transfers between devices with their start and end apart: 3, of which 3 were waited for; matrix products, arithmetic and copies ran while one was open for 4% of the time, Pallas kernels for 3%

profile of v10, /device:TPU:4, one launch (start us, length us, event | category | flops | bytes accessed | tf_op | source)
XLA Modules:
  0.0 407.7 jit_solution(18149274519850605597)
XLA Ops:
  8.9 13.4 %shard_map.68 = f32[12,3,256]{2,1,0:T(4,128)} custom-call(f32[3,256]{1,0:T(4,128)} %refs_0_.1), custom_call_target="tpu_custom_call" | custom-call | tf_op jit(solution)/shard_map/pallas_call | solution.py:302
  23.9 5.5 %broadcast_subtract_fusion = f32[12,3,256,256]{3,2,0,1:T(8,128)} fusion(f32[12,3,256]{2,0,1:T(8,128)S(1)} %copy.16, f32[3,256]{1,0:T(4,128)} %refs_0_.1), kind=kLoop, calls=%fused_computation.4 | loop fusion | flops 2359296 | bytes 9477120 | tf_op jit(solution)/shard_map/sub | solution.py:26
  29.4 9.9 %all-gather.2.cloned.1.call-done = f32[256,1024]{1,0:T(8,128)} async-done(((f32[256,256]{1,0:T(8,128)}), f32[256,1024]{1,0:T(8,128)}) %all-gather.2.cloned.1.call-update) | async-done | bytes 1048592 | tf_op jit(solution)/shard_map/all_gather | solution.py:342
  39.3 3.3 collective-permute-start.1
  43.4 6.4 %multiply_multiply_fusion = f32[12,256,256]{2,1,0:T(8,128)S(1)} fusion(f32[12,3,256,256]{3,2,0,1:T(8,128)} %broadcast_subtract_fusion, f32[12]{0:T(128)S(1)} %scatter_custom_fusion), kind=kLoop, calls=%fused_computation.17 | loop fusion | flops 17301504 | bytes 12582960 | tf_op jit(solution)/shard_map/mul | solution.py:337
  50.9 13.6 %collective-permute-done.1 = f32[256,1024]{1,0:T(8,128)S(1)} collective-permute-done((f32[256,1024]{1,0:T(8,128)}, f32[256,1024]{1,0:T(8,128)S(1)}, u32[]{:S(2)}, u32[]{:S(2)}) %collective-permute-start.1) | collective-permute-done | bytes 1048608 | tf_op jit(solution)/shard_map/ppermute | solution.py:22
  65.5 4.0 collective-permute-done
  71.1 3.0 fusion.11
  74.1 2.4 all_gather.7
  81.1 3.0 fusion.23
  84.2 2.3 reshape.153.refs_0_
  87.7 59.7 %shard_map.69 = (f32[2048,128]{1,0:T(8,128)}, f32[128,128]{1,0:T(8,128)}) custom-call(f32[2048,128]{1,0:T(8,128)} %reshape.153.refs_0_, f32[128,128]{1,0:T(8,128)} %reshape.154.refs_1_), custom_call_target="tpu_custom_call" | custom-call | tf_op jit(solution)/shard_map/pallas_call | solution.py:235
  150.4 11.7 %cholesky.104 = f32[128,128]{1,0:T(8,128)S(1)} custom-call(f32[128,128]{1,0:T(8,128)S(1)} %cholesky.266), custom_call_target="Cholesky" | custom-call | tf_op jit(solution)/shard_map/jit(cholesky)/cholesky | solution.py:386
  162.3 9.8 %custom-call.33 = f32[1,128,128]{1,2,0:T(8,128)S(1)} custom-call(f32[1,128,128]{2,1,0:T(8,128)S(1)} %get-tuple-element.61), custom_call_target="InvertDiagBlocksLowerTriangular" | custom-call | tf_op jit(solution)/shard_map/jit(cholesky)/cholesky | solution.py:386
  174.9 11.7 %cholesky.217 = f32[128,128]{1,0:T(8,128)S(1)} custom-call(f32[128,128]{1,0:T(8,128)S(1)} %cholesky.270), custom_call_target="Cholesky" | custom-call | tf_op jit(solution)/shard_map/jit(cholesky)/cholesky | solution.py:386
  186.6 9.8 %custom-call.34 = f32[1,128,128]{1,2,0:T(8,128)S(1)} custom-call(f32[1,128,128]{2,1,0:T(8,128)S(1)} %get-tuple-element.58), custom_call_target="InvertDiagBlocksLowerTriangular" | custom-call | tf_op jit(solution)/shard_map/jit(cholesky)/cholesky | solution.py:386
  198.0 11.7 %cholesky.238 = f32[128,128]{1,0:T(8,128)S(1)} custom-call(f32[128,128]{1,0:T(8,128)S(1)} %cholesky.275), custom_call_target="Cholesky" | custom-call | tf_op jit(solution)/shard_map/jit(cholesky)/cholesky | solution.py:386
  210.4 10.2 %custom-call.35 = f32[1,128,128]{1,2,0:T(8,128)S(1)} custom-call(f32[1,128,128]{2,1,0:T(8,128)S(1)} %get-tuple-element.55), custom_call_target="InvertDiagBlocksLowerTriangular" | custom-call | tf_op jit(solution)/shard_map/jit(cholesky)/cholesky | solution.py:386
  222.0 11.7 %cholesky.255 = f32[128,128]{1,0:T(8,128)S(1)} custom-call(f32[128,128]{1,0:T(8,128)S(1)} %convolution_subtract_fusion.8), custom_call_target="Cholesky" | custom-call | tf_op jit(solution)/shard_map/jit(cholesky)/cholesky | solution.py:386
  237.9 10.0 %while.8 = (s32[]{:T(128)}, f32[512,512]{1,0:T(8,128)S(1)}, s32[4,2]{0,1:T(2,128)S(1)}, f32[4,128,128]{2,1,0:T(8,128)}, s32[]{:T(128)}) while((s32[]{:T(128)}, f32[512,512]{1,0:T(8,128)S(1)}, s32[4,2]{0,1:T(2,128)S(1)}, f32[4,128,128]{2,1,0:T(8,128)}, s32[]{:T(128)}) %tuple.49), condition=%wide.while_cond.1, body=%wide.while_body.1.sunk | while | flops 2 | bytes 132705 | solution.py:390
  238.5 1.9 bitcast_dynamic-update-slice_fusion.2
  241.0 1.9 bitcast_dynamic-update-slice_fusion.2
  243.5 1.9 bitcast_dynamic-update-slice_fusion.2
  246.0 1.9 bitcast_dynamic-update-slice_fusion.2
  247.9 40.3 %custom-call.39 = f32[4,128,128]{1,2,0:T(8,128)S(1)} custom-call(f32[4,128,128]{2,1,0:T(8,128)} %get-tuple-element.37), custom_call_target="InvertDiagBlocksLowerTriangular" | custom-call | tf_op jit(solution)/shard_map/triangular_solve/custom-call.8 | solution.py:390
  292.7 11.0 %shard_map.70 = f32[12,32,256]{2,1,0:T(8,128)} custom-call(f32[32,256]{1,0:T(8,128)} %convolution_subtract_fusion.10.refs_0_), custom_call_target="tpu_custom_call" | custom-call | tf_op jit(solution)/shard_map/pallas_call | solution.py:302
  303.7 4.9 %multiply_reduce_fusion.3 = (f32[32]{0:T(128)S(1)}, f32[32]{0:T(128)S(1)}, f32[32,256]{1,0:T(8,128)S(1)}) fusion(f32[32,256]{1,0:T(8,128)} %convolution_subtract_fusion.10.refs_0_, f32[32,256]{1,0:T(8,128)S(1)} %copy-done.6, f32[256]{0:T(256)S(1)} %copy-done.9, f32[12,32,256]{2,1,0:T(8,128)} %shard_map.70, f32[12,256,256]{2,1,0:T(8,128)} %copy-done.1), kind=kOutput, calls=%fused_computation.176 | convolution fusion | flops 302038976 | bytes 3638528 | tf_op jit(solution)/shard_map/ncj,nij->ci/dot_general | solution.py:356
  309.9 31.1 %shard_map.71 = f32[136,128]{1,0:T(8,128)} custom-call(f32[136,128]{1,0:T(8,128)} %pad_maximum_fusion.refs_0_), custom_call_target="tpu_custom_call" | custom-call | tf_op jit(solution)/shard_map/pallas_call | solution.py:109
  347.3 14.6 %shard_map.72 = f32[8,128]{1,0:T(8,128)} custom-call(f32[8,128]{1,0:T(8,128)} %pad.13.refs_0_), custom_call_target="tpu_custom_call" | custom-call | tf_op jit(solution)/shard_map/pallas_call | solution.py:109
  363.3 10.7 %shard_map.73 = f32[12,32,256]{2,1,0:T(8,128)} custom-call(f32[32,256]{1,0:T(8,128)} %multiply_add_fusion.1.refs_0_), custom_call_target="tpu_custom_call" | custom-call | tf_op jit(solution)/shard_map/pallas_call | solution.py:302
  374.0 4.9 %multiply_reduce_fusion = (f32[32]{0:T(128)S(1)}, f32[32,256]{1,0:T(8,128)S(1)}) fusion(f32[32,256]{1,0:T(8,128)} %multiply_add_fusion.1.refs_0_, f32[12,32,256]{2,1,0:T(8,128)} %shard_map.73, f32[12,256,256]{2,1,0:T(8,128)} %copy-done.1), kind=kOutput, calls=%fused_computation.171 | convolution fusion | flops 302014432 | bytes 3604608 | tf_op jit(solution)/shard_map/ncj,nij->ci/dot_general | solution.py:356
  379.5 19.8 %shard_map.74 = f32[8,128]{1,0:T(8,128)} custom-call(f32[8,128]{1,0:T(8,128)} %pad.14.refs_0_), custom_call_target="tpu_custom_call" | custom-call | tf_op jit(solution)/shard_map/pallas_call | solution.py:109
  (117 shorter events, 42.2 us)
Async XLA Ops:
  7.2 1.0 copy-start
  7.2 32.1 %all-gather.2.cloned.1.call-start = ((), (), s32[]{:S(2)}) async-start(), calls=%async_computation | async-start | bytes 1310720 | tf_op jit(solution)/shard_map/all_gather | solution.py:342
  23.9 18.8 %copy-start.10 = (s32[1,8]{1,0:T(1,128)S(1)}, s32[1,8]{1,0:T(1,128)}, u32[]{:S(2)}) copy-start(s32[1,8]{1,0:T(1,128)} %param.10) | copy-start | bytes 100
  39.3 25.1 %collective-permute-start.1 = (f32[256,1024]{1,0:T(8,128)}, f32[256,1024]{1,0:T(8,128)S(1)}, u32[]{:S(2)}, u32[]{:S(2)}) collective-permute-start(f32[256,1024]{1,0:T(8,128)} %all-gather.2.cloned.1.call-done), channel_id=1, source_target_pairs={{8,0},{16,8},{24,16},{32,24},{40,32},{48,40},{56,48},{64,56},{72,6... | collective-permute-start | bytes 3145736 | tf_op jit(solution)/shard_map/ppermute | solution.py:22
  43.3 6.5 %copy-start.4 = (f32[256,1024]{1,0:T(8,128)S(1)}, f32[256,1024]{1,0:T(8,128)}, u32[]{:S(2)}) copy-start(f32[256,1024]{1,0:T(8,128)} %all-gather.2.cloned.1.call-done) | copy-start | bytes 3145732
  43.3 26.2 %collective-permute-start = (f32[256,1024]{1,0:T(8,128)}, f32[256,1024]{1,0:T(8,128)}, u32[]{:S(2)}, u32[]{:S(2)}) collective-permute-start(f32[256,1024]{1,0:T(8,128)} %all-gather.2.cloned.1.call-done), channel_id=1, source_target_pairs={{248,0},{0,8},{8,16},{16,24},{24,32},{32,40},{40,48},{48,56},{56,6... | collective-permute-start | bytes 3145736 | tf_op jit(solution)/shard_map/ppermute | solution.py:22
  49.8 14.7 %copy-start.1 = (f32[12,256,256]{2,1,0:T(8,128)}, f32[12,256,256]{2,1,0:T(8,128)S(1)}, u32[]{:S(2)}) copy-start(f32[12,256,256]{2,1,0:T(8,128)S(1)} %multiply_multiply_fusion) | copy-start | bytes 9437188
  49.8 21.3 %copy-start.3 = (f32[256,256]{1,0:T(8,128)S(1)}, f32[256,256]{1,0:T(8,128)}, u32[]{:S(2)}) copy-start(f32[256,256]{1,0:T(8,128)} %constant_dynamic-slice_fusion.1) | copy-start | bytes 786436
  81.1 5.3 %copy-start.6 = (f32[32,256]{1,0:T(8,128)S(1)}, f32[32,256]{1,0:T(8,128)}, u32[]{:S(2)}) copy-start(f32[32,256]{1,0:T(8,128)} %param.13) | copy-start | bytes 98308
  81.1 5.3 %copy-start.9 = (f32[256]{0:T(256)S(1)}, f32[256]{0:T(256)}, u32[]{:S(2)}) copy-start(f32[256]{0:T(256)} %param.12) | copy-start | bytes 3076
  149.4 1.0 copy-start.2
  172.1 116.1 %copy-start.8 = (f32[128,128]{1,0:T(8,128)S(1)}, f32[128,128]{1,0:T(8,128)}, u32[]{:S(2)}) copy-start(f32[128,128]{1,0:T(8,128)} %get-tuple-element.7) | copy-start | bytes 196612
  308.6 54.0 %copy-start.5 = (f32[32,256]{1,0:T(8,128)S(1)}, f32[32,256]{1,0:T(8,128)}, u32[]{:S(2)}) copy-start(f32[32,256]{1,0:T(8,128)} %convolution_subtract_fusion.10.refs_0_) | copy-start | bytes 98308
  363.3 36.7 %copy-start.7 = (f32[32,256]{1,0:T(8,128)S(1)}, f32[32,256]{1,0:T(8,128)}, u32[]{:S(2)}) copy-start(f32[32,256]{1,0:T(8,128)} %multiply_add_fusion.1.refs_0_) | copy-start | bytes 98308
Sparse Core Ops, SparseCore 0:
  9.8 29.4 all-gather.1

commit v11 on v10

--- a/solution.py
+++ b/solution.py
@@ -390,11 +390,11 @@
         solved = lax.linalg.triangular_solve(
             joint_factor, first_solve, left_side=True, lower=True, transpose_a=True
         )
-        return (vectors - high_dot(solved.T, sketch)) / noise_variance
+        return (vectors - high_dot(solved.T, sketch)) / noise_variance, solved
 
     residual = rhs
     projected = rhs_proj
-    precond = precond_from(residual, projected)
+    precond, _ = precond_from(residual, projected)
     direction = precond
     weights = jnp.zeros_like(rhs)
 
@@ -410,7 +410,11 @@
         [
             image_proj,
             pack_scalars(
-                jnp.sum(residual * precond, axis=1), jnp.sum(direction * image, axis=1)
+                jnp.sum(residual * precond, axis=1),
+                jnp.sum(direction * image, axis=1),
+                jnp.sum(residual * residual, axis=1),
+                jnp.sum(residual * image, axis=1),
+                jnp.sum(image * image, axis=1),
             ),
         ]
     )
@@ -418,12 +422,14 @@
     image_proj = packed[:-8].reshape(sketch_rows, width)
     inner_now = packed[-8, :width]
     curvature = packed[-7, :width]
+    residual_sq, residual_image, image_sq = packed[-6, :width], packed[-5, :width], packed[-4, :width]
     step_size = inner_now / curvature
     weights = weights + step_size[:, None] * direction
     residual = residual - step_size[:, None] * image
     projected = projected - step_size[None, :] * image_proj
-    precond = precond_from(residual, projected)
-    inner_next = group_sum(pack_scalars(jnp.sum(residual * precond, axis=1)), 1)[0, :width]
+    precond, solved = precond_from(residual, projected)
+    residual_sq = residual_sq - 2.0 * step_size * residual_image + step_size * step_size * image_sq
+    inner_next = (residual_sq - jnp.sum(projected * solved, axis=0)) / noise_variance
     direction = precond + (inner_next / inner_now)[:, None] * direction
     inner_now = inner_next
 

time: 415 us -> 395 us (0.952)
  Pallas kernels: 160 us -> 142 us
    pallas_call x3 -> x2, Pallas kernels: 65.5 us -> 47.8 us  [group_sum(): pl.pallas_call(lambda *refs: sum_kernel(phases, *refs), out_shape=jax.Sha...]
where the time goes in v11:
time: 395 us; the launch traced here: 388 us
  Pallas kernels  142 us (36%)
  other arithmetic  140 us (35%)
  matrix products  31.9 us (8%)
  waiting for transfers between devices  27.4 us (7%)
  local copies, waits for them, and re-layouts  23.4 us (6%)
  between operations  17.4 us (4%)
    another operation x14, other arithmetic, local(): joint_factor = jnp.linalg.cholesky(joint_gram)  78.8 us
    pallas_call x1, Pallas kernels, gram_sum(): pl.pallas_call(lambda *refs: gram_kernel(phases, *refs), out_shape=(jax.S...  59.7 us
    pallas_call x2, Pallas kernels, group_sum(): pl.pallas_call(lambda *refs: sum_kernel(phases, *refs), out_shape=jax.Sha...  47.8 us
    another operation x4, other arithmetic, precond_from(): lax.linalg.triangular_solve(joint_factor, first_solve, left_side=True, lo...  40.4 us
    pallas_call x3, Pallas kernels, halo_gather(): pl.pallas_call(lambda *refs: halo_kernel(n_blk, n_leaf, *refs), out_shape...  34.8 us
    ppermute x2, waiting for transfers between devices, shifted_2(): return lax.ppermute(block, axis, route)  17.5 us
    another operation x13, local copies, waits for them, and re-layouts, precond_from(): lax.linalg.triangular_solve(joint_factor, first_solve, left_side=True, lo...  9.98 us
    all_gather x1, waiting for transfers between devices, apply_kernel(): slab_values = lax.all_gather(values, 'leaf', axis=1, tiled=True)  9.9 us
  transfers between devices with their start and end apart: 3, of which 3 were waited for; matrix products, arithmetic and copies ran while one was open for 4% of the time, Pallas kernels for 3%

profile of v11, /device:TPU:4, one launch (start us, length us, event | category | flops | bytes accessed | tf_op | source)
XLA Modules:
  0.0 387.8 jit_solution(15604674343246245260)
XLA Ops:
  9.0 13.4 %shard_map.68 = f32[12,3,256]{2,1,0:T(4,128)} custom-call(f32[3,256]{1,0:T(4,128)} %refs_0_.1), custom_call_target="tpu_custom_call" | custom-call | tf_op jit(solution)/shard_map/pallas_call | solution.py:302
  23.9 5.5 %broadcast_subtract_fusion = f32[12,3,256,256]{3,2,0,1:T(8,128)} fusion(f32[12,3,256]{2,0,1:T(8,128)S(1)} %copy.18, f32[3,256]{1,0:T(4,128)} %refs_0_.1), kind=kLoop, calls=%fused_computation.4 | loop fusion | flops 2359296 | bytes 9477120 | tf_op jit(solution)/shard_map/sub | solution.py:26
  29.4 9.9 %all-gather.2.cloned.1.call-done = f32[256,1024]{1,0:T(8,128)} async-done(((f32[256,256]{1,0:T(8,128)}), f32[256,1024]{1,0:T(8,128)}) %all-gather.2.cloned.1.call-update) | async-done | bytes 1048592 | tf_op jit(solution)/shard_map/all_gather | solution.py:342
  39.3 3.3 collective-permute-start.1
  43.4 6.4 %multiply_multiply_fusion = f32[12,256,256]{2,1,0:T(8,128)S(1)} fusion(f32[12,3,256,256]{3,2,0,1:T(8,128)} %broadcast_subtract_fusion, f32[12]{0:T(128)S(1)} %scatter_custom_fusion), kind=kLoop, calls=%fused_computation.17 | loop fusion | flops 17301504 | bytes 12582960 | tf_op jit(solution)/shard_map/mul | solution.py:337
  50.9 13.6 %collective-permute-done.1 = f32[256,1024]{1,0:T(8,128)S(1)} collective-permute-done((f32[256,1024]{1,0:T(8,128)}, f32[256,1024]{1,0:T(8,128)S(1)}, u32[]{:S(2)}, u32[]{:S(2)}) %collective-permute-start.1) | collective-permute-done | bytes 1048608 | tf_op jit(solution)/shard_map/ppermute | solution.py:22
  65.5 3.9 %collective-permute-done = f32[256,1024]{1,0:T(8,128)S(1)} collective-permute-done((f32[256,1024]{1,0:T(8,128)}, f32[256,1024]{1,0:T(8,128)S(1)}, u32[]{:S(2)}, u32[]{:S(2)}) %collective-permute-start) | collective-permute-done | bytes 1048608 | tf_op jit(solution)/shard_map/ppermute | solution.py:22
  69.8 3.0 fusion.11
  72.8 2.4 all_gather.7
  79.8 3.0 fusion.24
  82.8 2.3 reshape.185.refs_0_
  86.4 59.7 %shard_map.69 = (f32[2048,128]{1,0:T(8,128)}, f32[128,128]{1,0:T(8,128)}) custom-call(f32[2048,128]{1,0:T(8,128)} %reshape.185.refs_0_, f32[128,128]{1,0:T(8,128)} %reshape.186.refs_1_), custom_call_target="tpu_custom_call" | custom-call | tf_op jit(solution)/shard_map/pallas_call | solution.py:235
  149.0 11.7 %cholesky.104 = f32[128,128]{1,0:T(8,128)S(1)} custom-call(f32[128,128]{1,0:T(8,128)S(1)} %cholesky.266), custom_call_target="Cholesky" | custom-call | tf_op jit(solution)/shard_map/jit(cholesky)/cholesky | solution.py:386
  160.9 9.8 %custom-call.33 = f32[1,128,128]{1,2,0:T(8,128)S(1)} custom-call(f32[1,128,128]{2,1,0:T(8,128)S(1)} %get-tuple-element.67), custom_call_target="InvertDiagBlocksLowerTriangular" | custom-call | tf_op jit(solution)/shard_map/jit(cholesky)/cholesky | solution.py:386
  170.7 1.5 constant_dynamic-update-slice_fusion
  173.5 11.7 %cholesky.217 = f32[128,128]{1,0:T(8,128)S(1)} custom-call(f32[128,128]{1,0:T(8,128)S(1)} %cholesky.270), custom_call_target="Cholesky" | custom-call | tf_op jit(solution)/shard_map/jit(cholesky)/cholesky | solution.py:386
  185.2 9.8 %custom-call.34 = f32[1,128,128]{1,2,0:T(8,128)S(1)} custom-call(f32[1,128,128]{2,1,0:T(8,128)S(1)} %get-tuple-element.64), custom_call_target="InvertDiagBlocksLowerTriangular" | custom-call | tf_op jit(solution)/shard_map/jit(cholesky)/cholesky | solution.py:386
  196.6 11.7 %cholesky.238 = f32[128,128]{1,0:T(8,128)S(1)} custom-call(f32[128,128]{1,0:T(8,128)S(1)} %cholesky.275), custom_call_target="Cholesky" | custom-call | tf_op jit(solution)/shard_map/jit(cholesky)/cholesky | solution.py:386
  209.0 10.2 %custom-call.35 = f32[1,128,128]{1,2,0:T(8,128)S(1)} custom-call(f32[1,128,128]{2,1,0:T(8,128)S(1)} %get-tuple-element.61), custom_call_target="InvertDiagBlocksLowerTriangular" | custom-call | tf_op jit(solution)/shard_map/jit(cholesky)/cholesky | solution.py:386
  220.7 11.7 %cholesky.255 = f32[128,128]{1,0:T(8,128)S(1)} custom-call(f32[128,128]{1,0:T(8,128)S(1)} %convolution_subtract_fusion.5), custom_call_target="Cholesky" | custom-call | tf_op jit(solution)/shard_map/jit(cholesky)/cholesky | solution.py:386
  236.5 10.0 %while.8 = (s32[]{:T(128)}, f32[512,512]{1,0:T(8,128)S(1)}, s32[4,2]{0,1:T(2,128)S(1)}, f32[4,128,128]{2,1,0:T(8,128)}, s32[]{:T(128)}) while((s32[]{:T(128)}, f32[512,512]{1,0:T(8,128)S(1)}, s32[4,2]{0,1:T(2,128)S(1)}, f32[4,128,128]{2,1,0:T(8,128)}, s32[]{:T(128)}) %tuple.53), condition=%wide.while_cond.1, body=%wide.while_body.1.sunk | while | flops 2 | bytes 132705 | solution.py:390
  237.1 1.9 bitcast_dynamic-update-slice_fusion.2
  239.6 1.9 bitcast_dynamic-update-slice_fusion.2
  242.1 1.9 bitcast_dynamic-update-slice_fusion.2
  244.6 1.9 bitcast_dynamic-update-slice_fusion.2
  246.5 40.3 %custom-call.39 = f32[4,128,128]{1,2,0:T(8,128)S(1)} custom-call(f32[4,128,128]{2,1,0:T(8,128)} %get-tuple-element.37), custom_call_target="InvertDiagBlocksLowerTriangular" | custom-call | tf_op jit(solution)/shard_map/triangular_solve/custom-call.8 | solution.py:390
  291.3 11.0 %shard_map.70 = f32[12,32,256]{2,1,0:T(8,128)} custom-call(f32[32,256]{1,0:T(8,128)} %convolution_subtract_fusion.7.refs_0_), custom_call_target="tpu_custom_call" | custom-call | tf_op jit(solution)/shard_map/pallas_call | solution.py:302
  302.3 5.0 %multiply_reduce_fusion.3 = (f32[32]{0:T(128)S(1)}, f32[32]{0:T(128)S(1)}, f32[32]{0:T(128)S(1)}, f32[32]{0:T(128)S(1)}, f32[32]{0:T(128)S(1)}, /*index=5*/f32[32,256]{1,0:T(8,128)S(1)}) fusion(f32[32,256]{1,0:T(8,128)S(1)} %copy-done.5, f32[256]{0:T(256)S(1)} %copy-done.9, f32[32,256]{1,0:T(8,128)} %convolution_subtract_fusion.7.refs_0_, ...), kind=kOutput, calls=%fused_computation.170 | convolution fusion | flops 302088032 | bytes 3638912 | tf_op jit(solution)/shard_map/ncj,nij->ci/dot_general | solution.py:356
  308.6 31.1 %shard_map.71 = f32[136,128]{1,0:T(8,128)} custom-call(f32[136,128]{1,0:T(8,128)} %select_maximum_fusion.refs_0_), custom_call_target="tpu_custom_call" | custom-call | tf_op jit(solution)/shard_map/pallas_call | solution.py:109
  346.8 10.3 %shard_map.72 = f32[12,32,256]{2,1,0:T(8,128)} custom-call(f32[32,256]{1,0:T(8,128)} %fusion.14.refs_0_), custom_call_target="tpu_custom_call" | custom-call | tf_op jit(solution)/shard_map/pallas_call | solution.py:302
  357.1 4.9 %multiply_reduce_fusion.1 = (f32[32]{0:T(128)S(1)}, f32[32,256]{1,0:T(8,128)S(1)}) fusion(f32[32,256]{1,0:T(8,128)} %fusion.14.refs_0_, f32[12,32,256]{2,1,0:T(8,128)} %shard_map.72, f32[12,256,256]{2,1,0:T(8,128)} %copy-done.1), kind=kOutput, calls=%fused_computation.167 | convolution fusion | flops 302014432 | bytes 3604608 | tf_op jit(solution)/shard_map/ncj,nij->ci/dot_general | solution.py:356
  362.6 16.7 %shard_map.73 = f32[8,128]{1,0:T(8,128)} custom-call(f32[8,128]{1,0:T(8,128)} %pad.10.refs_0_), custom_call_target="tpu_custom_call" | custom-call | tf_op jit(solution)/shard_map/pallas_call | solution.py:109
  (116 shorter events, 38.9 us)
Async XLA Ops:
  7.2 1.0 copy-start
  7.2 32.1 %all-gather.2.cloned.1.call-start = ((), (), s32[]{:S(2)}) async-start(), calls=%async_computation | async-start | bytes 1310720 | tf_op jit(solution)/shard_map/all_gather | solution.py:342
  23.9 18.7 %copy-start.10 = (s32[1,8]{1,0:T(1,128)S(1)}, s32[1,8]{1,0:T(1,128)}, u32[]{:S(2)}) copy-start(s32[1,8]{1,0:T(1,128)} %param.10) | copy-start | bytes 100
  39.3 25.1 %collective-permute-start.1 = (f32[256,1024]{1,0:T(8,128)}, f32[256,1024]{1,0:T(8,128)S(1)}, u32[]{:S(2)}, u32[]{:S(2)}) collective-permute-start(f32[256,1024]{1,0:T(8,128)} %all-gather.2.cloned.1.call-done), channel_id=1, source_target_pairs={{8,0},{16,8},{24,16},{32,24},{40,32},{48,40},{56,48},{64,56},{72,6... | collective-permute-start | bytes 3145736 | tf_op jit(solution)/shard_map/ppermute | solution.py:22
  43.3 6.5 %copy-start.4 = (f32[256,1024]{1,0:T(8,128)S(1)}, f32[256,1024]{1,0:T(8,128)}, u32[]{:S(2)}) copy-start(f32[256,1024]{1,0:T(8,128)} %all-gather.2.cloned.1.call-done) | copy-start | bytes 3145732
  43.3 26.1 %collective-permute-start = (f32[256,1024]{1,0:T(8,128)}, f32[256,1024]{1,0:T(8,128)S(1)}, u32[]{:S(2)}, u32[]{:S(2)}) collective-permute-start(f32[256,1024]{1,0:T(8,128)} %all-gather.2.cloned.1.call-done), channel_id=1, source_target_pairs={{248,0},{0,8},{8,16},{16,24},{24,32},{32,40},{40,48},{48,56},{56,6... | collective-permute-start | bytes 3145736 | tf_op jit(solution)/shard_map/ppermute | solution.py:22
  49.8 14.7 %copy-start.1 = (f32[12,256,256]{2,1,0:T(8,128)}, f32[12,256,256]{2,1,0:T(8,128)S(1)}, u32[]{:S(2)}) copy-start(f32[12,256,256]{2,1,0:T(8,128)S(1)} %multiply_multiply_fusion) | copy-start | bytes 9437188
  49.8 19.9 %copy-start.3 = (f32[256,256]{1,0:T(8,128)S(1)}, f32[256,256]{1,0:T(8,128)}, u32[]{:S(2)}) copy-start(f32[256,256]{1,0:T(8,128)} %constant_dynamic-slice_fusion.1) | copy-start | bytes 786436
  79.8 5.3 %copy-start.5 = (f32[32,256]{1,0:T(8,128)S(1)}, f32[32,256]{1,0:T(8,128)}, u32[]{:S(2)}) copy-start(f32[32,256]{1,0:T(8,128)} %param.13) | copy-start | bytes 98308
  79.8 5.3 %copy-start.9 = (f32[256]{0:T(256)S(1)}, f32[256]{0:T(256)}, u32[]{:S(2)}) copy-start(f32[256]{0:T(256)} %param.12) | copy-start | bytes 3076
  148.0 1.0 copy-start.2
  170.7 116.1 %copy-start.8 = (f32[128,128]{1,0:T(8,128)S(1)}, f32[128,128]{1,0:T(8,128)}, u32[]{:S(2)}) copy-start(f32[128,128]{1,0:T(8,128)} %get-tuple-element.7) | copy-start | bytes 196612
  307.3 38.5 %copy-start.6 = (f32[32,256]{1,0:T(8,128)S(1)}, f32[32,256]{1,0:T(8,128)}, u32[]{:S(2)}) copy-start(f32[32,256]{1,0:T(8,128)} %convolution_subtract_fusion.7.refs_0_) | copy-start | bytes 98308
  346.8 33.2 %copy-start.7 = (f32[32,256]{1,0:T(8,128)S(1)}, f32[32,256]{1,0:T(8,128)}, u32[]{:S(2)}) copy-start(f32[32,256]{1,0:T(8,128)} %fusion.14.refs_0_) | copy-start | bytes 98308
Sparse Core Ops, SparseCore 0:
  9.8 29.4 all-gather.1
